TPU v7x, 256 devices: a whole 4x4x8 slice. The times are simulated.
256 devices in a mesh: sub: 64 (over z, y, core), grp: 4 (over x).
Axes of the slice: x: 4, y: 4, z: 8, core: 2. Of those that a mesh axis runs over, the one named last changes fastest.
Arguments:
- coarse: float32 [6144, 128], P(('sub', 'grp')), may hold values from -6 to 6
- corner_idx: int32 [256, 24], P(('sub', 'grp')), may hold values from 0 to 6143, as said below
- coupling: bfloat16 [393216, 24], P(('sub', 'grp')), may hold values from -1.25 to 1.25
- force: bfloat16 [131072, 3, 128], P(('sub', 'grp')), may hold values from -6 to 6
- panel_inv: bfloat16 [1024, 384, 384], P(('sub', 'grp')), as said below
- panel_nodes: int32 [256, 4], P(('sub', 'grp')), may hold values from 64 to 128, as said below
- strain_disp: bfloat16 [6, 24, 32768], P(None, None, ('sub', 'grp')), may hold values from -1.25 to 1.25
- modulus: float32 [32768], P(('sub', 'grp')), may hold values from 0.5 to 4
- connect: int32 [8, 32768], P(None, ('sub', 'grp')), may hold values from 0 to 511, as said below
- interface: int32 [256, 224], P(('sub', 'grp')), may hold values from 0 to 511, as said below
- nodal_volume: float32 [131072], P(('sub', 'grp')), may hold values from 4 to 16
Outputs:
- displacement: bfloat16 [131072, 3, 128], P(('sub', 'grp'))
- nodal_stress: bfloat16 [131072, 6, 128], P(('sub', 'grp'))
Inputs may be any that keep to these rules, and one draw needn't show every extreme that they name: `corner_idx`: the rows of subdomain (s, g) lie in the coarse blocks of subdomains (s', g') with |s' - s| <= 1 that exist, including blocks of all grp indices; they come in triples of consecutive rows. `panel_nodes`: every subdomain has one panel with exactly 128 live nodes and one with 64. `connect`: every entry is a live node of its subdomain (slot j < panel_nodes of its panel). `interface`: each row holds 224 distinct live nodes as eight lists: sub-lo (64), sub-hi (64), grp-lo (32), grp-hi (32), then edges ll, lh, hl, hh (8 each; first letter the sub side, second the grp side). Entry k of a list of (s, g) is the same physical node as entry k of the facing list of each neighbour: sub-hi with sub-lo of (s + 1, g), grp-hi with grp-lo of (s, g + 1); edge (x, y) with the edge of the neighbour across it that has the opposite letter on each side crossed. `panel_inv`: given inverses of the padded panels.
All inputs are finite; a program needn't handle non-finite values.
Results may differ from a plain program's by a relative error of at most 0.0058.
Values sent between devices are 32-bit elements; how exact they have to be, the bound alone decides.
A program may use at most 64 MiB of HBM per device.

v0:
```python
import jax
import jax.numpy as jnp
from jax import lax
from jax.sharding import PartitionSpec as P

NIS = 64
NIG = 32
NED = 8


POISSON = 0.3


def padded(block, sides, width):
    for axis, dim in sides:
        count = lax.axis_size(axis)
        forward = [(i, i + 1) for i in range(count - 1)]
        backward = [(target, source) for source, target in forward]
        low = lax.ppermute(
            lax.slice_in_dim(block, block.shape[dim] - width, None, axis=dim), axis, forward
        )
        high = lax.ppermute(lax.slice_in_dim(block, 0, width, axis=dim), axis, backward)
        block = jnp.concatenate([low, block, high], axis=dim)
    return block


def iso_matrix():
    lame_first = POISSON / ((1.0 + POISSON) * (1.0 - 2.0 * POISSON))
    shear_mod = 0.5 / (1.0 + POISSON)
    upper_block = jnp.full((3, 3), lame_first, jnp.float32) + jnp.eye(3, dtype=jnp.float32) * (
        2.0 * shear_mod
    )
    shear_block = jnp.eye(3, dtype=jnp.float32) * shear_mod
    zero_block = jnp.zeros((3, 3), jnp.float32)
    return jnp.concatenate(
        [
            jnp.concatenate([upper_block, zero_block], 1),
            jnp.concatenate([zero_block, shear_block], 1),
        ],
        0,
    )


def shards(
    coarse,
    corner_idx,
    coupling,
    force,
    panel_inv,
    panel_nodes,
    strain_disp,
    modulus,
    connect,
    interface,
    nodal_volume,
):
    group_rows = lax.all_gather(coarse, "grp", axis=0, tiled=True)
    block_rows = group_rows.shape[0]
    nearby = padded(group_rows, (("sub", 0),), block_rows)
    offset = (lax.axis_index("sub") - 1) * block_rows
    local_rows = corner_idx[0] - offset
    selector = (local_rows[:, None] == jnp.arange(3 * block_rows, dtype=jnp.int32)[None, :]).astype(
        jnp.float32
    )
    corner_vals = jnp.dot(selector, nearby, precision=lax.Precision.HIGHEST)
    node_count = force.shape[0]
    load_cases = force.shape[2]
    panels = panel_inv.shape[0]
    panel_rows = panel_inv.shape[1]
    correction = jnp.dot(coupling.astype(jnp.float32), corner_vals, precision=lax.Precision.HIGHEST)
    live_mask = jnp.arange(panel_rows)[None, :] < 3 * panel_nodes[0][:, None]
    reduced = (force.reshape(3 * node_count, load_cases).astype(jnp.float32) - correction).reshape(
        panels, panel_rows, load_cases
    )
    reduced = jnp.where(live_mask[:, :, None], reduced, 0.0).astype(jnp.bfloat16)
    solved = jnp.einsum("prc,pcl->prl", panel_inv, reduced, preferred_element_type=jnp.float32)
    displaced = (
        jnp.where(live_mask[:, :, None], solved, 0.0)
        .astype(jnp.bfloat16)
        .reshape(node_count, 3 * load_cases)
    )
    elem_count = connect.shape[1]
    element = displaced[connect.T].reshape(elem_count, 24, load_cases)
    strain = jnp.einsum("ije,ejl->eil", strain_disp, element, preferred_element_type=jnp.float32)
    stress = (
        jnp.einsum("ik,ekl->eil", iso_matrix(), strain, precision=lax.Precision.HIGHEST)
        * modulus[:, None, None]
    )
    node_range = jnp.arange(node_count, dtype=jnp.int32)
    incidence = jnp.sum(
        (connect[:, None, :] == node_range[None, :, None]).astype(jnp.float32), axis=0
    )
    partial_value = jnp.dot(
        incidence, stress.reshape(elem_count, 6 * load_cases), precision=lax.Precision.HIGHEST
    ).reshape(node_count, 6, load_cases)
    node_ids = interface[0]
    picker = (node_ids[:, None] == node_range[None, :]).astype(jnp.float32)
    iface_rows = jnp.dot(
        picker, partial_value.reshape(node_count, 6 * load_cases), precision=lax.Precision.HIGHEST
    ).reshape(-1, 6, load_cases)
    start_edge = 2 * NIS + 2 * NIG
    faces_sub = iface_rows[: 2 * NIS].reshape(2, NIS, 6, load_cases)
    near_sub = padded(faces_sub, (("sub", 0),), 1)
    faces_sub = faces_sub + jnp.stack([near_sub[0], near_sub[3]])
    faces_grp = iface_rows[2 * NIS : start_edge].reshape(2, NIG, 6, load_cases)
    near_grp = padded(faces_grp, (("grp", 0),), 1)
    faces_grp = faces_grp + jnp.stack([near_grp[0], near_grp[3]])
    edge_block = iface_rows[start_edge:].reshape(2, 2, NED, 6, load_cases)
    beside_all = padded(edge_block, (("sub", 0), ("grp", 1)), 1)
    along_sub = jnp.stack([beside_all[0, 1:3], beside_all[3, 1:3]])
    along_grp = jnp.stack([beside_all[1:3, 0], beside_all[1:3, 3]], axis=1)
    diagonal = jnp.stack(
        [
            jnp.stack([beside_all[0, 0], beside_all[0, 3]]),
            jnp.stack([beside_all[3, 0], beside_all[3, 3]]),
        ]
    )
    edge_block = edge_block + along_sub + along_grp + diagonal
    summed_rows = jnp.concatenate(
        [
            faces_sub.reshape(-1, 6, load_cases),
            faces_grp.reshape(-1, 6, load_cases),
            edge_block.reshape(-1, 6, load_cases),
        ]
    )
    placed = jnp.dot(
        picker.T, summed_rows.reshape(-1, 6 * load_cases), precision=lax.Precision.HIGHEST
    ).reshape(node_count, 6, load_cases)
    on_face = jnp.sum(picker, axis=0) > 0.5
    summed = jnp.where(on_face[:, None, None], placed, partial_value)
    stress_out = (summed / nodal_volume[:, None, None]).astype(jnp.bfloat16)
    return (displaced.reshape(node_count, 3, load_cases), stress_out)


def solution(mesh):
    placed = (
        P(("sub", "grp"), None),
        P(("sub", "grp"), None),
        P(("sub", "grp"), None),
        P(("sub", "grp"), None, None),
        P(("sub", "grp"), None, None),
        P(("sub", "grp"), None),
        P(None, None, ("sub", "grp")),
        P(("sub", "grp")),
        P(None, ("sub", "grp")),
        P(("sub", "grp"), None),
        P(("sub", "grp")),
    )
    return jax.shard_map(
        shards,
        mesh=mesh,
        in_specs=placed,
        out_specs=(P(("sub", "grp"), None, None), P(("sub", "grp"), None, None)),
        check_vma=False,
    )
```

profile of v0, /device:TPU:121, one launch (start us, length us, event | category | flops | bytes accessed | tf_op | source)
XLA Modules:
  0.0 97.5 jit_solution(14922059316060356889)
XLA Ops:
  0.6 9.7 %all_gather.3 = f32[96,128]{1,0:T(8,128)S(1)} all-gather(f32[24,128]{1,0:T(8,128)} %param.11), channel_id=1, replica_groups=mesh['sub'=64,'grp'=4] {'grp'}, dimensions={0}, use_global_device_ids=true | all-gather | bytes 61440 | tf_op jit(solution)/shard_map/all_gather | solution.py:57
  10.4 5.5 %collective-permute-start.1 = (f32[96,128]{1,0:T(8,128)S(1)}, f32[96,128]{1,0:T(8,128)S(1)}, u32[]{:S(2)}, u32[]{:S(2)}) collective-permute-start(f32[96,128]{1,0:T(8,128)S(1)} %all_gather.3), channel_id=1, source_target_pairs={{4,0},{8,4},{12,8},{16,12},{20,16},{24,20},{28,24},{32,28},{36,32}... | collective-permute-start | bytes 147464 | tf_op jit(solution)/shard_map/ppermute | solution.py:22
  15.8 4.3 %collective-permute-start = (f32[96,128]{1,0:T(8,128)S(1)}, f32[96,128]{1,0:T(8,128)S(1)}, u32[]{:S(2)}, u32[]{:S(2)}) collective-permute-start(f32[96,128]{1,0:T(8,128)S(1)} %all_gather.3), channel_id=1, source_target_pairs={{0,4},{4,8},{8,12},{12,16},{16,20},{20,24},{24,28},{28,32},{32,36}... | collective-permute-start | bytes 147464 | tf_op jit(solution)/shard_map/ppermute | solution.py:19
  20.8 1.6 %convert_reduce_fusion = f32[512,128]{1,0:T(8,128)} fusion(s32[8,128]{1,0:T(8,128)} %param.19), kind=kLoop, calls=%fused_computation.3 | loop fusion | flops 1507328 | bytes 266240 | tf_op jit(solution)/shard_map/reduce_sum | solution.py:90
  24.1 1.6 %copy.35 = bf16[6,24,128]{1,0,2:T(8,128)(2,1)} copy(bf16[6,24,128]{2,1,0:T(8,128)(2,1)} %param.17) | data formatting | bytes 73728 | tf_op args[6]
  25.7 1.3 %copy.29 = f32[512,3,128]{2,1,0:T(4,128)S(1)} copy(bf16[512,3,128]{2,0,1:T(8,128)(2,1)} %param.14) | data formatting | bytes 1179648 | tf_op jit(solution)/shard_map/convert_element_type | solution.py:72
  27.1 1.2 %reshape.111 = f32[1536,128]{1,0:T(8,128)} reshape(f32[512,3,128]{2,1,0:T(4,128)S(1)} %copy.29) | data formatting | bytes 1572864 | tf_op jit(solution)/shard_map/convert_element_type | solution.py:72
  28.3 1.4 %copy.30 = f32[1536,128]{0,1:T(8,128)S(1)} copy(f32[1536,128]{1,0:T(8,128)} %reshape.111) | data formatting | bytes 1572864 | tf_op jit(solution)/shard_map/convert_element_type | solution.py:72
  31.4 3.9 %gather_fusion = bf16[1024,384]{1,0:T(8,128)(2,1)S(1)} fusion(bf16[512,384]{1,0:T(8,128)(2,1)S(1)} %reshape.106, s32[1024]{0:T(1024)S(1)} %broadcast_clamp_fusion), kind=kCustom, calls=%fused_computation | custom fusion | bytes 1576960 | tf_op jit(solution)/shard_map/gather | solution.py:83
  35.8 1.3 %convolution_bitcast_fusion.1 = f32[128,6,128]{2,1,0:T(8,128)S(1)} fusion(bf16[128,24,128]{2,1,0:T(8,128)(2,1)S(1)} %reshape.107, bf16[6,24,128]{1,0,2:T(8,128)(2,1)} %copy.35), kind=kOutput, calls=%fused_computation.10 | convolution fusion | flops 4718592 | bytes 1216512 | tf_op jit(solution)/shard_map/ije,ejl->eil/dot_general | solution.py:84
  37.9 2.3 %fusion.37 = f32[512,768]{1,0:T(8,128)S(1)} fusion(f32[512,128]{1,0:T(8,128)} %convert_reduce_fusion, f32[128,768]{0,1:T(8,128)S(1)} %bitcast.76), kind=kOutput, calls=%fused_computation.75 | convolution fusion | flops 603979776 | bytes 2228224 | tf_op jit(solution)/shard_map/dot_general | solution.py:93
  41.3 2.4 %collective-permute-start.6 = (f32[1,2,8,6,128]{4,2,3,1,0:T(8,128)S(1)}, f32[1,2,8,6,128]{4,2,3,1,0:T(8,128)S(1)}, u32[]{:S(2)}, u32[]{:S(2)}) collective-permute-start(f32[1,2,8,6,128]{4,2,3,1,0:T(8,128)S(1)} %get-tuple-element.12), channel_id=1, source_target_pairs={{0,4},{4,8},{8,12},{12,16},{16,20},{20,24},{24,28},{28,32},{32,36}... | collective-permute-start | bytes 147464 | tf_op jit(solution)/shard_map/ppermute | solution.py:19
  43.7 1.9 %collective-permute-start.7 = (f32[1,2,8,6,128]{4,2,3,1,0:T(8,128)S(1)}, f32[1,2,8,6,128]{4,2,3,1,0:T(8,128)S(1)}, u32[]{:S(2)}, u32[]{:S(2)}) collective-permute-start(f32[1,2,8,6,128]{4,2,3,1,0:T(8,128)S(1)} %get-tuple-element.13), channel_id=1, source_target_pairs={{4,0},{8,4},{12,8},{16,12},{20,16},{24,20},{28,24},{32,28},{36,32}... | collective-permute-start | bytes 147464 | tf_op jit(solution)/shard_map/ppermute | solution.py:22
  45.6 6.8 %collective-permute-done.7 = f32[1,2,8,6,128]{4,2,3,1,0:T(8,128)S(1)} collective-permute-done((f32[1,2,8,6,128]{4,2,3,1,0:T(8,128)S(1)}, f32[1,2,8,6,128]{4,2,3,1,0:T(8,128)S(1)}, u32[]{:S(2)}, u32[]{:S(2)}) %collective-permute-start.7) | collective-permute-done | bytes 49184 | tf_op jit(solution)/shard_map/ppermute | solution.py:22
  52.4 2.8 %collective-permute-start.8 = (f32[4,1,8,6,128]{4,2,3,1,0:T(8,128)S(1)}, f32[4,1,8,6,128]{4,2,3,1,0:T(8,128)S(1)}, u32[]{:S(2)}, u32[]{:S(2)}) collective-permute-start(f32[4,1,8,6,128]{4,2,3,1,0:T(8,128)S(1)} %get-tuple-element.14), channel_id=1, source_target_pairs={{0,1},{1,2},{2,3},{4,5},{5,6},{6,7},{8,9},{9,10},{10,11},{12,13},{... | collective-permute-start | bytes 294920 | tf_op jit(solution)/shard_map/ppermute | solution.py:19
  55.3 1.3 %collective-permute-start.9 = (f32[4,1,8,6,128]{4,2,3,1,0:T(8,128)S(1)}, f32[4,1,8,6,128]{4,2,3,1,0:T(8,128)S(1)}, u32[]{:S(2)}, u32[]{:S(2)}) collective-permute-start(f32[4,1,8,6,128]{4,2,3,1,0:T(8,128)S(1)} %get-tuple-element.15), channel_id=1, source_target_pairs={{1,0},{2,1},{3,2},{5,4},{6,5},{7,6},{9,8},{10,9},{11,10},{13,12},{... | collective-permute-start | bytes 294920 | tf_op jit(solution)/shard_map/ppermute | solution.py:22
  56.9 3.7 %collective-permute-done.9 = f32[4,1,8,6,128]{4,2,3,1,0:T(8,128)S(1)} collective-permute-done((f32[4,1,8,6,128]{4,2,3,1,0:T(8,128)S(1)}, f32[4,1,8,6,128]{4,2,3,1,0:T(8,128)S(1)}, u32[]{:S(2)}, u32[]{:S(2)}) %collective-permute-start.9) | collective-permute-done | bytes 98336 | tf_op jit(solution)/shard_map/ppermute | solution.py:22
  61.4 1.6 %slice.85 = f32[1,32,6,128]{3,2,1,0:T(8,128)} reshape(f32[32,768]{1,0:T(8,128)} %get-tuple-element.9) | data formatting | bytes 196608 | tf_op jit(solution)/shard_map/slice | solution.py:20
  63.7 1.3 %collective-permute-start.5 = (f32[1,32,6,128]{3,2,1,0:T(8,128)}, f32[1,32,6,128]{3,2,1,0:T(8,128)S(1)}, u32[]{:S(2)}, u32[]{:S(2)}) collective-permute-start(f32[1,32,6,128]{3,2,1,0:T(8,128)} %slice.87), channel_id=1, source_target_pairs={{1,0},{2,1},{3,2},{5,4},{6,5},{7,6},{9,8},{10,9},{11,10},{13,12},{... | collective-permute-start | bytes 294920 | tf_op jit(solution)/shard_map/ppermute | solution.py:22
  65.0 4.0 %collective-permute-start.4 = (f32[1,32,6,128]{3,2,1,0:T(8,128)}, f32[1,32,6,128]{3,2,1,0:T(8,128)S(1)}, u32[]{:S(2)}, u32[]{:S(2)}) collective-permute-start(f32[1,32,6,128]{3,2,1,0:T(8,128)} %slice.85), channel_id=1, source_target_pairs={{0,1},{1,2},{2,3},{4,5},{5,6},{6,7},{8,9},{9,10},{10,11},{12,13},{... | collective-permute-start | bytes 294920 | tf_op jit(solution)/shard_map/ppermute | solution.py:19
  69.6 1.6 %collective-permute-done.4 = f32[1,32,6,128]{3,2,1,0:T(8,128)S(1)} collective-permute-done((f32[1,32,6,128]{3,2,1,0:T(8,128)}, f32[1,32,6,128]{3,2,1,0:T(8,128)S(1)}, u32[]{:S(2)}, u32[]{:S(2)}) %collective-permute-start.4) | collective-permute-done | bytes 98336 | tf_op jit(solution)/shard_map/ppermute | solution.py:19
  72.1 1.7 %slice.80 = f32[1,64,6,128]{3,2,1,0:T(8,128)} reshape(f32[64,768]{1,0:T(8,128)} %get-tuple-element.6) | data formatting | bytes 393216 | tf_op jit(solution)/shard_map/slice | solution.py:20
  73.8 1.7 %slice.82 = f32[1,64,6,128]{3,2,1,0:T(8,128)} reshape(f32[64,768]{1,0:T(8,128)} %get-tuple-element.8) | data formatting | bytes 393216 | tf_op jit(solution)/shard_map/slice | solution.py:22
  75.4 1.9 %collective-permute-start.3 = (f32[1,64,6,128]{3,2,1,0:T(8,128)}, f32[1,64,6,128]{3,2,1,0:T(8,128)}, u32[]{:S(2)}, u32[]{:S(2)}) collective-permute-start(f32[1,64,6,128]{3,2,1,0:T(8,128)} %slice.82), channel_id=1, source_target_pairs={{4,0},{8,4},{12,8},{16,12},{20,16},{24,20},{28,24},{32,28},{36,32}... | collective-permute-start | bytes 589832 | tf_op jit(solution)/shard_map/ppermute | solution.py:22
  77.3 7.0 %collective-permute-start.2 = (f32[1,64,6,128]{3,2,1,0:T(8,128)}, f32[1,64,6,128]{3,2,1,0:T(8,128)}, u32[]{:S(2)}, u32[]{:S(2)}) collective-permute-start(f32[1,64,6,128]{3,2,1,0:T(8,128)} %slice.80), channel_id=1, source_target_pairs={{0,4},{4,8},{8,12},{12,16},{16,20},{20,24},{24,28},{28,32},{32,36}... | collective-permute-start | bytes 589832 | tf_op jit(solution)/shard_map/ppermute | solution.py:19
  84.3 2.1 %reshape_reshape.3 = bf16[512,3,128]{2,1,0:T(4,128)(2,1)} reshape(bf16[4,384,128]{2,1,0:T(8,128)(2,1)} %copy-done.1) | data formatting | bytes 786432 | tf_op jit(solution)/shard_map/reshape;reshape | solution.py:132
  86.4 1.6 %copy.39 = f32[512,768]{0,1:T(8,128)} copy(f32[512,768]{1,0:T(8,128)S(1)} %fusion.37) | data formatting | bytes 3145728 | tf_op jit(solution)/shard_map/dot_general | solution.py:93
  88.1 1.8 %copy.41 = bf16[512,3,128]{2,0,1:T(8,128)(2,1)} copy(bf16[512,3,128]{2,1,0:T(4,128)(2,1)} %reshape_reshape.3) | data formatting | bytes 786432
  89.9 1.9 %copy.40 = f32[512,6,128]{2,0,1:T(8,128)S(1)} copy(f32[512,6,128]{0,2,1:T(8,128)} %bitcast.74) | data formatting | bytes 3145728 | tf_op jit(solution)/shard_map/reshape | solution.py:95
  91.8 1.1 %pad_maximum_fusion = f32[2,64,6,128]{3,2,1,0:T(8,128)S(1)} fusion(f32[1,64,6,128]{3,2,1,0:T(8,128)} %collective-permute-done.3, f32[1,64,6,128]{3,2,1,0:T(8,128)} %collective-permute-done.2), kind=kLoop, calls=%fused_computation.15 | loop fusion | flops 98304 | bytes 786432 | tf_op jit(solution)/shard_map/stack | solution.py:104
  93.1 1.2 %copy.37 = f32[768,224]{1,0:T(8,128)} copy(f32[768,224]{0,1:T(8,128)S(1)} %maximum_bitcast_fusion) | data formatting | bytes 1376256 | tf_op jit(solution)/shard_map/dot_general | solution.py:126
  94.3 3.2 %divide_convert_fusion = bf16[512,6,128]{2,0,1:T(8,128)(2,1)} fusion(f32[512,6,128]{2,0,1:T(8,128)S(1)} %copy.40, f32[6,128,224]{2,1,0:T(8,128)} %bitcast.78, f32[512]{0:T(512)S(1)} %copy-done.7, pred[512]{0:T(512)(128)(4,1)S(1)} %broadcast_compare_fusion, s32[224]{0:T(256)S(1)} %bitcast.86), kind=kOutput, calls=%fused_computation.5 | convolution fusion | flops 1058373632 | bytes 3050880 | tf_op jit(solution)/shard_map/dot_general | solution.py:126
  (61 shorter events, 9.6 us)
Async XLA Ops:
  0.6 29.9 %copy-start = (bf16[4,384,384]{2,1,0:T(8,128)(2,1)S(1)}, bf16[4,384,384]{2,1,0:T(8,128)(2,1)}, u32[]{:S(2)}) copy-start(bf16[4,384,384]{2,1,0:T(8,128)(2,1)} %param.15) | copy-start | bytes 3538948
  10.4 19.3 %collective-permute-start.1 = (f32[96,128]{1,0:T(8,128)S(1)}, f32[96,128]{1,0:T(8,128)S(1)}, u32[]{:S(2)}, u32[]{:S(2)}) collective-permute-start(f32[96,128]{1,0:T(8,128)S(1)} %all_gather.3), channel_id=1, source_target_pairs={{4,0},{8,4},{12,8},{16,12},{20,16},{24,20},{28,24},{32,28},{36,32}... | collective-permute-start | bytes 147464 | tf_op jit(solution)/shard_map/ppermute | solution.py:22
  15.8 13.9 %collective-permute-start = (f32[96,128]{1,0:T(8,128)S(1)}, f32[96,128]{1,0:T(8,128)S(1)}, u32[]{:S(2)}, u32[]{:S(2)}) collective-permute-start(f32[96,128]{1,0:T(8,128)S(1)} %all_gather.3), channel_id=1, source_target_pairs={{0,4},{4,8},{8,12},{12,16},{16,20},{20,24},{24,28},{28,32},{32,36}... | collective-permute-start | bytes 147464 | tf_op jit(solution)/shard_map/ppermute | solution.py:19
  27.0 2.9 %copy-start.4 = (bf16[1536,24]{0,1:T(8,128)(2,1)S(1)}, bf16[1536,24]{0,1:T(8,128)(2,1)}, u32[]{:S(2)}) copy-start(bf16[1536,24]{0,1:T(8,128)(2,1)} %param.13) | copy-start | bytes 221188
  31.2 4.1 %copy-start.1 = (bf16[4,384,128]{2,1,0:T(8,128)(2,1)}, bf16[4,384,128]{2,1,0:T(8,128)(2,1)S(1)}, u32[]{:S(2)}) copy-start(bf16[4,384,128]{2,1,0:T(8,128)(2,1)S(1)} %copy.32) | copy-start | bytes 1179652
  35.4 1.7 %copy-start.6 = (f32[128]{0:T(128)S(1)}, f32[128]{0:T(128)}, u32[]{:S(2)}) copy-start(f32[128]{0:T(128)} %param.18) | copy-start | bytes 1540
  37.7 2.6 %copy-start.5 = (s32[1,224]{1,0:T(1,128)S(1)}, s32[1,224]{1,0:T(1,128)}, u32[]{:S(2)}) copy-start(s32[1,224]{1,0:T(1,128)} %param.20) | copy-start | bytes 2692
  41.3 4.4 %collective-permute-start.6 = (f32[1,2,8,6,128]{4,2,3,1,0:T(8,128)S(1)}, f32[1,2,8,6,128]{4,2,3,1,0:T(8,128)S(1)}, u32[]{:S(2)}, u32[]{:S(2)}) collective-permute-start(f32[1,2,8,6,128]{4,2,3,1,0:T(8,128)S(1)} %get-tuple-element.12), channel_id=1, source_target_pairs={{0,4},{4,8},{8,12},{12,16},{16,20},{20,24},{24,28},{28,32},{32,36}... | collective-permute-start | bytes 147464 | tf_op jit(solution)/shard_map/ppermute | solution.py:19
  43.7 8.7 %collective-permute-start.7 = (f32[1,2,8,6,128]{4,2,3,1,0:T(8,128)S(1)}, f32[1,2,8,6,128]{4,2,3,1,0:T(8,128)S(1)}, u32[]{:S(2)}, u32[]{:S(2)}) collective-permute-start(f32[1,2,8,6,128]{4,2,3,1,0:T(8,128)S(1)} %get-tuple-element.13), channel_id=1, source_target_pairs={{4,0},{8,4},{12,8},{16,12},{20,16},{24,20},{28,24},{32,28},{36,32}... | collective-permute-start | bytes 147464 | tf_op jit(solution)/shard_map/ppermute | solution.py:22
  52.4 4.5 %collective-permute-start.8 = (f32[4,1,8,6,128]{4,2,3,1,0:T(8,128)S(1)}, f32[4,1,8,6,128]{4,2,3,1,0:T(8,128)S(1)}, u32[]{:S(2)}, u32[]{:S(2)}) collective-permute-start(f32[4,1,8,6,128]{4,2,3,1,0:T(8,128)S(1)} %get-tuple-element.14), channel_id=1, source_target_pairs={{0,1},{1,2},{2,3},{4,5},{5,6},{6,7},{8,9},{9,10},{10,11},{12,13},{... | collective-permute-start | bytes 294920 | tf_op jit(solution)/shard_map/ppermute | solution.py:19
  55.3 5.4 %collective-permute-start.9 = (f32[4,1,8,6,128]{4,2,3,1,0:T(8,128)S(1)}, f32[4,1,8,6,128]{4,2,3,1,0:T(8,128)S(1)}, u32[]{:S(2)}, u32[]{:S(2)}) collective-permute-start(f32[4,1,8,6,128]{4,2,3,1,0:T(8,128)S(1)} %get-tuple-element.15), channel_id=1, source_target_pairs={{1,0},{2,1},{3,2},{5,4},{6,5},{7,6},{9,8},{10,9},{11,10},{13,12},{... | collective-permute-start | bytes 294920 | tf_op jit(solution)/shard_map/ppermute | solution.py:22
  63.7 5.9 %collective-permute-start.5 = (f32[1,32,6,128]{3,2,1,0:T(8,128)}, f32[1,32,6,128]{3,2,1,0:T(8,128)S(1)}, u32[]{:S(2)}, u32[]{:S(2)}) collective-permute-start(f32[1,32,6,128]{3,2,1,0:T(8,128)} %slice.87), channel_id=1, source_target_pairs={{1,0},{2,1},{3,2},{5,4},{6,5},{7,6},{9,8},{10,9},{11,10},{13,12},{... | collective-permute-start | bytes 294920 | tf_op jit(solution)/shard_map/ppermute | solution.py:22
  65.0 6.2 %collective-permute-start.4 = (f32[1,32,6,128]{3,2,1,0:T(8,128)}, f32[1,32,6,128]{3,2,1,0:T(8,128)S(1)}, u32[]{:S(2)}, u32[]{:S(2)}) collective-permute-start(f32[1,32,6,128]{3,2,1,0:T(8,128)} %slice.85), channel_id=1, source_target_pairs={{0,1},{1,2},{2,3},{4,5},{5,6},{6,7},{8,9},{9,10},{10,11},{12,13},{... | collective-permute-start | bytes 294920 | tf_op jit(solution)/shard_map/ppermute | solution.py:19
  75.4 16.4 %collective-permute-start.3 = (f32[1,64,6,128]{3,2,1,0:T(8,128)}, f32[1,64,6,128]{3,2,1,0:T(8,128)}, u32[]{:S(2)}, u32[]{:S(2)}) collective-permute-start(f32[1,64,6,128]{3,2,1,0:T(8,128)} %slice.82), channel_id=1, source_target_pairs={{4,0},{8,4},{12,8},{16,12},{20,16},{24,20},{28,24},{32,28},{36,32}... | collective-permute-start | bytes 589832 | tf_op jit(solution)/shard_map/ppermute | solution.py:22
  77.3 14.5 %collective-permute-start.2 = (f32[1,64,6,128]{3,2,1,0:T(8,128)}, f32[1,64,6,128]{3,2,1,0:T(8,128)}, u32[]{:S(2)}, u32[]{:S(2)}) collective-permute-start(f32[1,64,6,128]{3,2,1,0:T(8,128)} %slice.80), channel_id=1, source_target_pairs={{0,4},{4,8},{8,12},{12,16},{16,20},{20,24},{24,28},{28,32},{32,36}... | collective-permute-start | bytes 589832 | tf_op jit(solution)/shard_map/ppermute | solution.py:19
  91.8 1.3 %copy-start.2 = (f32[64,768]{1,0:T(8,128)S(1)}, f32[64,768]{1,0:T(8,128)}, u32[]{:S(2)}) copy-start(f32[64,768]{1,0:T(8,128)} %get-tuple-element.7) | copy-start | bytes 589828
  91.8 1.3 %copy-start.3 = (f32[32,768]{1,0:T(8,128)S(1)}, f32[32,768]{1,0:T(8,128)}, u32[]{:S(2)}) copy-start(f32[32,768]{1,0:T(8,128)} %get-tuple-element.10) | copy-start | bytes 294916
  93.1 1.2 %copy-start.7 = (f32[512]{0:T(512)S(1)}, f32[512]{0:T(512)}, u32[]{:S(2)}) copy-start(f32[512]{0:T(512)} %param.21) | copy-start | bytes 6148
where the time goes:
time: 98.9 us; the launch traced here: 97.5 us
  starting transfers between devices  32.4 us (33%)
  local copies, waits for them, and re-layouts  24.9 us (25%)
  waiting for transfers between devices  12.9 us (13%)
  blocking collectives  9.72 us (10%)
  matrix products  9.65 us (10%)
  other arithmetic  6.77 us (7%)
  between operations  1.1 us (1%)
    ppermute x5, starting transfers between devices, padded(): lax.ppermute(lax.slice_in_dim(block, block.shape[dim] - width, None, axis...  20.5 us
    ppermute x5, starting transfers between devices, padded(): lax.ppermute(lax.slice_in_dim(block, 0, width, axis=dim), axis, backward)  11.9 us
    ppermute x5, waiting for transfers between devices, padded(): lax.ppermute(lax.slice_in_dim(block, 0, width, axis=dim), axis, backward)  11 us
    all_gather x1, blocking collectives, shards(): group_rows = lax.all_gather(coarse, 'grp', axis=0, tiled=True)  9.72 us
    convert_element_type x3, local copies, waits for them, and re-layouts, shards(): force.reshape(3 * node_count, load_cases).astype(jnp.float32) - correction  3.97 us
    gather x1, local copies, waits for them, and re-layouts, shards(): element = displaced[connect.T].reshape(elem_count, 24, load_cases)  3.92 us
    unnamed x18, local copies, waits for them, and re-layouts  3.52 us
    slice x4, local copies, waits for them, and re-layouts, padded(): lax.slice_in_dim(block, block.shape[dim] - width, None, axis=dim)  3.25 us
  transfers between devices with their start and end apart: 10, of which 5 were waited for; matrix products, arithmetic and copies ran while one was open for 18% of the time, Pallas kernels for 0%

commit v1 on v0

v1 whole, which is shorter than its diff:
```python
import functools

import jax
import jax.numpy as jnp
import numpy as np
from jax import lax
from jax.experimental import pallas as pl
from jax.experimental.pallas import tpu as pltpu
from jax.sharding import PartitionSpec as P

NIS = 64
NIG = 32
NED = 8

MESH = pl.DeviceIdType.MESH

POISSON = 0.3

SUB_LO = np.arange(0, NIS)
SUB_HI = np.arange(NIS, 2 * NIS)
GRP_LO = np.arange(2 * NIS, 2 * NIS + NIG)
GRP_HI = np.arange(2 * NIS + NIG, 2 * NIS + 2 * NIG)
_E0 = 2 * NIS + 2 * NIG
EDGE_LL = np.arange(_E0, _E0 + NED)
EDGE_LH = np.arange(_E0 + NED, _E0 + 2 * NED)
EDGE_HL = np.arange(_E0 + 2 * NED, _E0 + 3 * NED)
EDGE_HH = np.arange(_E0 + 3 * NED, _E0 + 4 * NED)

DIRECTIONS = (
    (1, 0, (SUB_HI, EDGE_HL, EDGE_HH), (SUB_LO, EDGE_LL, EDGE_LH)),
    (-1, 0, (SUB_LO, EDGE_LL, EDGE_LH), (SUB_HI, EDGE_HL, EDGE_HH)),
    (0, 1, (GRP_HI, EDGE_LH, EDGE_HH), (GRP_LO, EDGE_LL, EDGE_HL)),
    (0, -1, (GRP_LO, EDGE_LL, EDGE_HL), (GRP_HI, EDGE_LH, EDGE_HH)),
    (1, 1, (EDGE_HH,), (EDGE_LL,)),
    (1, -1, (EDGE_HL,), (EDGE_LH,)),
    (-1, 1, (EDGE_LH,), (EDGE_HL,)),
    (-1, -1, (EDGE_LL,), (EDGE_HH,)),
)
SEND_ENTRIES = np.concatenate([np.concatenate(d[2]) for d in DIRECTIONS])
RECV_ENTRIES = np.concatenate([np.concatenate(d[3]) for d in DIRECTIONS])
SLOT_ROWS = [sum(len(x) for x in d[2]) for d in DIRECTIONS]
SLOT_START = np.concatenate([[0], np.cumsum(SLOT_ROWS)])


def iso_matrix():
    lame_first = POISSON / ((1.0 + POISSON) * (1.0 - 2.0 * POISSON))
    shear_mod = 0.5 / (1.0 + POISSON)
    upper_block = jnp.full((3, 3), lame_first, jnp.float32) + jnp.eye(3, dtype=jnp.float32) * (
        2.0 * shear_mod
    )
    shear_block = jnp.eye(3, dtype=jnp.float32) * shear_mod
    zero_block = jnp.zeros((3, 3), jnp.float32)
    return jnp.concatenate(
        [
            jnp.concatenate([upper_block, zero_block], 1),
            jnp.concatenate([zero_block, shear_block], 1),
        ],
        0,
    )


def _above(i, n):
    return (i + n - 1) // n


def _below(i, n):
    return (2 * n - 2 - i) // n


def _step_ok(i, d, n):
    if d < 0:
        return _above(i, n)
    if d > 0:
        return _below(i, n)
    return 1


def coarse_kernel(n_sub, n_grp, block_ref, out_ref, buf, send_sem, recv_sem):
    s = lax.axis_index("sub")
    g = lax.axis_index("grp")
    barrier = pltpu.get_barrier_semaphore()

    def peers():
        for ds in (-1, 0, 1):
            for gt in range(n_grp):
                yield ds, gt

    def exists(ds, gt):
        conds = []
        if ds < 0:
            conds.append(s + ds >= 0)
        if ds > 0:
            conds.append(s + ds < n_sub)
        if ds == 0:
            conds.append(g != gt)
        cond = conds[0]
        for c in conds[1:]:
            cond = jnp.logical_and(cond, c)
        return cond

    for ds, gt in peers():
        def signal(ds=ds, gt=gt):
            pl.semaphore_signal(barrier, inc=1, device_id=(s + ds, gt), device_id_type=MESH)
        pl.when(exists(ds, gt))(signal)
    count = (n_grp - 1) + n_grp * (_above(s, n_sub) + _below(s, n_sub))
    pl.semaphore_wait(barrier, count)

    copies = []
    for ds, gt in peers():
        slot_there = (1 - ds) * n_grp + g
        copy = pltpu.make_async_remote_copy(
            src_ref=block_ref,
            dst_ref=buf.at[slot_there],
            send_sem=send_sem.at[(ds + 1) * n_grp + gt],
            recv_sem=recv_sem.at[slot_there],
            device_id=(s + ds, gt),
            device_id_type=MESH,
        )
        pl.when(exists(ds, gt))(copy.start)
        copies.append(copy)
    for (ds, gt), copy in zip(peers(), copies):
        pl.when(exists(ds, gt))(copy.wait_send)
    for dr in (-1, 0, 1):
        for gr in range(n_grp):
            slot_here = (dr + 1) * n_grp + gr
            recv = pltpu.make_async_remote_copy(
                src_ref=block_ref,
                dst_ref=buf.at[slot_here],
                send_sem=send_sem.at[slot_here],
                recv_sem=recv_sem.at[slot_here],
                device_id=(s + dr, gr),
                device_id_type=MESH,
            )
            cond = exists(dr, gr)

            def take(slot_here=slot_here, recv=recv):
                recv.wait_recv()
                out_ref[slot_here] = buf[slot_here]

            def clear(slot_here=slot_here):
                out_ref[slot_here] = jnp.zeros(out_ref.shape[1:], out_ref.dtype)

            pl.when(cond)(take)
            def own(slot_here=slot_here):
                out_ref[slot_here] = block_ref[...]

            if dr == 0:
                pl.when(g == gr)(own)
            else:
                pl.when(jnp.logical_not(cond))(clear)


def face_kernel(n_sub, n_grp, send_ref, out_ref, buf, send_sem, recv_sem):
    s = lax.axis_index("sub")
    g = lax.axis_index("grp")
    barrier = pltpu.get_barrier_semaphore()

    def exists(ds, dg):
        conds = []
        if ds < 0:
            conds.append(s + ds >= 0)
        if ds > 0:
            conds.append(s + ds < n_sub)
        if dg < 0:
            conds.append(g + dg >= 0)
        if dg > 0:
            conds.append(g + dg < n_grp)
        cond = conds[0]
        for c in conds[1:]:
            cond = jnp.logical_and(cond, c)
        return cond

    for ds, dg, _, _ in DIRECTIONS:
        def signal(ds=ds, dg=dg):
            pl.semaphore_signal(barrier, inc=1, device_id=(s + ds, g + dg), device_id_type=MESH)
        pl.when(exists(ds, dg))(signal)
    count = 0
    for ds, dg, _, _ in DIRECTIONS:
        count = count + _step_ok(s, ds, n_sub) * _step_ok(g, dg, n_grp)
    pl.semaphore_wait(barrier, count)

    copies = []
    for k, (ds, dg, _, _) in enumerate(DIRECTIONS):
        rows = pl.ds(int(SLOT_START[k]), int(SLOT_ROWS[k]))
        copy = pltpu.make_async_remote_copy(
            src_ref=send_ref.at[rows],
            dst_ref=buf.at[rows],
            send_sem=send_sem.at[k],
            recv_sem=recv_sem.at[k],
            device_id=(s + ds, g + dg),
            device_id_type=MESH,
        )
        pl.when(exists(ds, dg))(copy.start)
        copies.append(copy)
    for k, (ds, dg, _, _) in enumerate(DIRECTIONS):
        pl.when(exists(ds, dg))(copies[k].wait_send)
    for k, (ds, dg, _, _) in enumerate(DIRECTIONS):
        rows = pl.ds(int(SLOT_START[k]), int(SLOT_ROWS[k]))
        cond = exists(-ds, -dg)

        def take(rows=rows, k=k):
            copies[k].wait_recv()
            out_ref[rows, :] = buf[rows, :]

        def clear(rows=rows):
            out_ref[rows, :] = jnp.zeros((rows.size, out_ref.shape[1]), out_ref.dtype)

        pl.when(cond)(take)
        pl.when(jnp.logical_not(cond))(clear)


def fetch_coarse(block, n_sub, n_grp):
    rows, width = block.shape
    slots = 3 * n_grp
    out = pl.pallas_call(
        functools.partial(coarse_kernel, n_sub, n_grp),
        out_shape=jax.ShapeDtypeStruct((slots, rows, width), block.dtype),
        in_specs=[pl.BlockSpec(memory_space=pltpu.VMEM)],
        out_specs=pl.BlockSpec(memory_space=pltpu.VMEM),
        scratch_shapes=[
            pltpu.VMEM((slots, rows, width), block.dtype),
            pltpu.SemaphoreType.DMA((slots,)),
            pltpu.SemaphoreType.DMA((slots,)),
        ],
        compiler_params=pltpu.CompilerParams(collective_id=0, has_side_effects=True),
    )(block)
    return out.reshape(slots * rows, width)


def exchange_faces(send, n_sub, n_grp):
    return pl.pallas_call(
        functools.partial(face_kernel, n_sub, n_grp),
        out_shape=jax.ShapeDtypeStruct(send.shape, send.dtype),
        in_specs=[pl.BlockSpec(memory_space=pltpu.VMEM)],
        out_specs=pl.BlockSpec(memory_space=pltpu.VMEM),
        scratch_shapes=[
            pltpu.VMEM(send.shape, send.dtype),
            pltpu.SemaphoreType.DMA((len(DIRECTIONS),)),
            pltpu.SemaphoreType.DMA((len(DIRECTIONS),)),
        ],
        compiler_params=pltpu.CompilerParams(collective_id=1, has_side_effects=True),
    )(send)


def shards(
    n_sub,
    n_grp,
    coarse,
    corner_idx,
    coupling,
    force,
    panel_inv,
    panel_nodes,
    strain_disp,
    modulus,
    connect,
    interface,
    nodal_volume,
):
    nearby = fetch_coarse(coarse, n_sub, n_grp)
    block_rows = n_grp * coarse.shape[0]
    offset = (lax.axis_index("sub") - 1) * block_rows
    local_rows = corner_idx[0] - offset
    selector = (local_rows[:, None] == jnp.arange(3 * block_rows, dtype=jnp.int32)[None, :]).astype(
        jnp.float32
    )
    corner_vals = jnp.dot(selector, nearby, precision=lax.Precision.HIGHEST)
    node_count = force.shape[0]
    load_cases = force.shape[2]
    panels = panel_inv.shape[0]
    panel_rows = panel_inv.shape[1]
    correction = jnp.dot(coupling.astype(jnp.float32), corner_vals, precision=lax.Precision.HIGHEST)
    live_mask = jnp.arange(panel_rows)[None, :] < 3 * panel_nodes[0][:, None]
    reduced = (force.reshape(3 * node_count, load_cases).astype(jnp.float32) - correction).reshape(
        panels, panel_rows, load_cases
    )
    reduced = jnp.where(live_mask[:, :, None], reduced, 0.0).astype(jnp.bfloat16)
    solved = jnp.einsum("prc,pcl->prl", panel_inv, reduced, preferred_element_type=jnp.float32)
    displaced = (
        jnp.where(live_mask[:, :, None], solved, 0.0)
        .astype(jnp.bfloat16)
        .reshape(node_count, 3 * load_cases)
    )
    elem_count = connect.shape[1]
    element = displaced[connect.T].reshape(elem_count, 24, load_cases)
    strain = jnp.einsum("ije,ejl->eil", strain_disp, element, preferred_element_type=jnp.float32)
    stress = (
        jnp.einsum("ik,ekl->eil", iso_matrix(), strain, precision=lax.Precision.HIGHEST)
        * modulus[:, None, None]
    )
    node_range = jnp.arange(node_count, dtype=jnp.int32)
    incidence = jnp.sum(
        (connect[:, None, :] == node_range[None, :, None]).astype(jnp.float32), axis=0
    )
    partial_value = jnp.dot(
        incidence, stress.reshape(elem_count, 6 * load_cases), precision=lax.Precision.HIGHEST
    )
    node_ids = interface[0]
    send_ids = node_ids[SEND_ENTRIES]
    recv_ids = node_ids[RECV_ENTRIES]
    send_pick = (send_ids[:, None] == node_range[None, :]).astype(jnp.float32)
    recv_pick = (recv_ids[:, None] == node_range[None, :]).astype(jnp.float32)
    send = jnp.dot(send_pick, partial_value, precision=lax.Precision.HIGHEST)
    received = exchange_faces(send, n_sub, n_grp)
    summed = partial_value + jnp.dot(recv_pick.T, received, precision=lax.Precision.HIGHEST)
    stress_out = (summed.reshape(node_count, 6, load_cases) / nodal_volume[:, None, None]).astype(
        jnp.bfloat16
    )
    return (displaced.reshape(node_count, 3, load_cases), stress_out)


def solution(mesh):
    n_sub = mesh.shape["sub"]
    n_grp = mesh.shape["grp"]
    placed = (
        P(("sub", "grp"), None),
        P(("sub", "grp"), None),
        P(("sub", "grp"), None),
        P(("sub", "grp"), None, None),
        P(("sub", "grp"), None, None),
        P(("sub", "grp"), None),
        P(None, None, ("sub", "grp")),
        P(("sub", "grp")),
        P(None, ("sub", "grp")),
        P(("sub", "grp"), None),
        P(("sub", "grp")),
    )
    return jax.shard_map(
        functools.partial(shards, n_sub, n_grp),
        mesh=mesh,
        in_specs=placed,
        out_specs=(P(("sub", "grp"), None, None), P(("sub", "grp"), None, None)),
        check_vma=False,
    )
```

time: 98.9 us -> 55.5 us (0.56); the launches traced: 97.5 us -> 55.1 us
  starting transfers between devices: 32.4 us -> 0 us
  Pallas kernels: 0 us -> 24.4 us
  waiting for transfers between devices: 12.9 us -> 0 us
  blocking collectives: 9.72 us -> 0 us
  local copies, waits for them, and re-layouts: 24.9 us -> 17.8 us
  other arithmetic: 6.77 us -> 1.43 us
    ppermute x10 -> x0, starting transfers between devices: 32.4 us -> none  [the longest x5 20.5 us: padded(): lax.ppermute(lax.slice_in_dim(block, block.shape[dim] - width, None, axis...]
    pallas_call x0 -> x2, Pallas kernels: none -> 24.4 us  [the longest x1 13 us: exchange_faces(): pl.pallas_call(functools.partial(face_kernel, n_sub, n_grp), out_shape=ja...]
    ppermute x10 -> x0, waiting for transfers between devices: 12.9 us -> none  [the longest x5 11 us: padded(): lax.ppermute(lax.slice_in_dim(block, 0, width, axis=dim), axis, backward)]
    all_gather x1 -> x0, blocking collectives: 9.72 us -> none  [shards(): group_rows = lax.all_gather(coarse, 'grp', axis=0, tiled=True)]
    slice x9 -> x0, local copies, waits for them, and re-layouts: 5.61 us -> none  [the longest x4 3.25 us: padded(): lax.slice_in_dim(block, block.shape[dim] - width, None, axis=dim)]
    gather x0 -> x2, local copies, waits for them, and re-layouts: none -> 4.91 us  [the longest x1 2.46 us: shards(): send_ids = node_ids[SEND_ENTRIES]]
    dot_general x2 -> x0, local copies, waits for them, and re-layouts: 2.81 us -> none  [the longest x1 1.65 us: shards(): jnp.dot(incidence, stress.reshape(elem_count, 6 * load_cases), precision=...]
    convert_element_type x3, local copies, waits for them, and re-layouts: 3.97 us -> 2.05 us  [shards(): force.reshape(3 * node_count, load_cases).astype(jnp.float32) - correction]
  transfers between devices with their start and end apart: 10 -> 0, of which waited for: 5 -> 0; matrix products, arithmetic and copies ran while one was open for 18% -> 0% of each run, Pallas kernels for 0% -> 0%
where the time goes in v1:
time: 55.5 us; the launch traced here: 55.1 us
  Pallas kernels  24.4 us (44%)
  local copies, waits for them, and re-layouts  17.8 us (32%)
  matrix products  10.5 us (19%)
  other arithmetic  1.43 us (3%)
  between operations  0.97 us (2%)
    pallas_call x1, Pallas kernels, exchange_faces(): pl.pallas_call(functools.partial(face_kernel, n_sub, n_grp), out_shape=ja...  13 us
    pallas_call x1, Pallas kernels, fetch_coarse(): pl.pallas_call(functools.partial(coarse_kernel, n_sub, n_grp), out_shape=...  11.3 us
    dot_general x1, matrix products, shards(): jnp.dot(recv_pick.T, received, precision=lax.Precision.HIGHEST)  3.94 us
    gather x1, local copies, waits for them, and re-layouts, shards(): element = displaced[connect.T].reshape(elem_count, 24, load_cases)  3.92 us
    unnamed x25, local copies, waits for them, and re-layouts  3.72 us
    gather x1, local copies, waits for them, and re-layouts, shards(): send_ids = node_ids[SEND_ENTRIES]  2.46 us
    gather x1, local copies, waits for them, and re-layouts, shards(): recv_ids = node_ids[RECV_ENTRIES]  2.46 us
    convert_element_type x3, local copies, waits for them, and re-layouts, shards(): force.reshape(3 * node_count, load_cases).astype(jnp.float32) - correction  2.05 us

profile of v1, /device:TPU:121, one launch (start us, length us, event | category | flops | bytes accessed | tf_op | source)
XLA Modules:
  0.0 55.1 jit_solution(13852086291512092960)
XLA Ops:
  0.6 0.0 copy-start
  0.6 1.4 %copy.30 = f32[512,3,128]{2,1,0:T(4,128)S(1)} copy(bf16[512,3,128]{2,0,1:T(8,128)(2,1)} %param.18) | data formatting | bytes 1179648 | tf_op jit(solution)/shard_map/convert_element_type | solution.py:274
  2.1 0.4 reshape.72
  2.5 0.3 copy.31
  2.8 11.3 %shard_map.158 = f32[12,24,128]{2,1,0:T(8,128)} custom-call(f32[24,128]{1,0:T(8,128)} %block_ref.1), custom_call_target="tpu_custom_call" | custom-call | tf_op jit(solution)/shard_map/pallas_call | solution.py:215
  14.1 1.1 %fusion.11 = f32[24,128]{1,0:T(8,128)S(1)} fusion(f32[288,128]{1,0:T(8,128)} %bitcast.44, s32[24]{0:T(128)S(1)} %subtract_bitcast_fusion), kind=kOutput, calls=%fused_computation.25 | convolution fusion | flops 10623744 | bytes 159840 | tf_op jit(solution)/shard_map/dot_general | solution.py:267
  15.2 0.5 fusion
  15.8 0.1 iota_compare_fusion.7
  15.9 0.5 fusion.3
  16.4 0.2 copy.33
  16.6 0.2 reshape.68
  16.8 0.1 copy.35
  16.9 0.1 reshape.75
  17.0 3.9 %gather_fusion = bf16[1024,384]{1,0:T(8,128)(2,1)S(1)} fusion(bf16[512,384]{1,0:T(8,128)(2,1)S(1)} %reshape.68, s32[1024]{0:T(1024)S(1)} %broadcast_clamp_fusion), kind=kCustom, calls=%fused_computation | custom fusion | bytes 1576960 | tf_op jit(solution)/shard_map/gather | solution.py:285
  21.0 0.4 reshape.69
  21.4 0.4 copy-done.3
  21.7 0.2 copy.36
  21.9 0.4 convolution_bitcast_fusion.1
  22.3 0.6 %fusion.2 = f32[128,6,128]{2,1,0:T(8,128)S(1)} fusion(f32[128,6,128]{2,1,0:T(8,128)S(1)} %convolution_bitcast_fusion.1, f32[128]{0:T(128)S(1)} %copy-done.8, f32[3,3]{1,0:T(4,128)S(1)} %get-tuple-element.7, f32[3,3]{1,0:T(4,128)S(1)} %get-tuple-element.6), kind=kOutput, calls=%fused_computation.12 | convolution fusion | flops 7176372 | bytes 787016 | tf_op jit(solution)/shard_map/ik,ekl->eil/dot_general | solution.py:288
  23.0 0.2 copy.37
  23.2 0.2 convert_reduce_fusion
  23.4 1.4 %fusion.25 = f32[512,768]{1,0:T(8,128)S(1)} fusion(f32[512,128]{1,0:T(8,128)S(1)} %convert_reduce_fusion, f32[128,768]{0,1:T(8,128)S(1)} %bitcast.43), kind=kOutput, calls=%fused_computation.50 | convolution fusion | flops 603979776 | bytes 2228224 | tf_op jit(solution)/shard_map/dot_general | solution.py:295
  24.9 2.5 %gather_fusion.2 = s32[288]{0:T(512)S(1)} fusion(s32[224]{0:T(256)S(1)} %bitcast.40, s32[1024]{0:T(1024)S(1)} %pad_clamp_fusion), kind=kCustom, calls=%fused_computation.2 | custom fusion | bytes 3456 | tf_op jit(solution)/shard_map/gather | solution.py:299
  27.3 2.0 %fusion.5.send_ref = f32[288,768]{1,0:T(8,128)} fusion(f32[512,768]{1,0:T(8,128)S(1)} %fusion.25, s32[288]{0:T(512)S(1)} %gather_fusion.2), kind=kOutput, calls=%fused_computation.19 | convolution fusion | flops 1359101952 | bytes 2458752 | tf_op jit(solution)/shard_map/dot_general | solution.py:303
  29.4 13.0 %shard_map.159 = f32[288,768]{1,0:T(8,128)} custom-call(f32[288,768]{1,0:T(8,128)} %fusion.5.send_ref), custom_call_target="tpu_custom_call" | custom-call | tf_op jit(solution)/shard_map/pallas_call | solution.py:231
  42.4 2.5 %gather_fusion.1 = s32[288]{0:T(512)S(1)} fusion(s32[224]{0:T(256)S(1)} %bitcast.41, s32[1024]{0:T(1024)S(1)} %pad_clamp_fusion.1), kind=kCustom, calls=%fused_computation.1 | custom fusion | bytes 3456 | tf_op jit(solution)/shard_map/gather | solution.py:300
  44.9 3.9 %convolution_add_fusion = f32[512,768]{1,0:T(8,128)} fusion(f32[512,768]{1,0:T(8,128)S(1)} %fusion.25, f32[288,768]{1,0:T(8,128)} %shard_map.159, s32[288]{0:T(512)S(1)} %gather_fusion.1), kind=kOutput, calls=%fused_computation.8 | convolution fusion | flops 1359495168 | bytes 4031616 | tf_op jit(solution)/shard_map/dot_general | solution.py:305
  48.9 1.9 %copy.38 = f32[512,768]{0,1:T(8,128)S(1)} copy(f32[512,768]{1,0:T(8,128)} %convolution_add_fusion) | data formatting | bytes 3145728 | tf_op jit(solution)/shard_map/add | solution.py:305
  50.8 1.1 %divide_convert_fusion = bf16[512,6,128]{0,2,1:T(8,128)(2,1)} fusion(f32[512,6,128]{0,2,1:T(8,128)S(1)} %bitcast.42, f32[512]{0:T(512)S(1)} %copy-done.7), kind=kLoop, calls=%fused_computation.7 | loop fusion | flops 786432 | bytes 2361344 | tf_op jit(solution)/shard_map/convert_element_type | solution.py:306
  51.8 2.3 %copy.40 = bf16[512,6,128]{2,0,1:T(8,128)(2,1)} copy(bf16[512,6,128]{0,2,1:T(8,128)(2,1)} %divide_convert_fusion) | data formatting | bytes 1572864
  54.1 0.2 reshape_reshape.3
  54.3 0.8 %copy.39 = bf16[512,3,128]{2,0,1:T(8,128)(2,1)} copy(bf16[512,3,128]{2,1,0:T(4,128)(2,1)S(1)} %reshape_reshape.3) | data formatting | bytes 786432
  (27 shorter events, 0.1 us)
Async XLA Ops:
  0.6 15.2 %copy-start = (bf16[4,384,384]{2,1,0:T(8,128)(2,1)S(1)}, bf16[4,384,384]{2,1,0:T(8,128)(2,1)}, u32[]{:S(2)}) copy-start(bf16[4,384,384]{2,1,0:T(8,128)(2,1)} %param.19) | copy-start | bytes 3538948
  2.1 12.0 %copy-start.9 = (s32[1,24]{1,0:T(1,128)S(1)}, s32[1,24]{1,0:T(1,128)}, u32[]{:S(2)}) copy-start(s32[1,24]{1,0:T(1,128)} %param.16) | copy-start | bytes 292
  2.1 13.2 %copy-start.2 = (bf16[1536,24]{0,1:T(8,128)(2,1)S(1)}, bf16[1536,24]{0,1:T(8,128)(2,1)}, u32[]{:S(2)}) copy-start(bf16[1536,24]{0,1:T(8,128)(2,1)} %param.17) | copy-start | bytes 221188
  2.5 13.3 %copy-start.10 = (s32[1,4]{1,0:T(1,128)S(1)}, s32[1,4]{1,0:T(1,128)}, u32[]{:S(2)}) copy-start(s32[1,4]{1,0:T(1,128)} %param.20) | copy-start | bytes 52
  15.9 0.9 %copy-start.4 = (s32[8,128]{1,0:T(8,128)S(1)}, s32[8,128]{1,0:T(8,128)}, u32[]{:S(2)}) copy-start(s32[8,128]{1,0:T(8,128)} %param.23) | copy-start | bytes 12292
  21.0 0.8 %copy-start.3 = (bf16[6,24,128]{2,1,0:T(8,128)(2,1)S(1)}, bf16[6,24,128]{2,1,0:T(8,128)(2,1)}, u32[]{:S(2)}) copy-start(bf16[6,24,128]{2,1,0:T(8,128)(2,1)} %param.21) | copy-start | bytes 110596
  21.0 1.3 %copy-start.8 = (f32[128]{0:T(128)S(1)}, f32[128]{0:T(128)}, u32[]{:S(2)}) copy-start(f32[128]{0:T(128)} %param.22) | copy-start | bytes 1540
  22.9 1.9 %copy-start.6 = (s32[288]{0:T(512)S(1)}, s32[288]{0:T(512)}, u32[]{:S(2)}) copy-start(s32[288]{0:T(512)} %constant.54) | copy-start | bytes 3460
  23.0 1.9 %copy-start.1 = (s32[1,224]{1,0:T(1,128)S(1)}, s32[1,224]{1,0:T(1,128)}, u32[]{:S(2)}) copy-start(s32[1,224]{1,0:T(1,128)} %param.24) | copy-start | bytes 2692
  27.3 15.1 %copy-start.5 = (s32[288]{0:T(512)S(1)}, s32[288]{0:T(512)}, u32[]{:S(2)}) copy-start(s32[288]{0:T(512)} %constant.53) | copy-start | bytes 3460
  48.8 1.9 %copy-start.7 = (f32[512]{0:T(512)S(1)}, f32[512]{0:T(512)}, u32[]{:S(2)}) copy-start(f32[512]{0:T(512)} %param.25) | copy-start | bytes 6148

commit v2 on v1

--- a/solution.py
+++ b/solution.py
@@ -40,6 +40,16 @@
 RECV_ENTRIES = np.concatenate([np.concatenate(d[3]) for d in DIRECTIONS])
 SLOT_ROWS = [sum(len(x) for x in d[2]) for d in DIRECTIONS]
 SLOT_START = np.concatenate([[0], np.cumsum(SLOT_ROWS)])
+
+
+def _runs(entries):
+    runs = []
+    for i in entries:
+        if runs and runs[-1][1] == i:
+            runs[-1][1] = i + 1
+        else:
+            runs.append([i, i + 1])
+    return runs
 
 
 def iso_matrix():
@@ -183,8 +193,8 @@
     for k, (ds, dg, _, _) in enumerate(DIRECTIONS):
         rows = pl.ds(int(SLOT_START[k]), int(SLOT_ROWS[k]))
         copy = pltpu.make_async_remote_copy(
-            src_ref=send_ref.at[rows],
-            dst_ref=buf.at[rows],
+            src_ref=send_ref.at[:, rows],
+            dst_ref=buf.at[:, rows],
             send_sem=send_sem.at[k],
             recv_sem=recv_sem.at[k],
             device_id=(s + ds, g + dg),
@@ -200,10 +210,12 @@
 
         def take(rows=rows, k=k):
             copies[k].wait_recv()
-            out_ref[rows, :] = buf[rows, :]
+            out_ref[:, rows, :] = buf[:, rows, :]
 
         def clear(rows=rows):
-            out_ref[rows, :] = jnp.zeros((rows.size, out_ref.shape[1]), out_ref.dtype)
+            out_ref[:, rows, :] = jnp.zeros(
+                (out_ref.shape[0], rows.size, out_ref.shape[2]), out_ref.dtype
+            )
 
         pl.when(cond)(take)
         pl.when(jnp.logical_not(cond))(clear)
@@ -282,30 +294,33 @@
         .reshape(node_count, 3 * load_cases)
     )
     elem_count = connect.shape[1]
-    element = displaced[connect.T].reshape(elem_count, 24, load_cases)
+    node_range = jnp.arange(node_count, dtype=jnp.int32)
+    corner_of = (connect.T.reshape(-1)[:, None] == node_range[None, :]).astype(jnp.bfloat16)
+    element = jnp.dot(corner_of, displaced, preferred_element_type=jnp.float32)
+    element = element.astype(jnp.bfloat16).reshape(elem_count, 24, load_cases)
     strain = jnp.einsum("ije,ejl->eil", strain_disp, element, preferred_element_type=jnp.float32)
     stress = (
-        jnp.einsum("ik,ekl->eil", iso_matrix(), strain, precision=lax.Precision.HIGHEST)
-        * modulus[:, None, None]
-    )
-    node_range = jnp.arange(node_count, dtype=jnp.int32)
+        jnp.einsum("ik,ekl->iel", iso_matrix(), strain, precision=lax.Precision.HIGHEST)
+        * modulus[None, :, None]
+    )
     incidence = jnp.sum(
         (connect[:, None, :] == node_range[None, :, None]).astype(jnp.float32), axis=0
     )
-    partial_value = jnp.dot(
-        incidence, stress.reshape(elem_count, 6 * load_cases), precision=lax.Precision.HIGHEST
+    partial_value = jnp.einsum(
+        "ne,cel->cnl", incidence, stress, precision=lax.Precision.HIGHEST
     )
     node_ids = interface[0]
-    send_ids = node_ids[SEND_ENTRIES]
-    recv_ids = node_ids[RECV_ENTRIES]
+    send_ids = jnp.concatenate([node_ids[int(a):int(b)] for a, b in _runs(SEND_ENTRIES)])
+    recv_ids = jnp.concatenate([node_ids[int(a):int(b)] for a, b in _runs(RECV_ENTRIES)])
     send_pick = (send_ids[:, None] == node_range[None, :]).astype(jnp.float32)
     recv_pick = (recv_ids[:, None] == node_range[None, :]).astype(jnp.float32)
-    send = jnp.dot(send_pick, partial_value, precision=lax.Precision.HIGHEST)
+    send_count = jnp.dot(send_pick, incidence)
+    send = jnp.einsum("re,cel->crl", send_count, stress, precision=lax.Precision.HIGHEST)
     received = exchange_faces(send, n_sub, n_grp)
-    summed = partial_value + jnp.dot(recv_pick.T, received, precision=lax.Precision.HIGHEST)
-    stress_out = (summed.reshape(node_count, 6, load_cases) / nodal_volume[:, None, None]).astype(
-        jnp.bfloat16
-    )
+    summed = partial_value + jnp.einsum(
+        "rn,crl->cnl", recv_pick, received, precision=lax.Precision.HIGHEST
+    )
+    stress_out = (summed / nodal_volume[None, :, None]).astype(jnp.bfloat16).transpose(1, 0, 2)
     return (displaced.reshape(node_count, 3, load_cases), stress_out)
 
 

time: 55.5 us -> 51.7 us (0.932)
  local copies, waits for them, and re-layouts: 17.8 us -> 10.6 us
  other arithmetic: 1.43 us -> 3.59 us
  matrix products: 10.5 us -> 11.9 us
    gather x3 -> x0, local copies, waits for them, and re-layouts: 8.83 us -> none  [the longest x1 3.92 us: shards(): element = displaced[connect.T].reshape(elem_count, 24, load_cases)]
    slice x0 -> x4, local copies, waits for them, and re-layouts: none -> 3.32 us  [shards(): node_ids[int(a):int(b)]]
    add x1 -> x0, local copies, waits for them, and re-layouts: 1.89 us -> none  [shards(): partial_value + jnp.dot(recv_pick.T, received, precision=lax.Precision.HI...]
    dot_general x4 -> x6, matrix products: 8.02 us -> 9.38 us  [the longest x1 2.52 us: shards(): jnp.einsum('rn,crl->cnl', recv_pick, received, precision=lax.Precision.HI...]
    unnamed x25 -> x24, local copies, waits for them, and re-layouts: 3.72 us -> 2.4 us
    convert_element_type x3, local copies, waits for them, and re-layouts: 2.05 us -> 0.96 us  [shards(): force.reshape(3 * node_count, load_cases).astype(jnp.float32) - correction]
    convert_element_type x1 -> x0, other arithmetic: 1.08 us -> none  [shards(): (summed.reshape(node_count, 6, load_cases) / nodal_volume[:, None, None])...]
    transpose x0 -> x1, local copies, waits for them, and re-layouts: none -> 0.79 us  [shards(): connect.T.reshape(-1)[:, None] == node_range[None, :]]
where the time goes in v2:
time: 51.7 us; the launch traced here: 51.2 us
  Pallas kernels  24.3 us (47%)
  matrix products  11.9 us (23%)
  local copies, waits for them, and re-layouts  10.6 us (21%)
  other arithmetic  3.59 us (7%)
  between operations  0.89 us (2%)
    pallas_call x1, Pallas kernels, exchange_faces(): pl.pallas_call(functools.partial(face_kernel, n_sub, n_grp), out_shape=ja...  13.1 us
    pallas_call x1, Pallas kernels, fetch_coarse(): pl.pallas_call(functools.partial(coarse_kernel, n_sub, n_grp), out_shape=...  11.2 us
    slice x4, local copies, waits for them, and re-layouts, shards(): node_ids[int(a):int(b)]  3.32 us
    dot_general x1, matrix products, shards(): jnp.einsum('rn,crl->cnl', recv_pick, received, precision=lax.Precision.HI...  2.52 us
    unnamed x24, local copies, waits for them, and re-layouts  2.4 us
    dot_general x1, matrix products, shards(): jnp.einsum('re,cel->crl', send_count, stress, precision=lax.Precision.HIG...  1.99 us
    dot_general x1, matrix products, shards(): element = jnp.dot(corner_of, displaced, preferred_element_type=jnp.float32)  1.75 us
    dot_general x1, matrix products, shards(): jnp.einsum('ne,cel->cnl', incidence, stress, precision=lax.Precision.HIGH...  1.54 us

profile of v2, /device:TPU:121, one launch (start us, length us, event | category | flops | bytes accessed | tf_op | source)
XLA Modules:
  0.0 51.2 jit_solution(4309708675906816667)
XLA Ops:
  0.7 0.8 %subtract_bitcast_fusion = s32[24]{0:T(128)S(1)} fusion(s32[1,24]{1,0:T(1,128)} %param.12, s32[]{:T(128)S(6)} %mul.30), kind=kLoop, calls=%fused_computation.57 | loop fusion | flops 24 | bytes 196 | tf_op jit(solution)/shard_map/sub | solution.py:275
  1.4 0.7 %multiply_bitcast_fusion = s32[4]{0:T(128)S(1)} fusion(s32[1,4]{1,0:T(1,128)} %param.16), kind=kLoop, calls=%fused_computation.58 | loop fusion | flops 4 | bytes 32 | tf_op jit(solution)/shard_map/mul | solution.py:285
  2.1 0.6 %iota_compare_fusion.10 = pred[4,384]{1,0:T(4,128)(4,1)} fusion(s32[4]{0:T(128)S(1)} %multiply_bitcast_fusion), kind=kLoop, calls=%fused_computation.32 | loop fusion | flops 1536 | bytes 1552 | tf_op jit(solution)/shard_map/lt | solution.py:285
  2.7 0.8 %slice_bitcast_fusion.9 = (s32[16]{0:T(128)S(1)}, s32[16]{0:T(128)S(1)}) fusion(s32[1,224]{1,0:T(1,128)} %param.20), kind=kLoop, calls=%fused_computation.55 | loop fusion | bytes 256 | tf_op jit(solution)/shard_map/slice | solution.py:313
  3.5 0.8 %slice_bitcast_fusion.10 = (s32[64]{0:T(128)S(1)}, s32[64]{0:T(128)S(1)}) fusion(s32[1,224]{1,0:T(1,128)} %param.20), kind=kLoop, calls=%fused_computation.56 | loop fusion | bytes 1024 | tf_op jit(solution)/shard_map/slice | solution.py:313
  4.3 0.8 %slice_bitcast_fusion = (s32[32]{0:T(128)S(1)}, s32[32]{0:T(128)S(1)}, s32[32]{0:T(128)S(1)}) fusion(s32[1,224]{1,0:T(1,128)} %param.20), kind=kLoop, calls=%fused_computation.46 | loop fusion | bytes 768 | tf_op jit(solution)/shard_map/slice | solution.py:314
  5.2 0.9 %slice_bitcast_fusion.4 = (s32[8]{0:T(128)S(1)}, s32[8]{0:T(128)S(1)}, s32[8]{0:T(128)S(1)}, s32[8]{0:T(128)S(1)}) fusion(s32[1,224]{1,0:T(1,128)} %param.20), kind=kLoop, calls=%fused_computation.50 | loop fusion | bytes 256 | tf_op jit(solution)/shard_map/slice | solution.py:313
  6.0 0.7 %concatenate.18 = s32[288]{0:T(512)} concatenate(s32[64]{0:T(128)S(1)} %get-tuple-element.17, s32[16]{0:T(128)S(1)} %get-tuple-element.15, s32[64]{0:T(128)S(1)} %get-tuple-element.18, s32[16]{0:T(128)S(1)} %get-tuple-element.16, s32[32]{0:T(128)S(1)} %get-tuple-element.10, s32[8]{0:T(128)S(1)} %get-tuple-element.13, s32[8]{0:T(128)S(1)} %get-tuple-element.11, ...), dimensions={0} | concatenate | bytes 2304 | tf_op jit(solution)/shard_map/concatenate | solution.py:314
  6.8 0.6 %select_add_fusion = (f32[3,3]{1,0:T(4,128)S(1)}, f32[3,3]{1,0:T(4,128)}) fusion(), kind=kLoop, calls=%fused_computation.43 | loop fusion | flops 36 | bytes 72 | tf_op jit(solution)/shard_map/add;broadcast_in_dim | solution.py:58
  7.4 0.8 %copy.38 = s32[128,8]{1,0:T(8,128)S(1)} copy(s32[128,8]{0,1:T(8,128)} %bitcast.68) | data formatting | bytes 8192 | tf_op jit(solution)/shard_map/transpose | solution.py:298
  8.2 0.7 %eq.80 = s32[1024]{0:T(1024)} reshape(s32[128,8]{1,0:T(8,128)S(1)} %copy.38) | data formatting | bytes 8192 | tf_op jit(solution)/shard_map/eq | solution.py:298
  8.9 11.2 %shard_map.122 = f32[12,24,128]{2,1,0:T(8,128)} custom-call(f32[24,128]{1,0:T(8,128)} %block_ref.1), custom_call_target="tpu_custom_call" | custom-call | tf_op jit(solution)/shard_map/pallas_call | solution.py:227
  20.1 1.1 %fusion.18 = f32[24,128]{1,0:T(8,128)S(1)} fusion(f32[288,128]{1,0:T(8,128)} %bitcast.66, s32[24]{0:T(128)S(1)} %subtract_bitcast_fusion), kind=kOutput, calls=%fused_computation.30 | convolution fusion | flops 10623744 | bytes 159840 | tf_op jit(solution)/shard_map/dot_general | solution.py:279
  21.2 0.9 %convert_reduce_fusion = f32[512,128]{1,0:T(8,128)S(1)} fusion(s32[8,128]{1,0:T(8,128)} %param.19), kind=kLoop, calls=%fused_computation.3 | loop fusion | flops 1507328 | bytes 266240 | tf_op jit(solution)/shard_map/reduce_sum | solution.py:306
  22.1 1.0 %convolution_bitcast_fusion.3 = f32[288,128,1]{1,0,2:T(8,128)} fusion(f32[512,128]{1,0:T(8,128)S(1)} %convert_reduce_fusion, s32[288]{0:T(512)S(1)} %concatenate.19), kind=kOutput, calls=%fused_computation.13 | convolution fusion | flops 37896192 | bytes 410752 | tf_op jit(solution)/shard_map/dot_general | solution.py:317
  23.1 0.9 %copy.40 = bf16[6,24,128]{1,0,2:T(8,128)(2,1)S(1)} copy(bf16[6,24,128]{2,1,0:T(8,128)(2,1)} %param.17) | data formatting | bytes 73728 | tf_op args[6]
  24.0 0.3 copy.34
  24.4 0.4 reshape.76
  24.8 0.3 copy.35
  25.1 0.6 %copy-done.4 = bf16[1536,24]{0,1:T(8,128)(2,1)S(1)} copy-done((bf16[1536,24]{0,1:T(8,128)(2,1)S(1)}, bf16[1536,24]{0,1:T(8,128)(2,1)}, u32[]{:S(2)}) %copy-start.4) | copy-done | bytes 73752
  25.6 0.5 %fusion = bf16[1536,128]{0,1:T(8,128)(2,1)S(1)} fusion(f32[1536,128]{0,1:T(8,128)S(1)} %copy.35, f32[24,128]{1,0:T(8,128)S(1)} %fusion.18, bf16[1536,24]{0,1:T(8,128)(2,1)S(1)} %copy-done.4), kind=kOutput, calls=%fused_computation.1 | convolution fusion | flops 57016320 | bytes 1265664 | tf_op jit(solution)/shard_map/dot_general | solution.py:284
  26.2 0.5 fusion.4
  26.9 0.9 %reshape.74 = bf16[512,384]{1,0:T(8,128)(2,1)} reshape(bf16[4,384,128]{2,1,0:T(8,128)(2,1)S(1)} %copy.37) | data formatting | bytes 786432 | tf_op jit(solution)/shard_map/reshape | solution.py:294
  28.1 0.8 %copy.42 = bf16[512,3,128]{2,0,1:T(8,128)(2,1)} copy(bf16[512,3,128]{2,1,0:T(4,128)(2,1)S(1)} %reshape_reshape.3) | data formatting | bytes 786432
  28.9 1.8 %fusion.2 = bf16[1024,384]{1,0:T(8,128)(2,1)S(1)} fusion(bf16[512,384]{1,0:T(8,128)(2,1)} %reshape.74, s32[1024]{0:T(1024)S(1)} %copy-done.6), kind=kOutput, calls=%fused_computation.7 | convolution fusion | flops 403570688 | bytes 1183744 | tf_op jit(solution)/shard_map/dot_general | solution.py:299
  30.6 0.4 reshape.75
  31.0 0.4 convolution_bitcast_fusion.2
  31.4 0.6 %fusion.21 = f32[6,128,128]{2,0,1:T(8,128)S(1)} fusion(f32[128,6,128]{2,1,0:T(8,128)S(1)} %convolution_bitcast_fusion.2, f32[3,3]{1,0:T(4,128)S(1)} %copy-done.5, f32[3,3]{1,0:T(4,128)S(1)} %get-tuple-element.19), kind=kOutput, calls=%fused_computation.35 | convolution fusion | flops 7078068 | bytes 786504 | tf_op jit(solution)/shard_map/ik,ekl->iel/dot_general | solution.py:303
  32.0 2.0 %convolution_bitcast_fusion.1.send_ref = f32[6,288,128]{2,1,0:T(8,128)} fusion(f32[288,128,1]{1,0,2:T(8,128)S(1)} %copy-done.2, f32[6,128,128]{2,0,1:T(8,128)S(1)} %fusion.21, f32[128]{0:T(128)S(1)} %copy-done.7), kind=kOutput, calls=%fused_computation.8 | convolution fusion | flops 339836928 | bytes 1425920 | tf_op jit(solution)/shard_map/re,cel->crl/dot_general | solution.py:318
  34.0 13.1 %shard_map.123 = f32[6,288,128]{2,1,0:T(8,128)} custom-call(f32[6,288,128]{2,1,0:T(8,128)} %convolution_bitcast_fusion.1.send_ref), custom_call_target="tpu_custom_call" | custom-call | tf_op jit(solution)/shard_map/pallas_call | solution.py:243
  47.1 1.5 %fusion.14 = f32[512,6,128]{2,0,1:T(8,128)S(1)} fusion(f32[6,128,128]{2,0,1:T(8,128)S(1)} %fusion.21, f32[512,128]{1,0:T(8,128)S(1)} %convert_reduce_fusion, f32[128]{0:T(128)S(1)} %copy-done.7), kind=kOutput, calls=%fused_computation.25 | convolution fusion | flops 604078080 | bytes 2228736 | tf_op jit(solution)/shard_map/ne,cel->cnl/dot_general | solution.py:309
  48.7 2.5 %divide_convert_fusion = bf16[512,6,128]{2,0,1:T(8,128)(2,1)} fusion(f32[512,6,128]{2,0,1:T(8,128)S(1)} %fusion.14, f32[6,288,128]{2,1,0:T(8,128)S(1)} %copy-done.1, f32[512]{0:T(512)S(1)} %copy-done.10, s32[288]{0:T(512)S(1)} %copy-done.8), kind=kOutput, calls=%fused_computation.6 | convolution fusion | flops 1360281600 | bytes 3247232 | tf_op jit(solution)/shard_map/rn,crl->cnl/dot_general | solution.py:320
  (24 shorter events, 0.5 us)
Async XLA Ops:
  0.6 25.5 %copy-start = (bf16[4,384,384]{2,1,0:T(8,128)(2,1)S(1)}, bf16[4,384,384]{2,1,0:T(8,128)(2,1)}, u32[]{:S(2)}) copy-start(bf16[4,384,384]{2,1,0:T(8,128)(2,1)} %param.15) | copy-start | bytes 3538948
  0.6 23.4 %copy-start.3 = (bf16[512,3,128]{2,0,1:T(8,128)(2,1)S(1)}, bf16[512,3,128]{2,0,1:T(8,128)(2,1)}, u32[]{:S(2)}) copy-start(bf16[512,3,128]{2,0,1:T(8,128)(2,1)} %param.14) | copy-start | bytes 1179652
  24.8 0.9 %copy-start.4 = (bf16[1536,24]{0,1:T(8,128)(2,1)S(1)}, bf16[1536,24]{0,1:T(8,128)(2,1)}, u32[]{:S(2)}) copy-start(bf16[1536,24]{0,1:T(8,128)(2,1)} %param.13) | copy-start | bytes 221188
  24.8 1.4 %copy-start.9 = (pred[4,384]{1,0:T(4,128)(4,1)S(1)}, pred[4,384]{1,0:T(4,128)(4,1)}, u32[]{:S(2)}) copy-start(pred[4,384]{1,0:T(4,128)(4,1)} %iota_compare_fusion.10) | copy-start | bytes 4612
  26.7 2.2 %copy-start.6 = (s32[1024]{0:T(1024)S(1)}, s32[1024]{0:T(1024)}, u32[]{:S(2)}) copy-start(s32[1024]{0:T(1024)} %eq.80) | copy-start | bytes 12292
  30.6 0.8 %copy-start.5 = (f32[3,3]{1,0:T(4,128)S(1)}, f32[3,3]{1,0:T(4,128)}, u32[]{:S(2)}) copy-start(f32[3,3]{1,0:T(4,128)} %get-tuple-element.20) | copy-start | bytes 112
  31.0 1.0 %copy-start.2 = (f32[288,128,1]{1,0,2:T(8,128)S(1)}, f32[288,128,1]{1,0,2:T(8,128)}, u32[]{:S(2)}) copy-start(f32[288,128,1]{1,0,2:T(8,128)} %convolution_bitcast_fusion.3) | copy-start | bytes 442372
  31.0 1.0 %copy-start.7 = (f32[128]{0:T(128)S(1)}, f32[128]{0:T(128)}, u32[]{:S(2)}) copy-start(f32[128]{0:T(128)} %param.18) | copy-start | bytes 1540
  34.0 14.6 %copy-start.8 = (s32[288]{0:T(512)S(1)}, s32[288]{0:T(512)}, u32[]{:S(2)}) copy-start(s32[288]{0:T(512)} %concatenate.18) | copy-start | bytes 3460
  34.0 14.6 %copy-start.10 = (f32[512]{0:T(512)S(1)}, f32[512]{0:T(512)}, u32[]{:S(2)}) copy-start(f32[512]{0:T(512)} %param.21) | copy-start | bytes 6148
  47.1 1.6 %copy-start.1 = (f32[6,288,128]{2,1,0:T(8,128)S(1)}, f32[6,288,128]{2,1,0:T(8,128)}, u32[]{:S(2)}) copy-start(f32[6,288,128]{2,1,0:T(8,128)} %shard_map.123) | copy-start | bytes 2654212

commit v3 on v2

--- a/solution.py
+++ b/solution.py
@@ -36,8 +36,6 @@
     (-1, 1, (EDGE_LH,), (EDGE_HL,)),
     (-1, -1, (EDGE_LL,), (EDGE_HH,)),
 )
-SEND_ENTRIES = np.concatenate([np.concatenate(d[2]) for d in DIRECTIONS])
-RECV_ENTRIES = np.concatenate([np.concatenate(d[3]) for d in DIRECTIONS])
 SLOT_ROWS = [sum(len(x) for x in d[2]) for d in DIRECTIONS]
 SLOT_START = np.concatenate([[0], np.cumsum(SLOT_ROWS)])
 
@@ -49,7 +47,20 @@
             runs[-1][1] = i + 1
         else:
             runs.append([i, i + 1])
-    return runs
+    return [(int(a), int(b)) for a, b in runs]
+
+
+def _pieces(k, which):
+    out = []
+    row = int(SLOT_START[k])
+    for a, b in _runs(np.concatenate(DIRECTIONS[k][which])):
+        out.append((a, b, row))
+        row += b - a
+    return out
+
+
+SEND_PIECES = [(k, a, b, row) for k in range(len(DIRECTIONS)) for a, b, row in _pieces(k, 2)]
+RECV_PIECES = [_pieces(k, 3) for k in range(len(DIRECTIONS))]
 
 
 def iso_matrix():
@@ -190,35 +201,32 @@
     pl.semaphore_wait(barrier, count)
 
     copies = []
-    for k, (ds, dg, _, _) in enumerate(DIRECTIONS):
-        rows = pl.ds(int(SLOT_START[k]), int(SLOT_ROWS[k]))
+    for j, (k, lo, hi, row) in enumerate(SEND_PIECES):
+        ds, dg = DIRECTIONS[k][:2]
         copy = pltpu.make_async_remote_copy(
-            src_ref=send_ref.at[:, rows],
-            dst_ref=buf.at[:, rows],
-            send_sem=send_sem.at[k],
-            recv_sem=recv_sem.at[k],
+            src_ref=send_ref.at[:, pl.ds(lo, hi - lo)],
+            dst_ref=buf.at[:, pl.ds(row, hi - lo)],
+            send_sem=send_sem.at[j],
+            recv_sem=recv_sem.at[j],
             device_id=(s + ds, g + dg),
             device_id_type=MESH,
         )
         pl.when(exists(ds, dg))(copy.start)
         copies.append(copy)
+    out_ref[...] = jnp.zeros(out_ref.shape, out_ref.dtype)
+    for j, (k, lo, hi, row) in enumerate(SEND_PIECES):
+        ds, dg = DIRECTIONS[k][:2]
+        pl.when(exists(ds, dg))(copies[j].wait_send)
     for k, (ds, dg, _, _) in enumerate(DIRECTIONS):
-        pl.when(exists(ds, dg))(copies[k].wait_send)
-    for k, (ds, dg, _, _) in enumerate(DIRECTIONS):
-        rows = pl.ds(int(SLOT_START[k]), int(SLOT_ROWS[k]))
-        cond = exists(-ds, -dg)
-
-        def take(rows=rows, k=k):
-            copies[k].wait_recv()
-            out_ref[:, rows, :] = buf[:, rows, :]
-
-        def clear(rows=rows):
-            out_ref[:, rows, :] = jnp.zeros(
-                (out_ref.shape[0], rows.size, out_ref.shape[2]), out_ref.dtype
-            )
-
-        pl.when(cond)(take)
-        pl.when(jnp.logical_not(cond))(clear)
+        mine = [j for j, piece in enumerate(SEND_PIECES) if piece[0] == k]
+
+        def take(k=k, mine=mine):
+            for j in mine:
+                copies[j].wait_recv()
+            for lo, hi, row in RECV_PIECES[k]:
+                out_ref[:, lo:hi, :] += buf[:, row:row + hi - lo, :]
+
+        pl.when(exists(-ds, -dg))(take)
 
 
 def fetch_coarse(block, n_sub, n_grp):
@@ -246,9 +254,9 @@
         in_specs=[pl.BlockSpec(memory_space=pltpu.VMEM)],
         out_specs=pl.BlockSpec(memory_space=pltpu.VMEM),
         scratch_shapes=[
-            pltpu.VMEM(send.shape, send.dtype),
-            pltpu.SemaphoreType.DMA((len(DIRECTIONS),)),
-            pltpu.SemaphoreType.DMA((len(DIRECTIONS),)),
+            pltpu.VMEM((send.shape[0], int(SLOT_START[-1]), send.shape[2]), send.dtype),
+            pltpu.SemaphoreType.DMA((len(SEND_PIECES),)),
+            pltpu.SemaphoreType.DMA((len(SEND_PIECES),)),
         ],
         compiler_params=pltpu.CompilerParams(collective_id=1, has_side_effects=True),
     )(send)
@@ -309,16 +317,12 @@
     partial_value = jnp.einsum(
         "ne,cel->cnl", incidence, stress, precision=lax.Precision.HIGHEST
     )
-    node_ids = interface[0]
-    send_ids = jnp.concatenate([node_ids[int(a):int(b)] for a, b in _runs(SEND_ENTRIES)])
-    recv_ids = jnp.concatenate([node_ids[int(a):int(b)] for a, b in _runs(RECV_ENTRIES)])
-    send_pick = (send_ids[:, None] == node_range[None, :]).astype(jnp.float32)
-    recv_pick = (recv_ids[:, None] == node_range[None, :]).astype(jnp.float32)
-    send_count = jnp.dot(send_pick, incidence)
-    send = jnp.einsum("re,cel->crl", send_count, stress, precision=lax.Precision.HIGHEST)
-    received = exchange_faces(send, n_sub, n_grp)
+    picker = (interface[0][:, None] == node_range[None, :]).astype(jnp.float32)
+    iface_count = jnp.dot(picker, incidence)
+    send = jnp.einsum("re,cel->crl", iface_count, stress, precision=lax.Precision.HIGHEST)
+    added = exchange_faces(send, n_sub, n_grp)
     summed = partial_value + jnp.einsum(
-        "rn,crl->cnl", recv_pick, received, precision=lax.Precision.HIGHEST
+        "rn,crl->cnl", picker, added, precision=lax.Precision.HIGHEST
     )
     stress_out = (summed / nodal_volume[None, :, None]).astype(jnp.bfloat16).transpose(1, 0, 2)
     return (displaced.reshape(node_count, 3, load_cases), stress_out)

time: 51.7 us -> 47.4 us (0.917)
  local copies, waits for them, and re-layouts: 10.6 us -> 6.53 us
    slice x4 -> x0, local copies, waits for them, and re-layouts: 3.32 us -> none  [shards(): node_ids[int(a):int(b)]]
    concatenate x2 -> x0, local copies, waits for them, and re-layouts: 0.75 us -> none  [the longest x1 0.66 us: shards(): jnp.concatenate([node_ids[int(a):int(b)] for a, b in _runs(RECV_ENTRIES)])]
where the time goes in v3:
time: 47.4 us; the launch traced here: 46.9 us
  Pallas kernels  24.2 us (51%)
  matrix products  11.6 us (24%)
  local copies, waits for them, and re-layouts  6.53 us (14%)
  other arithmetic  3.6 us (8%)
  between operations  0.89 us (2%)
    pallas_call x1, Pallas kernels, exchange_faces(): pl.pallas_call(functools.partial(face_kernel, n_sub, n_grp), out_shape=ja...  13.1 us
    pallas_call x1, Pallas kernels, fetch_coarse(): pl.pallas_call(functools.partial(coarse_kernel, n_sub, n_grp), out_shape=...  11.2 us
    unnamed x24, local copies, waits for them, and re-layouts  2.4 us
    dot_general x1, matrix products, shards(): jnp.einsum('rn,crl->cnl', picker, added, precision=lax.Precision.HIGHEST)  1.94 us
    dot_general x1, matrix products, shards(): element = jnp.dot(corner_of, displaced, preferred_element_type=jnp.float32)  1.74 us
    dot_general x1, matrix products, shards(): jnp.einsum('re,cel->crl', iface_count, stress, precision=lax.Precision.HI...  1.72 us
    dot_general x1, matrix products, shards(): iface_count = jnp.dot(picker, incidence)  1.59 us
    dot_general x1, matrix products, shards(): jnp.einsum('ne,cel->cnl', incidence, stress, precision=lax.Precision.HIGH...  1.52 us

profile of v3, /device:TPU:121, one launch (start us, length us, event | category | flops | bytes accessed | tf_op | source)
XLA Modules:
  0.0 46.9 jit_solution(5806479196994160205)
XLA Ops:
  0.6 0.0 copy-start
  0.7 0.8 %subtract_bitcast_fusion = s32[24]{0:T(128)S(1)} fusion(s32[1,24]{1,0:T(1,128)} %param.12, s32[]{:T(128)S(6)} %mul.30), kind=kLoop, calls=%fused_computation.45 | loop fusion | flops 24 | bytes 196 | tf_op jit(solution)/shard_map/sub | solution.py:283
  1.4 0.7 %multiply_bitcast_fusion = s32[4]{0:T(128)S(1)} fusion(s32[1,4]{1,0:T(1,128)} %param.16), kind=kLoop, calls=%fused_computation.46 | loop fusion | flops 4 | bytes 32 | tf_op jit(solution)/shard_map/mul | solution.py:293
  2.1 0.6 %iota_compare_fusion.9 = pred[4,384]{1,0:T(4,128)(4,1)} fusion(s32[4]{0:T(128)S(1)} %multiply_bitcast_fusion), kind=kLoop, calls=%fused_computation.31 | loop fusion | flops 1536 | bytes 1552 | tf_op jit(solution)/shard_map/lt | solution.py:293
  2.7 0.6 %select_add_fusion = (f32[3,3]{1,0:T(4,128)S(1)}, f32[3,3]{1,0:T(4,128)}) fusion(), kind=kLoop, calls=%fused_computation.42 | loop fusion | flops 36 | bytes 72 | tf_op jit(solution)/shard_map/add;broadcast_in_dim | solution.py:69
  3.3 0.8 %copy.38 = s32[128,8]{1,0:T(8,128)S(1)} copy(s32[128,8]{0,1:T(8,128)} %bitcast.47) | data formatting | bytes 8192 | tf_op jit(solution)/shard_map/transpose | solution.py:306
  4.1 0.7 %eq.69 = s32[1024]{0:T(1024)} reshape(s32[128,8]{1,0:T(8,128)S(1)} %copy.38) | data formatting | bytes 8192 | tf_op jit(solution)/shard_map/eq | solution.py:306
  4.8 11.2 %shard_map.122 = f32[12,24,128]{2,1,0:T(8,128)} custom-call(f32[24,128]{1,0:T(8,128)} %block_ref.1), custom_call_target="tpu_custom_call" | custom-call | tf_op jit(solution)/shard_map/pallas_call | solution.py:235
  16.0 1.1 %fusion.18 = f32[24,128]{1,0:T(8,128)S(1)} fusion(f32[288,128]{1,0:T(8,128)} %bitcast.45, s32[24]{0:T(128)S(1)} %subtract_bitcast_fusion), kind=kOutput, calls=%fused_computation.29 | convolution fusion | flops 10623744 | bytes 159840 | tf_op jit(solution)/shard_map/dot_general | solution.py:287
  17.1 0.9 %convert_reduce_fusion = f32[512,128]{1,0:T(8,128)S(1)} fusion(s32[8,128]{1,0:T(8,128)} %param.19), kind=kLoop, calls=%fused_computation.3 | loop fusion | flops 1507328 | bytes 266240 | tf_op jit(solution)/shard_map/reduce_sum | solution.py:314
  18.1 1.6 %convolution_bitcast_fusion.3 = f32[224,128,1]{1,0,2:T(8,128)} fusion(f32[512,128]{1,0:T(8,128)S(1)} %convert_reduce_fusion, s32[224]{0:T(256)} %bitcast.48), kind=kOutput, calls=%fused_computation.13 | convolution fusion | flops 29474816 | bytes 377728 | tf_op jit(solution)/shard_map/dot_general | solution.py:321
  19.6 0.9 %copy.40 = bf16[6,24,128]{1,0,2:T(8,128)(2,1)S(1)} copy(bf16[6,24,128]{2,1,0:T(8,128)(2,1)} %param.17) | data formatting | bytes 73728 | tf_op args[6]
  20.6 0.3 copy.34
  21.0 0.4 reshape.64
  21.3 0.0 copy-start.4
  21.4 0.3 copy.35
  21.6 0.6 %copy-done.4 = bf16[1536,24]{0,1:T(8,128)(2,1)S(1)} copy-done((bf16[1536,24]{0,1:T(8,128)(2,1)S(1)}, bf16[1536,24]{0,1:T(8,128)(2,1)}, u32[]{:S(2)}) %copy-start.4) | copy-done | bytes 73752
  22.2 0.5 %fusion = bf16[1536,128]{0,1:T(8,128)(2,1)S(1)} fusion(f32[1536,128]{0,1:T(8,128)S(1)} %copy.35, f32[24,128]{1,0:T(8,128)S(1)} %fusion.18, bf16[1536,24]{0,1:T(8,128)(2,1)S(1)} %copy-done.4), kind=kOutput, calls=%fused_computation.1 | convolution fusion | flops 57016320 | bytes 1265664 | tf_op jit(solution)/shard_map/dot_general | solution.py:292
  22.8 0.5 %fusion.4 = bf16[4,384,128]{1,2,0:T(8,128)(2,1)S(1)} fusion(bf16[4,384,384]{2,1,0:T(8,128)(2,1)S(1)} %copy-done, bf16[16,4,8,384]{3,2,1,0:T(8,128)(2,1)S(1)} %bitcast.46, pred[4,384]{1,0:T(4,128)(4,1)S(1)} %copy-done.8), kind=kOutput, calls=%fused_computation.12 | convolution fusion | flops 151584768 | bytes 1967616 | tf_op jit(solution)/shard_map/prc,pcl->prl/dot_general | solution.py:298
  23.3 0.2 copy.37
  23.5 0.9 %reshape.62 = bf16[512,384]{1,0:T(8,128)(2,1)} reshape(bf16[4,384,128]{2,1,0:T(8,128)(2,1)S(1)} %copy.37) | data formatting | bytes 786432 | tf_op jit(solution)/shard_map/reshape | solution.py:302
  24.4 0.2 reshape_reshape.3
  24.6 0.8 %copy.42 = bf16[512,3,128]{2,0,1:T(8,128)(2,1)} copy(bf16[512,3,128]{2,1,0:T(4,128)(2,1)S(1)} %reshape_reshape.3) | data formatting | bytes 786432
  25.4 1.7 %fusion.2 = bf16[1024,384]{1,0:T(8,128)(2,1)S(1)} fusion(bf16[512,384]{1,0:T(8,128)(2,1)} %reshape.62, s32[1024]{0:T(1024)S(1)} %copy-done.6), kind=kOutput, calls=%fused_computation.7 | convolution fusion | flops 403570688 | bytes 1183744 | tf_op jit(solution)/shard_map/dot_general | solution.py:307
  27.2 0.4 reshape.63
  27.6 0.0 copy-start.7
  27.6 0.4 convolution_bitcast_fusion.2
  27.9 0.6 %fusion.21 = f32[6,128,128]{2,0,1:T(8,128)S(1)} fusion(f32[128,6,128]{2,1,0:T(8,128)S(1)} %convolution_bitcast_fusion.2, f32[3,3]{1,0:T(4,128)S(1)} %copy-done.5, f32[3,3]{1,0:T(4,128)S(1)} %get-tuple-element.8), kind=kOutput, calls=%fused_computation.34 | convolution fusion | flops 7078068 | bytes 786504 | tf_op jit(solution)/shard_map/ik,ekl->iel/dot_general | solution.py:311
  28.6 1.7 %convolution_bitcast_fusion.1.send_ref = f32[6,224,128]{2,1,0:T(8,128)} fusion(f32[224,128,1]{1,0,2:T(8,128)S(1)} %copy-done.2, f32[6,128,128]{2,0,1:T(8,128)S(1)} %fusion.21, f32[128]{0:T(128)S(1)} %copy-done.7), kind=kOutput, calls=%fused_computation.9 | convolution fusion | flops 264339456 | bytes 1196544 | tf_op jit(solution)/shard_map/re,cel->crl/dot_general | solution.py:322
  30.3 13.1 %shard_map.123 = f32[6,224,128]{2,1,0:T(8,128)} custom-call(f32[6,224,128]{2,1,0:T(8,128)} %convolution_bitcast_fusion.1.send_ref), custom_call_target="tpu_custom_call" | custom-call | tf_op jit(solution)/shard_map/pallas_call | solution.py:251
  43.4 1.5 %fusion.12 = f32[512,6,128]{2,0,1:T(8,128)S(1)} fusion(f32[6,128,128]{2,0,1:T(8,128)S(1)} %fusion.21, f32[512,128]{1,0:T(8,128)S(1)} %convert_reduce_fusion, f32[128]{0:T(128)S(1)} %copy-done.7), kind=kOutput, calls=%fused_computation.22 | convolution fusion | flops 604078080 | bytes 2228736 | tf_op jit(solution)/shard_map/ne,cel->cnl/dot_general | solution.py:317
  45.0 1.9 %divide_convert_fusion = bf16[512,6,128]{2,0,1:T(8,128)(2,1)} fusion(f32[512,6,128]{2,0,1:T(8,128)S(1)} %fusion.12, f32[6,224,128]{2,1,0:T(8,128)S(1)} %copy-done.1, f32[512]{0:T(512)S(1)} %copy-done.10, s32[224]{0:T(256)S(1)} %bitcast.49), kind=kOutput, calls=%fused_computation.6 | convolution fusion | flops 1058258944 | bytes 3050368 | tf_op jit(solution)/shard_map/rn,crl->cnl/dot_general | solution.py:324
  (18 shorter events, 0.0 us)
Async XLA Ops:
  0.6 22.1 %copy-start = (bf16[4,384,384]{2,1,0:T(8,128)(2,1)S(1)}, bf16[4,384,384]{2,1,0:T(8,128)(2,1)}, u32[]{:S(2)}) copy-start(bf16[4,384,384]{2,1,0:T(8,128)(2,1)} %param.15) | copy-start | bytes 3538948
  0.6 20.0 %copy-start.3 = (bf16[512,3,128]{2,0,1:T(8,128)(2,1)S(1)}, bf16[512,3,128]{2,0,1:T(8,128)(2,1)}, u32[]{:S(2)}) copy-start(bf16[512,3,128]{2,0,1:T(8,128)(2,1)} %param.14) | copy-start | bytes 1179652
  21.3 0.9 %copy-start.4 = (bf16[1536,24]{0,1:T(8,128)(2,1)S(1)}, bf16[1536,24]{0,1:T(8,128)(2,1)}, u32[]{:S(2)}) copy-start(bf16[1536,24]{0,1:T(8,128)(2,1)} %param.13) | copy-start | bytes 221188
  21.3 1.4 %copy-start.8 = (pred[4,384]{1,0:T(4,128)(4,1)S(1)}, pred[4,384]{1,0:T(4,128)(4,1)}, u32[]{:S(2)}) copy-start(pred[4,384]{1,0:T(4,128)(4,1)} %iota_compare_fusion.9) | copy-start | bytes 4612
  23.3 2.2 %copy-start.6 = (s32[1024]{0:T(1024)S(1)}, s32[1024]{0:T(1024)}, u32[]{:S(2)}) copy-start(s32[1024]{0:T(1024)} %eq.69) | copy-start | bytes 12292
  27.2 0.8 %copy-start.5 = (f32[3,3]{1,0:T(4,128)S(1)}, f32[3,3]{1,0:T(4,128)}, u32[]{:S(2)}) copy-start(f32[3,3]{1,0:T(4,128)} %get-tuple-element.9) | copy-start | bytes 112
  27.6 1.0 %copy-start.2 = (f32[224,128,1]{1,0,2:T(8,128)S(1)}, f32[224,128,1]{1,0,2:T(8,128)}, u32[]{:S(2)}) copy-start(f32[224,128,1]{1,0,2:T(8,128)} %convolution_bitcast_fusion.3) | copy-start | bytes 344068
  27.6 1.0 %copy-start.7 = (f32[128]{0:T(128)S(1)}, f32[128]{0:T(128)}, u32[]{:S(2)}) copy-start(f32[128]{0:T(128)} %param.18) | copy-start | bytes 1540
  30.3 14.6 %copy-start.9 = (s32[1,224]{1,0:T(1,128)S(1)}, s32[1,224]{1,0:T(1,128)}, u32[]{:S(2)}) copy-start(s32[1,224]{1,0:T(1,128)} %param.20) | copy-start | bytes 2692
  30.3 14.6 %copy-start.10 = (f32[512]{0:T(512)S(1)}, f32[512]{0:T(512)}, u32[]{:S(2)}) copy-start(f32[512]{0:T(512)} %param.21) | copy-start | bytes 6148
  43.4 1.6 %copy-start.1 = (f32[6,224,128]{2,1,0:T(8,128)S(1)}, f32[6,224,128]{2,1,0:T(8,128)}, u32[]{:S(2)}) copy-start(f32[6,224,128]{2,1,0:T(8,128)} %shard_map.123) | copy-start | bytes 2064388

commit v4 on v3

--- a/solution.py
+++ b/solution.py
@@ -66,18 +66,11 @@
 def iso_matrix():
     lame_first = POISSON / ((1.0 + POISSON) * (1.0 - 2.0 * POISSON))
     shear_mod = 0.5 / (1.0 + POISSON)
-    upper_block = jnp.full((3, 3), lame_first, jnp.float32) + jnp.eye(3, dtype=jnp.float32) * (
-        2.0 * shear_mod
-    )
-    shear_block = jnp.eye(3, dtype=jnp.float32) * shear_mod
-    zero_block = jnp.zeros((3, 3), jnp.float32)
-    return jnp.concatenate(
-        [
-            jnp.concatenate([upper_block, zero_block], 1),
-            jnp.concatenate([zero_block, shear_block], 1),
-        ],
-        0,
-    )
+    elastic = np.zeros((6, 6), np.float32)
+    elastic[:3, :3] = lame_first
+    elastic[:3, :3] += np.eye(3, dtype=np.float32) * np.float32(2.0 * shear_mod)
+    elastic[3:, 3:] = np.eye(3, dtype=np.float32) * np.float32(shear_mod)
+    return elastic
 
 
 def _above(i, n):
@@ -296,15 +289,16 @@
     )
     reduced = jnp.where(live_mask[:, :, None], reduced, 0.0).astype(jnp.bfloat16)
     solved = jnp.einsum("prc,pcl->prl", panel_inv, reduced, preferred_element_type=jnp.float32)
-    displaced = (
-        jnp.where(live_mask[:, :, None], solved, 0.0)
-        .astype(jnp.bfloat16)
-        .reshape(node_count, 3 * load_cases)
+    displaced = jnp.where(live_mask[:, :, None], solved, 0.0).astype(jnp.bfloat16)
+    by_component = (
+        displaced.reshape(panels, panel_rows // 3, 3, load_cases)
+        .transpose(2, 0, 1, 3)
+        .reshape(3, node_count, load_cases)
     )
     elem_count = connect.shape[1]
     node_range = jnp.arange(node_count, dtype=jnp.int32)
     corner_of = (connect.T.reshape(-1)[:, None] == node_range[None, :]).astype(jnp.bfloat16)
-    element = jnp.dot(corner_of, displaced, preferred_element_type=jnp.float32)
+    element = jnp.einsum("xn,cnl->xcl", corner_of, by_component, preferred_element_type=jnp.float32)
     element = element.astype(jnp.bfloat16).reshape(elem_count, 24, load_cases)
     strain = jnp.einsum("ije,ejl->eil", strain_disp, element, preferred_element_type=jnp.float32)
     stress = (
@@ -314,18 +308,16 @@
     incidence = jnp.sum(
         (connect[:, None, :] == node_range[None, :, None]).astype(jnp.float32), axis=0
     )
-    partial_value = jnp.einsum(
-        "ne,cel->cnl", incidence, stress, precision=lax.Precision.HIGHEST
-    )
     picker = (interface[0][:, None] == node_range[None, :]).astype(jnp.float32)
-    iface_count = jnp.dot(picker, incidence)
-    send = jnp.einsum("re,cel->crl", iface_count, stress, precision=lax.Precision.HIGHEST)
-    added = exchange_faces(send, n_sub, n_grp)
+    counts = jnp.concatenate([incidence, jnp.dot(picker, incidence)])
+    both = jnp.einsum("re,cel->crl", counts, stress, precision=lax.Precision.HIGHEST)
+    partial_value = both[:, :node_count]
+    added = exchange_faces(both[:, node_count:], n_sub, n_grp)
     summed = partial_value + jnp.einsum(
         "rn,crl->cnl", picker, added, precision=lax.Precision.HIGHEST
     )
     stress_out = (summed / nodal_volume[None, :, None]).astype(jnp.bfloat16).transpose(1, 0, 2)
-    return (displaced.reshape(node_count, 3, load_cases), stress_out)
+    return (by_component.transpose(1, 0, 2), stress_out)
 
 
 def solution(mesh):

time: 47.4 us -> 45 us (0.949)
  matrix products: 11.6 us -> 9.79 us
  other arithmetic: 3.6 us -> 2.45 us
  local copies, waits for them, and re-layouts: 6.53 us -> 7.03 us
    dot_general x4 -> x3, matrix products: 6.58 us -> 3.66 us  [the longest x1 1.97 us: shards(): jnp.einsum('re,cel->crl', counts, stress, precision=lax.Precision.HIGHEST)]
    dot_general x1, matrix products: 1.94 us -> 3.04 us  [shards(): jnp.einsum('rn,crl->cnl', picker, added, precision=lax.Precision.HIGHEST)]
    reshape x1 -> x0, local copies, waits for them, and re-layouts: 0.93 us -> none  [shards(): displaced = jnp.where(live_mask[:, :, None], solved, 0.0).astype(jnp.bflo...]
    slice x0 -> x1, local copies, waits for them, and re-layouts: none -> 0.89 us  [shards(): added = exchange_faces(both[:, node_count:], n_sub, n_grp)]
    convert_element_type x1 -> x2, local copies, waits for them, and re-layouts: 0.23 us -> 0.92 us  [the longest x1 0.68 us: shards(): element = element.astype(jnp.bfloat16).reshape(elem_count, 24, load_cases)]
    another operation x1 -> x0, other arithmetic: 0.59 us -> none  [iso_matrix(): jnp.full((3, 3), lame_first, jnp.float32)]
    eq x1, local copies, waits for them, and re-layouts: 0.68 us -> 0.09 us  [shards(): connect.T.reshape(-1)[:, None] == node_range[None, :]]
    lt x1, other arithmetic: 0.64 us -> 0.08 us  [shards(): live_mask = jnp.arange(panel_rows)[None, :] < 3 * panel_nodes[0][:, None]]
where the time goes in v4:
time: 45 us; the launch traced here: 44.5 us
  Pallas kernels  24.3 us (54%)
  matrix products  9.79 us (22%)
  local copies, waits for them, and re-layouts  7.03 us (16%)
  other arithmetic  2.45 us (5%)
  between operations  0.9 us (2%)
    pallas_call x1, Pallas kernels, exchange_faces(): pl.pallas_call(functools.partial(face_kernel, n_sub, n_grp), out_shape=ja...  13 us
    pallas_call x1, Pallas kernels, fetch_coarse(): pl.pallas_call(functools.partial(coarse_kernel, n_sub, n_grp), out_shape=...  11.3 us
    dot_general x1, matrix products, shards(): jnp.einsum('rn,crl->cnl', picker, added, precision=lax.Precision.HIGHEST)  3.04 us
    unnamed x21, local copies, waits for them, and re-layouts  2.68 us
    dot_general x1, matrix products, shards(): jnp.einsum('re,cel->crl', counts, stress, precision=lax.Precision.HIGHEST)  1.97 us
    dot_general x1, matrix products, shards(): corner_vals = jnp.dot(selector, nearby, precision=lax.Precision.HIGHEST)  1.13 us
    convert_element_type x3, local copies, waits for them, and re-layouts, shards(): force.reshape(3 * node_count, load_cases).astype(jnp.float32) - correction  0.96 us
    reduce_sum x1, other arithmetic, shards(): jnp.sum((connect[:, None, :] == node_range[None, :, None]).astype(jnp.flo...  0.94 us

profile of v4, /device:TPU:121, one launch (start us, length us, event | category | flops | bytes accessed | tf_op | source)
XLA Modules:
  0.0 44.5 jit_solution(2938695791704553617)
XLA Ops:
  0.6 0.0 copy-start
  0.7 0.8 %subtract_bitcast_fusion = s32[24]{0:T(128)S(1)} fusion(s32[1,24]{1,0:T(1,128)} %param.13, s32[]{:T(128)S(6)} %mul.27), kind=kLoop, calls=%fused_computation.37 | loop fusion | flops 24 | bytes 196 | tf_op jit(solution)/shard_map/sub | solution.py:276
  1.4 0.7 %multiply_bitcast_fusion = s32[4]{0:T(128)S(1)} fusion(s32[1,4]{1,0:T(1,128)} %param.17), kind=kLoop, calls=%fused_computation.38 | loop fusion | flops 4 | bytes 32 | tf_op jit(solution)/shard_map/mul | solution.py:286
  2.1 0.1 iota_compare_fusion.6
  2.2 0.8 %copy.40 = s32[128,8]{1,0:T(8,128)S(1)} copy(s32[128,8]{0,1:T(8,128)} %bitcast.65) | data formatting | bytes 8192 | tf_op jit(solution)/shard_map/transpose | solution.py:300
  3.0 0.1 eq.59
  3.0 11.3 %shard_map.131 = f32[12,24,128]{2,1,0:T(8,128)} custom-call(f32[24,128]{1,0:T(8,128)} %block_ref.1), custom_call_target="tpu_custom_call" | custom-call | tf_op jit(solution)/shard_map/pallas_call | solution.py:228
  14.4 1.1 %fusion.26 = f32[24,128]{1,0:T(8,128)S(1)} fusion(f32[288,128]{1,0:T(8,128)} %bitcast.61, s32[24]{0:T(128)S(1)} %subtract_bitcast_fusion), kind=kOutput, calls=%fused_computation.34 | convolution fusion | flops 10623744 | bytes 159840 | tf_op jit(solution)/shard_map/dot_general | solution.py:280
  15.5 0.9 %convert_reduce_fusion = f32[512,128]{1,0:T(8,128)S(1)} fusion(s32[8,128]{1,0:T(8,128)} %param.20), kind=kLoop, calls=%fused_computation.2 | loop fusion | flops 1507328 | bytes 266240 | tf_op jit(solution)/shard_map/reduce_sum | solution.py:308
  16.5 0.7 %copy-done.1 = f32[512,128]{1,0:T(8,128)} copy-done((f32[512,128]{1,0:T(8,128)}, f32[512,128]{1,0:T(8,128)S(1)}, u32[]{:S(2)}) %copy-start.1) | copy-done | bytes 262168
  17.2 0.9 %fusion.16 = f32[224,128]{1,0:T(8,128)S(1)} fusion(f32[512,128]{1,0:T(8,128)S(1)} %convert_reduce_fusion, s32[224]{0:T(256)} %bitcast.66), kind=kOutput, calls=%fused_computation.24 | convolution fusion | flops 29474816 | bytes 377728 | tf_op jit(solution)/shard_map/dot_general | solution.py:312
  18.1 1.0 %copy.42 = bf16[6,24,128]{1,0,2:T(8,128)(2,1)S(1)} copy(bf16[6,24,128]{2,1,0:T(8,128)(2,1)} %param.18) | data formatting | bytes 73728 | tf_op args[6]
  19.1 0.3 copy.35
  19.4 0.4 reshape.68
  19.8 0.3 copy.36
  20.1 0.2 copy-done.5
  20.3 0.5 %fusion = bf16[1536,128]{0,1:T(8,128)(2,1)S(1)} fusion(f32[1536,128]{0,1:T(8,128)S(1)} %copy.36, f32[24,128]{1,0:T(8,128)S(1)} %fusion.26, bf16[1536,24]{0,1:T(8,128)(2,1)S(1)} %copy-done.5), kind=kOutput, calls=%fused_computation.1 | convolution fusion | flops 57016320 | bytes 1265664 | tf_op jit(solution)/shard_map/dot_general | solution.py:285
  20.8 0.5 %fusion.12 = bf16[4,384,128]{1,2,0:T(8,128)(2,1)S(1)} fusion(bf16[4,384,384]{2,1,0:T(8,128)(2,1)S(1)} %copy-done, bf16[16,4,8,384]{3,2,1,0:T(8,128)(2,1)S(1)} %bitcast.62, pred[4,384]{1,0:T(4,128)(4,1)S(1)} %iota_compare_fusion.6), kind=kOutput, calls=%fused_computation.18 | convolution fusion | flops 151584768 | bytes 1967616 | tf_op jit(solution)/shard_map/prc,pcl->prl/dot_general | solution.py:291
  21.4 0.2 copy.38
  21.6 0.1 copy.39
  21.7 0.0 copy-start.3
  21.7 0.7 %copy-done.3 = bf16[3,4,128,128]{3,2,1,0:T(8,128)(2,1)} copy-done((bf16[3,4,128,128]{3,2,1,0:T(8,128)(2,1)}, bf16[3,4,128,128]{3,2,1,0:T(8,128)(2,1)S(1)}, u32[]{:S(2)}) %copy-start.3) | copy-done | bytes 393240
  22.4 0.8 %fusion.6 = bf16[1024,3,128]{2,0,1:T(8,128)(2,1)S(1)} fusion(bf16[3,512,128]{2,1,0:T(8,128)(2,1)S(1)} %bitcast.63, s32[1024]{0:T(1024)S(1)} %eq.59), kind=kOutput, calls=%fused_computation.11 | convolution fusion | flops 403570688 | bytes 1183744 | tf_op jit(solution)/shard_map/xn,cnl->xcl/dot_general | solution.py:301
  23.2 0.7 %copy.41 = bf16[1024,3,128]{2,1,0:T(4,128)(2,1)S(1)} copy(bf16[1024,3,128]{2,0,1:T(8,128)(2,1)S(1)} %fusion.6) | data formatting | bytes 1572864 | tf_op jit(solution)/shard_map/convert_element_type | solution.py:302
  23.9 0.0 copy-start.6
  23.9 0.6 %reshape.67 = bf16[128,24,128]{2,1,0:T(8,128)(2,1)S(1)} reshape(bf16[1024,3,128]{2,1,0:T(4,128)(2,1)S(1)} %copy.41) | data formatting | bytes 1572864 | tf_op jit(solution)/shard_map/reshape | solution.py:302
  24.6 0.4 convolution_bitcast_fusion.2
  24.9 0.6 %fusion.11 = f32[6,128,128]{2,0,1:T(8,128)S(1)} fusion(f32[128,6,128]{2,1,0:T(8,128)S(1)} %convolution_bitcast_fusion.2, f32[6,6,1]{1,0,2:T(8,128)S(1)} %copy-done.6, f32[128]{0:T(128)S(1)} %copy-done.8), kind=kOutput, calls=%fused_computation.16 | convolution fusion | flops 7176192 | bytes 787088 | tf_op jit(solution)/shard_map/ik,ekl->iel/dot_general | solution.py:305
  25.5 2.0 %convolution_bitcast_fusion.1 = f32[6,736,128]{2,1,0:T(8,128)S(1)} fusion(f32[6,128,128]{2,0,1:T(8,128)S(1)} %fusion.11, f32[224,128]{1,0:T(8,128)S(1)} %fusion.16, f32[512,128]{1,0:T(8,128)S(1)} %copy-done.2), kind=kOutput, calls=%fused_computation.7 | convolution fusion | flops 868315136 | bytes 3031040 | tf_op jit(solution)/shard_map/re,cel->crl/dot_general | solution.py:313
  27.5 0.9 %slice.9.send_ref = f32[6,224,128]{2,1,0:T(8,128)} slice(f32[6,736,128]{2,1,0:T(8,128)S(1)} %convolution_bitcast_fusion.1), slice={[0:6], [512:736], [0:128]} | slice | bytes 1376256 | tf_op jit(solution)/shard_map/slice | solution.py:315
  28.4 13.0 %shard_map.132 = f32[6,224,128]{2,1,0:T(8,128)} custom-call(f32[6,224,128]{2,1,0:T(8,128)} %slice.9.send_ref), custom_call_target="tpu_custom_call" | custom-call | tf_op jit(solution)/shard_map/pallas_call | solution.py:244
  41.5 3.0 %fusion.9 = bf16[512,6,128]{2,0,1:T(8,128)(2,1)} fusion(f32[6,224,128]{2,1,0:T(8,128)} %shard_map.132, f32[6,736,128]{2,1,0:T(8,128)S(1)} %convolution_bitcast_fusion.1, f32[512]{0:T(512)S(1)} %copy-done.9, s32[224]{0:T(256)S(1)} %bitcast.67), kind=kOutput, calls=%fused_computation.12 | convolution fusion | flops 1058258944 | bytes 3050368 | tf_op jit(solution)/shard_map/rn,crl->cnl/dot_general | solution.py:316
  (14 shorter events, 0.0 us)
Async XLA Ops:
  0.6 20.2 %copy-start = (bf16[4,384,384]{2,1,0:T(8,128)(2,1)S(1)}, bf16[4,384,384]{2,1,0:T(8,128)(2,1)}, u32[]{:S(2)}) copy-start(bf16[4,384,384]{2,1,0:T(8,128)(2,1)} %param.16) | copy-start | bytes 3538948
  0.6 18.4 %copy-start.4 = (bf16[512,3,128]{2,0,1:T(8,128)(2,1)S(1)}, bf16[512,3,128]{2,0,1:T(8,128)(2,1)}, u32[]{:S(2)}) copy-start(bf16[512,3,128]{2,0,1:T(8,128)(2,1)} %param.15) | copy-start | bytes 1179652
  16.5 0.7 %copy-start.1 = (f32[512,128]{1,0:T(8,128)}, f32[512,128]{1,0:T(8,128)S(1)}, u32[]{:S(2)}) copy-start(f32[512,128]{1,0:T(8,128)S(1)} %convert_reduce_fusion) | copy-start | bytes 786436
  19.4 0.9 %copy-start.5 = (bf16[1536,24]{0,1:T(8,128)(2,1)S(1)}, bf16[1536,24]{0,1:T(8,128)(2,1)}, u32[]{:S(2)}) copy-start(bf16[1536,24]{0,1:T(8,128)(2,1)} %param.14) | copy-start | bytes 221188
  21.7 0.7 %copy-start.3 = (bf16[3,4,128,128]{3,2,1,0:T(8,128)(2,1)}, bf16[3,4,128,128]{3,2,1,0:T(8,128)(2,1)S(1)}, u32[]{:S(2)}) copy-start(bf16[3,4,128,128]{3,2,1,0:T(8,128)(2,1)S(1)} %copy.39) | copy-start | bytes 1179652
  23.9 1.0 %copy-start.6 = (f32[6,6,1]{1,0,2:T(8,128)S(1)}, f32[6,6,1]{1,0,2:T(8,128)}, u32[]{:S(2)}) copy-start(f32[6,6,1]{1,0,2:T(8,128)} %constant.26) | copy-start | bytes 436
  23.9 1.0 %copy-start.8 = (f32[128]{0:T(128)S(1)}, f32[128]{0:T(128)}, u32[]{:S(2)}) copy-start(f32[128]{0:T(128)} %param.19) | copy-start | bytes 1540
  24.5 1.0 %copy-start.2 = (f32[512,128]{1,0:T(8,128)S(1)}, f32[512,128]{1,0:T(8,128)}, u32[]{:S(2)}) copy-start(f32[512,128]{1,0:T(8,128)} %copy-done.1) | copy-start | bytes 786436
  27.5 14.0 %copy-start.7 = (s32[1,224]{1,0:T(1,128)S(1)}, s32[1,224]{1,0:T(1,128)}, u32[]{:S(2)}) copy-start(s32[1,224]{1,0:T(1,128)} %param.21) | copy-start | bytes 2692
  27.5 13.9 %copy-start.9 = (f32[512]{0:T(512)S(1)}, f32[512]{0:T(512)}, u32[]{:S(2)}) copy-start(f32[512]{0:T(512)} %param.22) | copy-start | bytes 6148

commit v5 on v4

--- a/solution.py
+++ b/solution.py
@@ -89,9 +89,10 @@
     return 1
 
 
-def coarse_kernel(n_sub, n_grp, block_ref, out_ref, buf, send_sem, recv_sem):
+def coarse_kernel(n_sub, n_grp, block_ref, idx_ref, out_ref, buf, send_sem, recv_sem):
     s = lax.axis_index("sub")
     g = lax.axis_index("grp")
+    rows = block_ref.shape[0]
     barrier = pltpu.get_barrier_semaphore()
 
     def peers():
@@ -100,17 +101,11 @@
                 yield ds, gt
 
     def exists(ds, gt):
-        conds = []
         if ds < 0:
-            conds.append(s + ds >= 0)
+            return s + ds >= 0
         if ds > 0:
-            conds.append(s + ds < n_sub)
-        if ds == 0:
-            conds.append(g != gt)
-        cond = conds[0]
-        for c in conds[1:]:
-            cond = jnp.logical_and(cond, c)
-        return cond
+            return s + ds < n_sub
+        return g != gt
 
     for ds, gt in peers():
         def signal(ds=ds, gt=gt):
@@ -124,7 +119,7 @@
         slot_there = (1 - ds) * n_grp + g
         copy = pltpu.make_async_remote_copy(
             src_ref=block_ref,
-            dst_ref=buf.at[slot_there],
+            dst_ref=buf.at[pl.ds(slot_there * rows, rows)],
             send_sem=send_sem.at[(ds + 1) * n_grp + gt],
             recv_sem=recv_sem.at[slot_there],
             device_id=(s + ds, gt),
@@ -132,6 +127,7 @@
         )
         pl.when(exists(ds, gt))(copy.start)
         copies.append(copy)
+    buf[pl.ds((n_grp + g) * rows, rows), :] = block_ref[...]
     for (ds, gt), copy in zip(peers(), copies):
         pl.when(exists(ds, gt))(copy.wait_send)
     for dr in (-1, 0, 1):
@@ -139,32 +135,20 @@
             slot_here = (dr + 1) * n_grp + gr
             recv = pltpu.make_async_remote_copy(
                 src_ref=block_ref,
-                dst_ref=buf.at[slot_here],
+                dst_ref=buf.at[pl.ds(slot_here * rows, rows)],
                 send_sem=send_sem.at[slot_here],
                 recv_sem=recv_sem.at[slot_here],
                 device_id=(s + dr, gr),
                 device_id_type=MESH,
             )
-            cond = exists(dr, gr)
-
-            def take(slot_here=slot_here, recv=recv):
-                recv.wait_recv()
-                out_ref[slot_here] = buf[slot_here]
-
-            def clear(slot_here=slot_here):
-                out_ref[slot_here] = jnp.zeros(out_ref.shape[1:], out_ref.dtype)
-
-            pl.when(cond)(take)
-            def own(slot_here=slot_here):
-                out_ref[slot_here] = block_ref[...]
-
-            if dr == 0:
-                pl.when(g == gr)(own)
-            else:
-                pl.when(jnp.logical_not(cond))(clear)
-
-
-def face_kernel(n_sub, n_grp, send_ref, out_ref, buf, send_sem, recv_sem):
+            pl.when(exists(dr, gr))(recv.wait_recv)
+    first = (s - 1) * n_grp * rows
+    for r in range(idx_ref.shape[1]):
+        row = jnp.minimum(jnp.maximum(idx_ref[0, r] - first, 0), buf.shape[0] - 1)
+        out_ref[pl.ds(r, 1), :] = buf[pl.ds(row, 1), :]
+
+
+def face_kernel(n_sub, n_grp, base, send_ref, out_ref, buf, send_sem, recv_sem):
     s = lax.axis_index("sub")
     g = lax.axis_index("grp")
     barrier = pltpu.get_barrier_semaphore()
@@ -197,7 +181,7 @@
     for j, (k, lo, hi, row) in enumerate(SEND_PIECES):
         ds, dg = DIRECTIONS[k][:2]
         copy = pltpu.make_async_remote_copy(
-            src_ref=send_ref.at[:, pl.ds(lo, hi - lo)],
+            src_ref=send_ref.at[:, pl.ds(base + lo, hi - lo)],
             dst_ref=buf.at[:, pl.ds(row, hi - lo)],
             send_sem=send_sem.at[j],
             recv_sem=recv_sem.at[j],
@@ -222,28 +206,32 @@
         pl.when(exists(-ds, -dg))(take)
 
 
-def fetch_coarse(block, n_sub, n_grp):
+def fetch_corners(block, corner_idx, n_sub, n_grp):
     rows, width = block.shape
     slots = 3 * n_grp
-    out = pl.pallas_call(
+    return pl.pallas_call(
         functools.partial(coarse_kernel, n_sub, n_grp),
-        out_shape=jax.ShapeDtypeStruct((slots, rows, width), block.dtype),
-        in_specs=[pl.BlockSpec(memory_space=pltpu.VMEM)],
+        out_shape=jax.ShapeDtypeStruct((corner_idx.shape[1], width), block.dtype),
+        in_specs=[
+            pl.BlockSpec(memory_space=pltpu.VMEM),
+            pl.BlockSpec(memory_space=pltpu.SMEM),
+        ],
         out_specs=pl.BlockSpec(memory_space=pltpu.VMEM),
         scratch_shapes=[
-            pltpu.VMEM((slots, rows, width), block.dtype),
+            pltpu.VMEM((slots * rows, width), block.dtype),
             pltpu.SemaphoreType.DMA((slots,)),
             pltpu.SemaphoreType.DMA((slots,)),
         ],
         compiler_params=pltpu.CompilerParams(collective_id=0, has_side_effects=True),
-    )(block)
-    return out.reshape(slots * rows, width)
-
-
-def exchange_faces(send, n_sub, n_grp):
+    )(block, corner_idx)
+
+
+def exchange_faces(send, base, n_sub, n_grp):
     return pl.pallas_call(
-        functools.partial(face_kernel, n_sub, n_grp),
-        out_shape=jax.ShapeDtypeStruct(send.shape, send.dtype),
+        functools.partial(face_kernel, n_sub, n_grp, base),
+        out_shape=jax.ShapeDtypeStruct(
+            (send.shape[0], send.shape[1] - base, send.shape[2]), send.dtype
+        ),
         in_specs=[pl.BlockSpec(memory_space=pltpu.VMEM)],
         out_specs=pl.BlockSpec(memory_space=pltpu.VMEM),
         scratch_shapes=[
@@ -270,14 +258,7 @@
     interface,
     nodal_volume,
 ):
-    nearby = fetch_coarse(coarse, n_sub, n_grp)
-    block_rows = n_grp * coarse.shape[0]
-    offset = (lax.axis_index("sub") - 1) * block_rows
-    local_rows = corner_idx[0] - offset
-    selector = (local_rows[:, None] == jnp.arange(3 * block_rows, dtype=jnp.int32)[None, :]).astype(
-        jnp.float32
-    )
-    corner_vals = jnp.dot(selector, nearby, precision=lax.Precision.HIGHEST)
+    corner_vals = fetch_corners(coarse, corner_idx, n_sub, n_grp)
     node_count = force.shape[0]
     load_cases = force.shape[2]
     panels = panel_inv.shape[0]
@@ -312,7 +293,7 @@
     counts = jnp.concatenate([incidence, jnp.dot(picker, incidence)])
     both = jnp.einsum("re,cel->crl", counts, stress, precision=lax.Precision.HIGHEST)
     partial_value = both[:, :node_count]
-    added = exchange_faces(both[:, node_count:], n_sub, n_grp)
+    added = exchange_faces(both, node_count, n_sub, n_grp)
     summed = partial_value + jnp.einsum(
         "rn,crl->cnl", picker, added, precision=lax.Precision.HIGHEST
     )

time: 45 us -> 46.2 us (1.027)
  matrix products: 9.79 us -> 10.7 us
  Pallas kernels: 24.3 us -> 25.1 us
    dot_general x1, matrix products: 1.97 us -> 3.36 us  [shards(): jnp.einsum('re,cel->crl', counts, stress, precision=lax.Precision.HIGHEST)]
    dot_general x1 -> x0, matrix products: 1.13 us -> none  [shards(): corner_vals = jnp.dot(selector, nearby, precision=lax.Precision.HIGHEST)]
    convert_element_type x3, local copies, waits for them, and re-layouts: 0.96 us -> 1.96 us  [shards(): force.reshape(3 * node_count, load_cases).astype(jnp.float32) - correction]
    slice x1 -> x0, local copies, waits for them, and re-layouts: 0.89 us -> none  [shards(): added = exchange_faces(both[:, node_count:], n_sub, n_grp)]
    sub x1 -> x0, other arithmetic: 0.77 us -> none  [shards(): local_rows = corner_idx[0] - offset]
    pallas_call x2, Pallas kernels: 24.3 us -> 25.1 us  [the longest x1 13.7 us: exchange_faces(): pl.pallas_call(functools.partial(face_kernel, n_sub, n_grp, base), out_sh...]
    dot_general x1, matrix products: 0.94 us -> 1.59 us  [shards(): counts = jnp.concatenate([incidence, jnp.dot(picker, incidence)])]
    lt x1, other arithmetic: 0.08 us -> 0.64 us  [shards(): live_mask = jnp.arange(panel_rows)[None, :] < 3 * panel_nodes[0][:, None]]
where the time goes in v5:
time: 46.2 us; the launch traced here: 45.7 us
  Pallas kernels  25.1 us (54%)
  matrix products  10.7 us (23%)
  local copies, waits for them, and re-layouts  6.8 us (15%)
  other arithmetic  2.33 us (5%)
  between operations  0.86 us (2%)
    pallas_call x1, Pallas kernels, exchange_faces(): pl.pallas_call(functools.partial(face_kernel, n_sub, n_grp, base), out_sh...  13.7 us
    pallas_call x1, Pallas kernels, fetch_corners(): pl.pallas_call(functools.partial(coarse_kernel, n_sub, n_grp), out_shape=...  11.3 us
    dot_general x1, matrix products, shards(): jnp.einsum('re,cel->crl', counts, stress, precision=lax.Precision.HIGHEST)  3.36 us
    dot_general x1, matrix products, shards(): jnp.einsum('rn,crl->cnl', picker, added, precision=lax.Precision.HIGHEST)  3.03 us
    unnamed x23, local copies, waits for them, and re-layouts  2.33 us
    convert_element_type x3, local copies, waits for them, and re-layouts, shards(): force.reshape(3 * node_count, load_cases).astype(jnp.float32) - correction  1.96 us
    dot_general x1, matrix products, shards(): counts = jnp.concatenate([incidence, jnp.dot(picker, incidence)])  1.59 us
    reduce_sum x1, other arithmetic, shards(): jnp.sum((connect[:, None, :] == node_range[None, :, None]).astype(jnp.flo...  0.94 us

profile of v5, /device:TPU:121, one launch (start us, length us, event | category | flops | bytes accessed | tf_op | source)
XLA Modules:
  0.0 45.7 jit_solution(5393616146135522176)
XLA Ops:
  0.6 0.0 copy-start
  0.6 0.8 %multiply_bitcast_fusion = s32[4]{0:T(128)S(1)} fusion(s32[1,4]{1,0:T(1,128)} %param.17), kind=kLoop, calls=%fused_computation.34 | loop fusion | flops 4 | bytes 32 | tf_op jit(solution)/shard_map/mul | solution.py:267
  1.4 0.6 %iota_compare_fusion.4 = pred[4,384]{1,0:T(4,128)(4,1)} fusion(s32[4]{0:T(128)S(1)} %multiply_bitcast_fusion), kind=kLoop, calls=%fused_computation.33 | loop fusion | flops 1536 | bytes 1552 | tf_op jit(solution)/shard_map/lt | solution.py:267
  2.0 11.3 %shard_map.131 = f32[24,128]{1,0:T(8,128)} custom-call(f32[24,128]{1,0:T(8,128)} %block_ref.1, s32[1,24]{1,0:T(1,128)} %idx_ref.1), custom_call_target="tpu_custom_call" | custom-call | tf_op jit(solution)/shard_map/pallas_call | solution.py:212
  13.4 0.8 %copy.40 = s32[128,8]{1,0:T(8,128)S(1)} copy(s32[128,8]{0,1:T(8,128)} %bitcast.60) | data formatting | bytes 8192 | tf_op jit(solution)/shard_map/transpose | solution.py:281
  14.2 0.1 eq.43
  14.3 0.9 %convert_reduce_fusion = f32[512,128]{1,0:T(8,128)S(1)} fusion(s32[8,128]{1,0:T(8,128)} %param.20), kind=kLoop, calls=%fused_computation.2 | loop fusion | flops 1507328 | bytes 266240 | tf_op jit(solution)/shard_map/reduce_sum | solution.py:289
  15.2 1.6 %fusion.16 = f32[224,128]{1,0:T(8,128)} fusion(f32[512,128]{1,0:T(8,128)S(1)} %convert_reduce_fusion, s32[224]{0:T(256)} %bitcast.61), kind=kOutput, calls=%fused_computation.24 | convolution fusion | flops 29474816 | bytes 377728 | tf_op jit(solution)/shard_map/dot_general | solution.py:293
  16.8 0.9 %copy.42 = bf16[6,24,128]{1,0,2:T(8,128)(2,1)S(1)} copy(bf16[6,24,128]{2,1,0:T(8,128)(2,1)} %param.18) | data formatting | bytes 73728 | tf_op args[6]
  17.8 1.3 %copy.35 = f32[512,3,128]{2,1,0:T(4,128)S(1)} copy(bf16[512,3,128]{2,0,1:T(8,128)(2,1)} %param.15) | data formatting | bytes 1179648 | tf_op jit(solution)/shard_map/convert_element_type | solution.py:268
  19.1 0.4 reshape.57
  19.5 0.0 copy-start.4
  19.5 0.0 copy-start.7
  19.5 0.3 copy.36
  19.8 0.0 copy-done.5
  19.8 0.6 %copy-done.4 = bf16[1536,24]{0,1:T(8,128)(2,1)S(1)} copy-done((bf16[1536,24]{0,1:T(8,128)(2,1)S(1)}, bf16[1536,24]{0,1:T(8,128)(2,1)}, u32[]{:S(2)}) %copy-start.4) | copy-done | bytes 73752
  20.4 0.5 %fusion = bf16[1536,128]{0,1:T(8,128)(2,1)S(1)} fusion(f32[1536,128]{0,1:T(8,128)S(1)} %copy.36, f32[24,128]{1,0:T(8,128)S(1)} %copy-done.5, bf16[1536,24]{0,1:T(8,128)(2,1)S(1)} %copy-done.4), kind=kOutput, calls=%fused_computation.1 | convolution fusion | flops 57016320 | bytes 1265664 | tf_op jit(solution)/shard_map/dot_general | solution.py:266
  20.9 0.5 %fusion.12 = bf16[4,384,128]{1,2,0:T(8,128)(2,1)S(1)} fusion(bf16[4,384,384]{2,1,0:T(8,128)(2,1)S(1)} %copy-done, bf16[16,4,8,384]{3,2,1,0:T(8,128)(2,1)S(1)} %bitcast.57, pred[4,384]{1,0:T(4,128)(4,1)S(1)} %copy-done.7), kind=kOutput, calls=%fused_computation.18 | convolution fusion | flops 151584768 | bytes 1967616 | tf_op jit(solution)/shard_map/prc,pcl->prl/dot_general | solution.py:272
  21.4 0.2 copy.38
  21.7 0.1 copy.39
  21.7 0.0 copy-start.3
  21.8 0.7 %copy-done.3 = bf16[3,4,128,128]{3,2,1,0:T(8,128)(2,1)} copy-done((bf16[3,4,128,128]{3,2,1,0:T(8,128)(2,1)}, bf16[3,4,128,128]{3,2,1,0:T(8,128)(2,1)S(1)}, u32[]{:S(2)}) %copy-start.3) | copy-done | bytes 393240
  22.5 0.8 %fusion.6 = bf16[1024,3,128]{2,0,1:T(8,128)(2,1)S(1)} fusion(bf16[3,512,128]{2,1,0:T(8,128)(2,1)S(1)} %bitcast.58, s32[1024]{0:T(1024)S(1)} %eq.43), kind=kOutput, calls=%fused_computation.11 | convolution fusion | flops 403570688 | bytes 1183744 | tf_op jit(solution)/shard_map/xn,cnl->xcl/dot_general | solution.py:282
  23.3 0.7 %copy.41 = bf16[1024,3,128]{2,1,0:T(4,128)(2,1)S(1)} copy(bf16[1024,3,128]{2,0,1:T(8,128)(2,1)S(1)} %fusion.6) | data formatting | bytes 1572864 | tf_op jit(solution)/shard_map/convert_element_type | solution.py:283
  23.9 0.0 copy-start.6
  24.0 0.0 copy-start.9
  24.0 0.6 %reshape.56 = bf16[128,24,128]{2,1,0:T(8,128)(2,1)S(1)} reshape(bf16[1024,3,128]{2,1,0:T(4,128)(2,1)S(1)} %copy.41) | data formatting | bytes 1572864 | tf_op jit(solution)/shard_map/reshape | solution.py:283
  24.6 0.4 convolution_bitcast_fusion.2
  25.0 0.6 %fusion.11 = f32[6,128,128]{2,0,1:T(8,128)S(1)} fusion(f32[128,6,128]{2,1,0:T(8,128)S(1)} %convolution_bitcast_fusion.2, f32[6,6,1]{1,0,2:T(8,128)S(1)} %copy-done.6, f32[128]{0:T(128)S(1)} %copy-done.9), kind=kOutput, calls=%fused_computation.16 | convolution fusion | flops 7176192 | bytes 787088 | tf_op jit(solution)/shard_map/ik,ekl->iel/dot_general | solution.py:286
  25.6 3.4 %convolution_bitcast_fusion.1.send_ref = f32[6,736,128]{2,1,0:T(8,128)} fusion(f32[6,128,128]{2,0,1:T(8,128)S(1)} %fusion.11, f32[224,128]{1,0:T(8,128)S(1)} %copy-done.2, f32[512,128]{1,0:T(8,128)S(1)} %convert_reduce_fusion), kind=kOutput, calls=%fused_computation.7 | convolution fusion | flops 868315136 | bytes 3031040 | tf_op jit(solution)/shard_map/re,cel->crl/dot_general | solution.py:294
  29.0 13.7 %shard_map.132 = f32[6,224,128]{2,1,0:T(8,128)} custom-call(f32[6,736,128]{2,1,0:T(8,128)} %convolution_bitcast_fusion.1.send_ref), custom_call_target="tpu_custom_call" | custom-call | tf_op jit(solution)/shard_map/pallas_call | solution.py:230
  42.7 3.0 %fusion.9 = bf16[512,6,128]{2,0,1:T(8,128)(2,1)} fusion(f32[6,224,128]{2,1,0:T(8,128)} %shard_map.132, f32[6,736,128]{2,1,0:T(8,128)S(1)} %copy-done.1, f32[512]{0:T(512)S(1)} %copy-done.10, s32[224]{0:T(256)S(1)} %bitcast.62), kind=kOutput, calls=%fused_computation.12 | convolution fusion | flops 1058258944 | bytes 3050368 | tf_op jit(solution)/shard_map/rn,crl->cnl/dot_general | solution.py:297
  (13 shorter events, 0.0 us)
Async XLA Ops:
  0.6 20.3 %copy-start = (bf16[4,384,384]{2,1,0:T(8,128)(2,1)S(1)}, bf16[4,384,384]{2,1,0:T(8,128)(2,1)}, u32[]{:S(2)}) copy-start(bf16[4,384,384]{2,1,0:T(8,128)(2,1)} %param.16) | copy-start | bytes 3538948
  19.1 0.7 %copy-start.5 = (f32[24,128]{1,0:T(8,128)S(1)}, f32[24,128]{1,0:T(8,128)}, u32[]{:S(2)}) copy-start(f32[24,128]{1,0:T(8,128)} %shard_map.131) | copy-start | bytes 36868
  19.5 0.9 %copy-start.4 = (bf16[1536,24]{0,1:T(8,128)(2,1)S(1)}, bf16[1536,24]{0,1:T(8,128)(2,1)}, u32[]{:S(2)}) copy-start(bf16[1536,24]{0,1:T(8,128)(2,1)} %param.14) | copy-start | bytes 221188
  19.5 1.4 %copy-start.7 = (pred[4,384]{1,0:T(4,128)(4,1)S(1)}, pred[4,384]{1,0:T(4,128)(4,1)}, u32[]{:S(2)}) copy-start(pred[4,384]{1,0:T(4,128)(4,1)} %iota_compare_fusion.4) | copy-start | bytes 4612
  21.7 0.7 %copy-start.3 = (bf16[3,4,128,128]{3,2,1,0:T(8,128)(2,1)}, bf16[3,4,128,128]{3,2,1,0:T(8,128)(2,1)S(1)}, u32[]{:S(2)}) copy-start(bf16[3,4,128,128]{3,2,1,0:T(8,128)(2,1)S(1)} %copy.39) | copy-start | bytes 1179652
  23.9 1.0 %copy-start.6 = (f32[6,6,1]{1,0,2:T(8,128)S(1)}, f32[6,6,1]{1,0,2:T(8,128)}, u32[]{:S(2)}) copy-start(f32[6,6,1]{1,0,2:T(8,128)} %constant.15) | copy-start | bytes 436
  24.0 1.0 %copy-start.9 = (f32[128]{0:T(128)S(1)}, f32[128]{0:T(128)}, u32[]{:S(2)}) copy-start(f32[128]{0:T(128)} %param.19) | copy-start | bytes 1540
  24.6 1.0 %copy-start.2 = (f32[224,128]{1,0:T(8,128)S(1)}, f32[224,128]{1,0:T(8,128)}, u32[]{:S(2)}) copy-start(f32[224,128]{1,0:T(8,128)} %fusion.16) | copy-start | bytes 344068
  29.0 13.7 %copy-start.1 = (f32[6,736,128]{2,1,0:T(8,128)S(1)}, f32[6,736,128]{2,1,0:T(8,128)}, u32[]{:S(2)}) copy-start(f32[6,736,128]{2,1,0:T(8,128)} %convolution_bitcast_fusion.1.send_ref) | copy-start | bytes 6782980
  29.0 13.7 %copy-start.8 = (s32[1,224]{1,0:T(1,128)S(1)}, s32[1,224]{1,0:T(1,128)}, u32[]{:S(2)}) copy-start(s32[1,224]{1,0:T(1,128)} %param.21) | copy-start | bytes 2692
  29.0 13.7 %copy-start.10 = (f32[512]{0:T(512)S(1)}, f32[512]{0:T(512)}, u32[]{:S(2)}) copy-start(f32[512]{0:T(512)} %param.22) | copy-start | bytes 6148

commit v6 on v5

--- a/solution.py
+++ b/solution.py
@@ -148,7 +148,9 @@
         out_ref[pl.ds(r, 1), :] = buf[pl.ds(row, 1), :]
 
 
-def face_kernel(n_sub, n_grp, base, send_ref, out_ref, buf, send_sem, recv_sem):
+def face_kernel(
+    n_sub, n_grp, send_ref, stress_ref, own_ref, spread_ref, out_ref, buf, added, acc, send_sem, recv_sem
+):
     s = lax.axis_index("sub")
     g = lax.axis_index("grp")
     barrier = pltpu.get_barrier_semaphore()
@@ -181,7 +183,7 @@
     for j, (k, lo, hi, row) in enumerate(SEND_PIECES):
         ds, dg = DIRECTIONS[k][:2]
         copy = pltpu.make_async_remote_copy(
-            src_ref=send_ref.at[:, pl.ds(base + lo, hi - lo)],
+            src_ref=send_ref.at[:, pl.ds(lo, hi - lo)],
             dst_ref=buf.at[:, pl.ds(row, hi - lo)],
             send_sem=send_sem.at[j],
             recv_sem=recv_sem.at[j],
@@ -190,7 +192,12 @@
         )
         pl.when(exists(ds, dg))(copy.start)
         copies.append(copy)
-    out_ref[...] = jnp.zeros(out_ref.shape, out_ref.dtype)
+    added[...] = jnp.zeros(added.shape, added.dtype)
+    for c in range(acc.shape[0]):
+        acc[c] = jnp.dot(
+            own_ref[...], stress_ref[c], precision=lax.Precision.HIGHEST,
+            preferred_element_type=jnp.float32,
+        )
     for j, (k, lo, hi, row) in enumerate(SEND_PIECES):
         ds, dg = DIRECTIONS[k][:2]
         pl.when(exists(ds, dg))(copies[j].wait_send)
@@ -201,9 +208,15 @@
             for j in mine:
                 copies[j].wait_recv()
             for lo, hi, row in RECV_PIECES[k]:
-                out_ref[:, lo:hi, :] += buf[:, row:row + hi - lo, :]
+                added[:, lo:hi, :] += buf[:, row:row + hi - lo, :]
 
         pl.when(exists(-ds, -dg))(take)
+    for c in range(acc.shape[0]):
+        total = acc[c] + jnp.dot(
+            spread_ref[...], added[c], precision=lax.Precision.HIGHEST,
+            preferred_element_type=jnp.float32,
+        )
+        out_ref[c] = total.astype(out_ref.dtype)
 
 
 def fetch_corners(block, corner_idx, n_sub, n_grp):
@@ -226,21 +239,22 @@
     )(block, corner_idx)
 
 
-def exchange_faces(send, base, n_sub, n_grp):
+def exchange_faces(send, stress, own, spread, n_sub, n_grp):
+    parts, nodes = stress.shape[0], own.shape[0]
     return pl.pallas_call(
-        functools.partial(face_kernel, n_sub, n_grp, base),
-        out_shape=jax.ShapeDtypeStruct(
-            (send.shape[0], send.shape[1] - base, send.shape[2]), send.dtype
-        ),
-        in_specs=[pl.BlockSpec(memory_space=pltpu.VMEM)],
+        functools.partial(face_kernel, n_sub, n_grp),
+        out_shape=jax.ShapeDtypeStruct((parts, nodes, send.shape[2]), jnp.bfloat16),
+        in_specs=[pl.BlockSpec(memory_space=pltpu.VMEM)] * 4,
         out_specs=pl.BlockSpec(memory_space=pltpu.VMEM),
         scratch_shapes=[
             pltpu.VMEM((send.shape[0], int(SLOT_START[-1]), send.shape[2]), send.dtype),
+            pltpu.VMEM(send.shape, send.dtype),
+            pltpu.VMEM((parts, nodes, send.shape[2]), jnp.float32),
             pltpu.SemaphoreType.DMA((len(SEND_PIECES),)),
             pltpu.SemaphoreType.DMA((len(SEND_PIECES),)),
         ],
         compiler_params=pltpu.CompilerParams(collective_id=1, has_side_effects=True),
-    )(send)
+    )(send, stress, own, spread)
 
 
 def shards(
@@ -290,14 +304,13 @@
         (connect[:, None, :] == node_range[None, :, None]).astype(jnp.float32), axis=0
     )
     picker = (interface[0][:, None] == node_range[None, :]).astype(jnp.float32)
-    counts = jnp.concatenate([incidence, jnp.dot(picker, incidence)])
-    both = jnp.einsum("re,cel->crl", counts, stress, precision=lax.Precision.HIGHEST)
-    partial_value = both[:, :node_count]
-    added = exchange_faces(both, node_count, n_sub, n_grp)
-    summed = partial_value + jnp.einsum(
-        "rn,crl->cnl", picker, added, precision=lax.Precision.HIGHEST
-    )
-    stress_out = (summed / nodal_volume[None, :, None]).astype(jnp.bfloat16).transpose(1, 0, 2)
+    send = jnp.einsum(
+        "re,cel->crl", jnp.dot(picker, incidence), stress, precision=lax.Precision.HIGHEST
+    )
+    inverse_volume = 1.0 / nodal_volume
+    own = incidence * inverse_volume[:, None]
+    spread = picker.T * inverse_volume[:, None]
+    stress_out = exchange_faces(send, stress, own, spread, n_sub, n_grp).transpose(1, 0, 2)
     return (by_component.transpose(1, 0, 2), stress_out)
 
 

time: 46.2 us -> 43 us (0.931)
  matrix products: 10.7 us -> 5.23 us
  Pallas kernels: 25.1 us -> 27.5 us
    dot_general x3 -> x2, matrix products: 7.99 us -> 1.83 us  [the longest x1 1.57 us: shards(): jnp.einsum('re,cel->crl', jnp.dot(picker, incidence), stress, precision=l...]
    pallas_call x1, Pallas kernels: 13.7 us -> 16 us  [exchange_faces(): pl.pallas_call(functools.partial(face_kernel, n_sub, n_grp), out_shape=ja...]
    mul x0 -> x3, other arithmetic: none -> 1.92 us  [the longest x1 0.94 us: shards(): spread = picker.T * inverse_volume[:, None]]
    mul x1, other arithmetic: 0.75 us -> 0.01 us  [shards(): live_mask = jnp.arange(panel_rows)[None, :] < 3 * panel_nodes[0][:, None]]
    dot_general x1, matrix products: 0.52 us -> 1.23 us  [shards(): jnp.dot(coupling.astype(jnp.float32), corner_vals, precision=lax.Precisio...]
    reduce_sum x1, other arithmetic: 0.94 us -> 0.24 us  [shards(): jnp.sum((connect[:, None, :] == node_range[None, :, None]).astype(jnp.flo...]
    transpose x1, local copies, waits for them, and re-layouts: 0.79 us -> 0.1 us  [shards(): connect.T.reshape(-1)[:, None] == node_range[None, :]]
    lt x1, other arithmetic: 0.64 us -> 0.07 us  [shards(): live_mask = jnp.arange(panel_rows)[None, :] < 3 * panel_nodes[0][:, None]]
where the time goes in v6:
time: 43 us; the launch traced here: 42.6 us
  Pallas kernels  27.5 us (64%)
  local copies, waits for them, and re-layouts  6.76 us (16%)
  matrix products  5.23 us (12%)
  other arithmetic  2.24 us (5%)
  between operations  0.86 us (2%)
    pallas_call x1, Pallas kernels, exchange_faces(): pl.pallas_call(functools.partial(face_kernel, n_sub, n_grp), out_shape=ja...  16 us
    pallas_call x1, Pallas kernels, fetch_corners(): pl.pallas_call(functools.partial(coarse_kernel, n_sub, n_grp), out_shape=...  11.5 us
    unnamed x24, local copies, waits for them, and re-layouts  2.9 us
    convert_element_type x3, local copies, waits for them, and re-layouts, shards(): force.reshape(3 * node_count, load_cases).astype(jnp.float32) - correction  2.05 us
    dot_general x1, matrix products, shards(): jnp.einsum('re,cel->crl', jnp.dot(picker, incidence), stress, precision=l...  1.57 us
    dot_general x1, matrix products, shards(): jnp.dot(coupling.astype(jnp.float32), corner_vals, precision=lax.Precisio...  1.23 us
    mul x1, other arithmetic, shards(): spread = picker.T * inverse_volume[:, None]  0.94 us

profile of v6, /device:TPU:121, one launch (start us, length us, event | category | flops | bytes accessed | tf_op | source)
XLA Modules:
  0.0 42.6 jit_solution(3477845955004529535)
XLA Ops:
  0.6 0.0 copy-start
  0.6 1.4 %copy.34 = f32[512,3,128]{2,1,0:T(4,128)S(1)} copy(bf16[512,3,128]{2,0,1:T(8,128)(2,1)} %param.15) | data formatting | bytes 1179648 | tf_op jit(solution)/shard_map/convert_element_type | solution.py:282
  2.1 0.4 reshape.57
  2.4 0.0 copy-start.3
  2.5 0.3 copy.35
  2.7 11.5 %shard_map.131 = f32[24,128]{1,0:T(8,128)} custom-call(f32[24,128]{1,0:T(8,128)} %block_ref.1, s32[1,24]{1,0:T(1,128)} %idx_ref.1), custom_call_target="tpu_custom_call" | custom-call | tf_op jit(solution)/shard_map/pallas_call | solution.py:225
  14.2 1.2 %fusion = bf16[1536,128]{0,1:T(8,128)(2,1)S(1)} fusion(f32[1536,128]{0,1:T(8,128)S(1)} %copy.35, f32[24,128]{1,0:T(8,128)} %shard_map.131, bf16[1536,24]{0,1:T(8,128)(2,1)S(1)} %copy-done.3), kind=kOutput, calls=%fused_computation.1 | convolution fusion | flops 57016320 | bytes 1265664 | tf_op jit(solution)/shard_map/dot_general | solution.py:280
  15.5 0.1 iota_compare_fusion.5
  15.6 0.5 %fusion.8 = bf16[4,384,128]{1,2,0:T(8,128)(2,1)S(1)} fusion(bf16[4,384,384]{2,1,0:T(8,128)(2,1)S(1)} %copy-done, bf16[16,4,8,384]{3,2,1,0:T(8,128)(2,1)S(1)} %bitcast.50, pred[4,384]{1,0:T(4,128)(4,1)S(1)} %iota_compare_fusion.5), kind=kOutput, calls=%fused_computation.12 | convolution fusion | flops 151584768 | bytes 1967616 | tf_op jit(solution)/shard_map/prc,pcl->prl/dot_general | solution.py:286
  16.1 0.0 copy-start.5
  16.1 0.2 copy.37
  16.3 0.1 copy.38
  16.4 0.0 copy-start.2
  16.4 0.3 copy-done.5
  16.8 0.1 copy.39
  16.9 0.1 eq.50
  17.0 0.8 %fusion.4 = bf16[1024,3,128]{2,0,1:T(8,128)(2,1)S(1)} fusion(bf16[3,512,128]{2,1,0:T(8,128)(2,1)S(1)} %bitcast.51, s32[1024]{0:T(1024)S(1)} %eq.50), kind=kOutput, calls=%fused_computation.7 | convolution fusion | flops 403570688 | bytes 1183744 | tf_op jit(solution)/shard_map/xn,cnl->xcl/dot_general | solution.py:296
  17.7 0.7 %copy.40 = bf16[1024,3,128]{2,1,0:T(4,128)(2,1)S(1)} copy(bf16[1024,3,128]{2,0,1:T(8,128)(2,1)S(1)} %fusion.4) | data formatting | bytes 1572864 | tf_op jit(solution)/shard_map/convert_element_type | solution.py:297
  18.4 0.6 %reshape.56 = bf16[128,24,128]{2,1,0:T(8,128)(2,1)S(1)} reshape(bf16[1024,3,128]{2,1,0:T(4,128)(2,1)S(1)} %copy.40) | data formatting | bytes 1572864 | tf_op jit(solution)/shard_map/reshape | solution.py:297
  19.1 0.1 copy-done.4
  19.2 0.2 copy.41
  19.4 0.4 convolution_bitcast_fusion.2
  19.8 0.1 copy-done.6
  19.9 0.6 %fusion.18 = f32[128,128,6]{1,2,0:T(8,128)S(1)} fusion(f32[128,6,128]{2,1,0:T(8,128)S(1)} %convolution_bitcast_fusion.2, f32[6,6,1]{1,0,2:T(8,128)S(1)} %copy-done.6), kind=kOutput, calls=%fused_computation.30 | convolution fusion | flops 7077888 | bytes 786576 | tf_op jit(solution)/shard_map/ik,ekl->iel/dot_general | solution.py:300
  20.5 0.1 fusion.13.stress_ref
  20.6 0.2 convert_reduce_fusion
  20.9 0.3 convolution_bitcast_fusion.3
  21.1 1.6 %convolution_bitcast_fusion.1.send_ref = f32[6,224,128]{2,1,0:T(8,128)} fusion(f32[6,128,128]{2,1,0:T(8,128)S(1)} %fusion.13.stress_ref, f32[224,128,1]{1,0,2:T(8,128)S(1)} %convolution_bitcast_fusion.3), kind=kOutput, calls=%fused_computation.9 | convolution fusion | flops 264241152 | bytes 1196032 | tf_op jit(solution)/shard_map/re,cel->crl/dot_general | solution.py:307
  22.7 0.8 %broadcast_multiply_fusion.own_ref = f32[512,128]{1,0:T(8,128)} fusion(f32[512,128]{1,0:T(8,128)S(1)} %convert_reduce_fusion, f32[512]{0:T(512)S(1)} %broadcast_divide_fusion), kind=kLoop, calls=%fused_computation.25 | loop fusion | flops 65536 | bytes 526336 | tf_op jit(solution)/shard_map/mul | solution.py:311
  23.6 0.9 %fusion.11.spread_ref = f32[512,224]{1,0:T(8,128)} fusion(f32[512]{0:T(512)S(1)} %broadcast_divide_fusion, s32[224]{0:T(256)S(1)} %bitcast.55), kind=kLoop, calls=%fused_computation.18 | loop fusion | flops 229376 | bytes 461696 | tf_op jit(solution)/shard_map/mul | solution.py:312
  24.5 16.0 %shard_map.132 = bf16[6,512,128]{2,1,0:T(8,128)(2,1)} custom-call(f32[6,224,128]{2,1,0:T(8,128)} %convolution_bitcast_fusion.1.send_ref, f32[6,128,128]{2,1,0:T(8,128)} %copy-done.1, f32[512,128]{1,0:T(8,128)} %broadcast_multiply_fusion.own_ref, f32[512,224]{1,0:T(8,128)} %fusion.11.spread_ref), custom_call_target="tpu_custom_call" | custom-call | tf_op jit(solution)/shard_map/pallas_call | solution.py:244
  40.5 2.1 %copy.50 = bf16[512,6,128]{2,0,1:T(8,128)(2,1)} copy(bf16[512,6,128]{2,0,1:T(8,128)(2,1)} %bitcast.48) | data formatting | bytes 1572864
  (17 shorter events, 0.0 us)
Async XLA Ops:
  0.6 14.9 %copy-start = (bf16[4,384,384]{2,1,0:T(8,128)(2,1)S(1)}, bf16[4,384,384]{2,1,0:T(8,128)(2,1)}, u32[]{:S(2)}) copy-start(bf16[4,384,384]{2,1,0:T(8,128)(2,1)} %param.16) | copy-start | bytes 3538948
  2.4 11.8 %copy-start.3 = (bf16[1536,24]{0,1:T(8,128)(2,1)S(1)}, bf16[1536,24]{0,1:T(8,128)(2,1)}, u32[]{:S(2)}) copy-start(bf16[1536,24]{0,1:T(8,128)(2,1)} %param.14) | copy-start | bytes 221188
  2.5 13.0 %copy-start.10 = (s32[1,4]{1,0:T(1,128)S(1)}, s32[1,4]{1,0:T(1,128)}, u32[]{:S(2)}) copy-start(s32[1,4]{1,0:T(1,128)} %param.17) | copy-start | bytes 52
  16.1 0.7 %copy-start.5 = (s32[8,128]{1,0:T(8,128)S(1)}, s32[8,128]{1,0:T(8,128)}, u32[]{:S(2)}) copy-start(s32[8,128]{1,0:T(8,128)} %param.20) | copy-start | bytes 12292
  16.4 1.3 %copy-start.2 = (bf16[3,4,128,128]{3,2,1,0:T(8,128)(2,1)}, bf16[3,4,128,128]{3,2,1,0:T(8,128)(2,1)S(1)}, u32[]{:S(2)}) copy-start(bf16[3,4,128,128]{3,2,1,0:T(8,128)(2,1)S(1)} %copy.38) | copy-start | bytes 1179652
  18.4 0.8 %copy-start.4 = (bf16[6,24,128]{2,1,0:T(8,128)(2,1)S(1)}, bf16[6,24,128]{2,1,0:T(8,128)(2,1)}, u32[]{:S(2)}) copy-start(bf16[6,24,128]{2,1,0:T(8,128)(2,1)} %param.18) | copy-start | bytes 110596
  19.2 0.7 %copy-start.6 = (f32[6,6,1]{1,0,2:T(8,128)S(1)}, f32[6,6,1]{1,0,2:T(8,128)}, u32[]{:S(2)}) copy-start(f32[6,6,1]{1,0,2:T(8,128)} %constant.18) | copy-start | bytes 436
  19.4 1.1 %copy-start.9 = (f32[128]{0:T(128)S(1)}, f32[128]{0:T(128)}, u32[]{:S(2)}) copy-start(f32[128]{0:T(128)} %param.19) | copy-start | bytes 1540
  19.9 1.0 %copy-start.7 = (s32[1,224]{1,0:T(1,128)S(1)}, s32[1,224]{1,0:T(1,128)}, u32[]{:S(2)}) copy-start(s32[1,224]{1,0:T(1,128)} %param.21) | copy-start | bytes 2692
  20.5 2.2 %copy-start.8 = (f32[512]{0:T(512)S(1)}, f32[512]{0:T(512)}, u32[]{:S(2)}) copy-start(f32[512]{0:T(512)} %param.22) | copy-start | bytes 6148
  20.6 3.0 %copy-start.1 = (f32[6,128,128]{2,1,0:T(8,128)}, f32[6,128,128]{2,1,0:T(8,128)S(1)}, u32[]{:S(2)}) copy-start(f32[6,128,128]{2,1,0:T(8,128)S(1)} %fusion.13.stress_ref) | copy-start | bytes 1179652

commit v7 on v6

--- a/solution.py
+++ b/solution.py
@@ -243,7 +243,7 @@
     parts, nodes = stress.shape[0], own.shape[0]
     return pl.pallas_call(
         functools.partial(face_kernel, n_sub, n_grp),
-        out_shape=jax.ShapeDtypeStruct((parts, nodes, send.shape[2]), jnp.bfloat16),
+        out_shape=jax.ShapeDtypeStruct((parts, nodes, send.shape[2]), jnp.float32),
         in_specs=[pl.BlockSpec(memory_space=pltpu.VMEM)] * 4,
         out_specs=pl.BlockSpec(memory_space=pltpu.VMEM),
         scratch_shapes=[
@@ -310,7 +310,8 @@
     inverse_volume = 1.0 / nodal_volume
     own = incidence * inverse_volume[:, None]
     spread = picker.T * inverse_volume[:, None]
-    stress_out = exchange_faces(send, stress, own, spread, n_sub, n_grp).transpose(1, 0, 2)
+    stress_out = exchange_faces(send, stress, own, spread, n_sub, n_grp)
+    stress_out = stress_out.astype(jnp.bfloat16).transpose(1, 0, 2)
     return (by_component.transpose(1, 0, 2), stress_out)
 
 

time: 43 us -> 46.3 us (1.077)
  other arithmetic: 2.24 us -> 6.76 us
  local copies, waits for them, and re-layouts: 6.76 us -> 5.43 us
    transpose x0 -> x1, other arithmetic: none -> 2.39 us  [shards(): stress_out = stress_out.astype(jnp.bfloat16).transpose(1, 0, 2)]
    convert_element_type x3, local copies, waits for them, and re-layouts: 2.05 us -> 0.96 us  [shards(): force.reshape(3 * node_count, load_cases).astype(jnp.float32) - correction]
    unnamed x24 -> x19, local copies, waits for them, and re-layouts: 2.9 us -> 1.96 us
    mul x1, other arithmetic: 0.01 us -> 0.77 us  [shards(): live_mask = jnp.arange(panel_rows)[None, :] < 3 * panel_nodes[0][:, None]]
    dot_general x1, matrix products: 1.23 us -> 0.52 us  [shards(): jnp.dot(coupling.astype(jnp.float32), corner_vals, precision=lax.Precisio...]
    reduce_sum x1, other arithmetic: 0.24 us -> 0.94 us  [shards(): jnp.sum((connect[:, None, :] == node_range[None, :, None]).astype(jnp.flo...]
    transpose x1, local copies, waits for them, and re-layouts: 0.1 us -> 0.79 us  [shards(): connect.T.reshape(-1)[:, None] == node_range[None, :]]
    dot_general x1, matrix products: 0.26 us -> 0.94 us  [shards(): jnp.dot(picker, incidence)]
where the time goes in v7:
time: 46.3 us; the launch traced here: 45.9 us
  Pallas kernels  27.6 us (60%)
  other arithmetic  6.76 us (15%)
  local copies, waits for them, and re-layouts  5.43 us (12%)
  matrix products  5.2 us (11%)
  between operations  0.85 us (2%)
    pallas_call x1, Pallas kernels, exchange_faces(): pl.pallas_call(functools.partial(face_kernel, n_sub, n_grp), out_shape=ja...  16.3 us
    pallas_call x1, Pallas kernels, fetch_corners(): pl.pallas_call(functools.partial(coarse_kernel, n_sub, n_grp), out_shape=...  11.4 us
    transpose x1, other arithmetic, shards(): stress_out = stress_out.astype(jnp.bfloat16).transpose(1, 0, 2)  2.39 us
    unnamed x19, local copies, waits for them, and re-layouts  1.96 us
    dot_general x1, matrix products, shards(): jnp.einsum('re,cel->crl', jnp.dot(picker, incidence), stress, precision=l...  1.57 us
    convert_element_type x3, local copies, waits for them, and re-layouts, shards(): force.reshape(3 * node_count, load_cases).astype(jnp.float32) - correction  0.96 us
    dot_general x1, matrix products, shards(): jnp.dot(picker, incidence)  0.94 us
    reduce_sum x1, other arithmetic, shards(): jnp.sum((connect[:, None, :] == node_range[None, :, None]).astype(jnp.flo...  0.94 us

profile of v7, /device:TPU:121, one launch (start us, length us, event | category | flops | bytes accessed | tf_op | source)
XLA Modules:
  0.0 45.9 jit_solution(9678865291360477630)
XLA Ops:
  0.6 0.0 copy-start
  0.7 0.8 %multiply_bitcast_fusion = s32[4]{0:T(128)S(1)} fusion(s32[1,4]{1,0:T(1,128)} %param.17), kind=kLoop, calls=%fused_computation.29 | loop fusion | flops 4 | bytes 32 | tf_op jit(solution)/shard_map/mul | solution.py:281
  1.4 0.1 iota_compare_fusion.5
  1.5 0.7 %broadcast_divide_fusion = f32[512]{0:T(512)S(1)} fusion(f32[512]{0:T(512)} %param.22), kind=kLoop, calls=%fused_computation.28 | loop fusion | flops 512 | bytes 4096 | tf_op jit(solution)/shard_map/div | solution.py:310
  2.2 11.4 %shard_map.131 = f32[24,128]{1,0:T(8,128)} custom-call(f32[24,128]{1,0:T(8,128)} %block_ref.1, s32[1,24]{1,0:T(1,128)} %idx_ref.1), custom_call_target="tpu_custom_call" | custom-call | tf_op jit(solution)/shard_map/pallas_call | solution.py:225
  13.6 0.8 %copy.39 = s32[128,8]{1,0:T(8,128)S(1)} copy(s32[128,8]{0,1:T(8,128)} %bitcast.53) | data formatting | bytes 8192 | tf_op jit(solution)/shard_map/transpose | solution.py:295
  14.3 0.1 eq.50
  14.4 0.9 %convert_reduce_fusion = f32[512,128]{1,0:T(8,128)S(1)} fusion(s32[8,128]{1,0:T(8,128)} %param.20), kind=kLoop, calls=%fused_computation.2 | loop fusion | flops 1507328 | bytes 266240 | tf_op jit(solution)/shard_map/reduce_sum | solution.py:303
  15.4 0.9 %convolution_bitcast_fusion.3 = f32[224,128,1]{1,0,2:T(8,128)S(1)} fusion(f32[512,128]{1,0:T(8,128)S(1)} %convert_reduce_fusion, s32[224]{0:T(256)} %bitcast.54), kind=kOutput, calls=%fused_computation.13 | convolution fusion | flops 29474816 | bytes 377728 | tf_op jit(solution)/shard_map/dot_general | solution.py:308
  16.3 0.8 %broadcast_multiply_fusion.own_ref = f32[512,128]{1,0:T(8,128)} fusion(f32[512,128]{1,0:T(8,128)S(1)} %convert_reduce_fusion, f32[512]{0:T(512)S(1)} %broadcast_divide_fusion), kind=kLoop, calls=%fused_computation.26 | loop fusion | flops 65536 | bytes 526336 | tf_op jit(solution)/shard_map/mul | solution.py:311
  17.2 0.9 %copy.41 = bf16[6,24,128]{1,0,2:T(8,128)(2,1)S(1)} copy(bf16[6,24,128]{2,1,0:T(8,128)(2,1)} %param.18) | data formatting | bytes 73728 | tf_op args[6]
  18.1 0.9 %fusion.11.spread_ref = f32[512,224]{1,0:T(8,128)} fusion(f32[512]{0:T(512)S(1)} %broadcast_divide_fusion, s32[224]{0:T(256)S(1)} %bitcast.55), kind=kLoop, calls=%fused_computation.19 | loop fusion | flops 229376 | bytes 461696 | tf_op jit(solution)/shard_map/mul | solution.py:312
  19.1 0.3 copy.34
  19.4 0.4 reshape.57
  19.8 0.3 copy.35
  20.1 0.2 copy-done.4
  20.3 0.5 %fusion = bf16[1536,128]{0,1:T(8,128)(2,1)S(1)} fusion(f32[1536,128]{0,1:T(8,128)S(1)} %copy.35, f32[24,128]{1,0:T(8,128)S(1)} %copy-done.5, bf16[1536,24]{0,1:T(8,128)(2,1)S(1)} %copy-done.4), kind=kOutput, calls=%fused_computation.1 | convolution fusion | flops 57016320 | bytes 1265664 | tf_op jit(solution)/shard_map/dot_general | solution.py:280
  20.8 0.5 %fusion.8 = bf16[4,384,128]{1,2,0:T(8,128)(2,1)S(1)} fusion(bf16[4,384,384]{2,1,0:T(8,128)(2,1)S(1)} %copy-done, bf16[16,4,8,384]{3,2,1,0:T(8,128)(2,1)S(1)} %bitcast.50, pred[4,384]{1,0:T(4,128)(4,1)S(1)} %iota_compare_fusion.5), kind=kOutput, calls=%fused_computation.12 | convolution fusion | flops 151584768 | bytes 1967616 | tf_op jit(solution)/shard_map/prc,pcl->prl/dot_general | solution.py:286
  21.4 0.2 copy.37
  21.6 0.1 copy.38
  21.7 0.0 copy-start.2
  21.7 0.7 %copy-done.2 = bf16[3,4,128,128]{3,2,1,0:T(8,128)(2,1)} copy-done((bf16[3,4,128,128]{3,2,1,0:T(8,128)(2,1)}, bf16[3,4,128,128]{3,2,1,0:T(8,128)(2,1)S(1)}, u32[]{:S(2)}) %copy-start.2) | copy-done | bytes 393240
  22.4 0.8 %fusion.4 = bf16[1024,3,128]{2,0,1:T(8,128)(2,1)S(1)} fusion(bf16[3,512,128]{2,1,0:T(8,128)(2,1)S(1)} %bitcast.51, s32[1024]{0:T(1024)S(1)} %eq.50), kind=kOutput, calls=%fused_computation.7 | convolution fusion | flops 403570688 | bytes 1183744 | tf_op jit(solution)/shard_map/xn,cnl->xcl/dot_general | solution.py:296
  23.2 0.7 %copy.40 = bf16[1024,3,128]{2,1,0:T(4,128)(2,1)S(1)} copy(bf16[1024,3,128]{2,0,1:T(8,128)(2,1)S(1)} %fusion.4) | data formatting | bytes 1572864 | tf_op jit(solution)/shard_map/convert_element_type | solution.py:297
  23.9 0.0 copy-start.6
  23.9 0.6 %reshape.56 = bf16[128,24,128]{2,1,0:T(8,128)(2,1)S(1)} reshape(bf16[1024,3,128]{2,1,0:T(4,128)(2,1)S(1)} %copy.40) | data formatting | bytes 1572864 | tf_op jit(solution)/shard_map/reshape | solution.py:297
  24.5 0.4 convolution_bitcast_fusion.2
  24.9 0.6 %fusion.18 = f32[128,128,6]{1,2,0:T(8,128)S(1)} fusion(f32[128,6,128]{2,1,0:T(8,128)S(1)} %convolution_bitcast_fusion.2, f32[6,6,1]{1,0,2:T(8,128)S(1)} %copy-done.6), kind=kOutput, calls=%fused_computation.31 | convolution fusion | flops 7077888 | bytes 786576 | tf_op jit(solution)/shard_map/ik,ekl->iel/dot_general | solution.py:300
  25.5 0.1 fusion.13.stress_ref
  25.6 1.6 %convolution_bitcast_fusion.1.send_ref = f32[6,224,128]{2,1,0:T(8,128)} fusion(f32[6,128,128]{2,1,0:T(8,128)S(1)} %fusion.13.stress_ref, f32[224,128,1]{1,0,2:T(8,128)S(1)} %convolution_bitcast_fusion.3), kind=kOutput, calls=%fused_computation.9 | convolution fusion | flops 264241152 | bytes 1196032 | tf_op jit(solution)/shard_map/re,cel->crl/dot_general | solution.py:307
  27.2 16.3 %shard_map.132 = f32[6,512,128]{2,1,0:T(8,128)} custom-call(f32[6,224,128]{2,1,0:T(8,128)} %convolution_bitcast_fusion.1.send_ref, f32[6,128,128]{2,1,0:T(8,128)} %copy-done.1, f32[512,128]{1,0:T(8,128)} %broadcast_multiply_fusion.own_ref, f32[512,224]{1,0:T(8,128)} %fusion.11.spread_ref), custom_call_target="tpu_custom_call" | custom-call | tf_op jit(solution)/shard_map/pallas_call | solution.py:244
  43.5 2.4 %convert_bitcast_fusion = bf16[512,6,128]{2,0,1:T(8,128)(2,1)} fusion(f32[6,512,128]{2,1,0:T(8,128)} %shard_map.132), kind=kLoop, calls=%fused_computation.17 | loop fusion | flops 393216 | bytes 2359296 | tf_op jit(solution)/shard_map/transpose | solution.py:314
  (13 shorter events, 0.0 us)
Async XLA Ops:
  0.6 20.2 %copy-start = (bf16[4,384,384]{2,1,0:T(8,128)(2,1)S(1)}, bf16[4,384,384]{2,1,0:T(8,128)(2,1)}, u32[]{:S(2)}) copy-start(bf16[4,384,384]{2,1,0:T(8,128)(2,1)} %param.16) | copy-start | bytes 3538948
  0.6 17.5 %copy-start.7 = (s32[1,224]{1,0:T(1,128)S(1)}, s32[1,224]{1,0:T(1,128)}, u32[]{:S(2)}) copy-start(s32[1,224]{1,0:T(1,128)} %param.21) | copy-start | bytes 2692
  0.7 18.4 %copy-start.3 = (bf16[512,3,128]{2,0,1:T(8,128)(2,1)S(1)}, bf16[512,3,128]{2,0,1:T(8,128)(2,1)}, u32[]{:S(2)}) copy-start(bf16[512,3,128]{2,0,1:T(8,128)(2,1)} %param.15) | copy-start | bytes 1179652
  19.4 0.9 %copy-start.4 = (bf16[1536,24]{0,1:T(8,128)(2,1)S(1)}, bf16[1536,24]{0,1:T(8,128)(2,1)}, u32[]{:S(2)}) copy-start(bf16[1536,24]{0,1:T(8,128)(2,1)} %param.14) | copy-start | bytes 221188
  19.4 0.9 %copy-start.5 = (f32[24,128]{1,0:T(8,128)S(1)}, f32[24,128]{1,0:T(8,128)}, u32[]{:S(2)}) copy-start(f32[24,128]{1,0:T(8,128)} %shard_map.131) | copy-start | bytes 36868
  21.7 0.7 %copy-start.2 = (bf16[3,4,128,128]{3,2,1,0:T(8,128)(2,1)}, bf16[3,4,128,128]{3,2,1,0:T(8,128)(2,1)S(1)}, u32[]{:S(2)}) copy-start(bf16[3,4,128,128]{3,2,1,0:T(8,128)(2,1)S(1)} %copy.38) | copy-start | bytes 1179652
  23.9 1.0 %copy-start.6 = (f32[6,6,1]{1,0,2:T(8,128)S(1)}, f32[6,6,1]{1,0,2:T(8,128)}, u32[]{:S(2)}) copy-start(f32[6,6,1]{1,0,2:T(8,128)} %constant.18) | copy-start | bytes 436
  24.5 0.9 %copy-start.8 = (f32[128]{0:T(128)S(1)}, f32[128]{0:T(128)}, u32[]{:S(2)}) copy-start(f32[128]{0:T(128)} %param.19) | copy-start | bytes 1540
  25.6 1.6 %copy-start.1 = (f32[6,128,128]{2,1,0:T(8,128)}, f32[6,128,128]{2,1,0:T(8,128)S(1)}, u32[]{:S(2)}) copy-start(f32[6,128,128]{2,1,0:T(8,128)S(1)} %fusion.13.stress_ref) | copy-start | bytes 1179652

commit v8 on v6

--- a/solution.py
+++ b/solution.py
@@ -149,7 +149,8 @@
 
 
 def face_kernel(
-    n_sub, n_grp, send_ref, stress_ref, own_ref, spread_ref, out_ref, buf, added, acc, send_sem, recv_sem
+    n_sub, n_grp, send_ref, stress_ref, own_ref, spread_ref, vol_ref, out_ref, buf, added, acc,
+    send_sem, recv_sem,
 ):
     s = lax.axis_index("sub")
     g = lax.axis_index("grp")
@@ -216,7 +217,7 @@
             spread_ref[...], added[c], precision=lax.Precision.HIGHEST,
             preferred_element_type=jnp.float32,
         )
-        out_ref[c] = total.astype(out_ref.dtype)
+        out_ref[c] = (total / vol_ref[...]).astype(out_ref.dtype)
 
 
 def fetch_corners(block, corner_idx, n_sub, n_grp):
@@ -239,12 +240,12 @@
     )(block, corner_idx)
 
 
-def exchange_faces(send, stress, own, spread, n_sub, n_grp):
+def exchange_faces(send, stress, own, spread, volume, n_sub, n_grp):
     parts, nodes = stress.shape[0], own.shape[0]
     return pl.pallas_call(
         functools.partial(face_kernel, n_sub, n_grp),
         out_shape=jax.ShapeDtypeStruct((parts, nodes, send.shape[2]), jnp.bfloat16),
-        in_specs=[pl.BlockSpec(memory_space=pltpu.VMEM)] * 4,
+        in_specs=[pl.BlockSpec(memory_space=pltpu.VMEM)] * 5,
         out_specs=pl.BlockSpec(memory_space=pltpu.VMEM),
         scratch_shapes=[
             pltpu.VMEM((send.shape[0], int(SLOT_START[-1]), send.shape[2]), send.dtype),
@@ -254,7 +255,7 @@
             pltpu.SemaphoreType.DMA((len(SEND_PIECES),)),
         ],
         compiler_params=pltpu.CompilerParams(collective_id=1, has_side_effects=True),
-    )(send, stress, own, spread)
+    )(send, stress, own, spread, volume)
 
 
 def shards(
@@ -307,10 +308,9 @@
     send = jnp.einsum(
         "re,cel->crl", jnp.dot(picker, incidence), stress, precision=lax.Precision.HIGHEST
     )
-    inverse_volume = 1.0 / nodal_volume
-    own = incidence * inverse_volume[:, None]
-    spread = picker.T * inverse_volume[:, None]
-    stress_out = exchange_faces(send, stress, own, spread, n_sub, n_grp).transpose(1, 0, 2)
+    spread = (node_range[:, None] == interface[0][None, :]).astype(jnp.float32)
+    volume = nodal_volume.reshape(node_count, 1)
+    stress_out = exchange_faces(send, stress, incidence, spread, volume, n_sub, n_grp).transpose(1, 0, 2)
     return (by_component.transpose(1, 0, 2), stress_out)
 
 

time: 43 us -> 43 us (level)
  other arithmetic: 2.24 us -> 1.29 us
  local copies, waits for them, and re-layouts: 6.76 us -> 7.66 us
    mul x2 -> x0, other arithmetic: 1.79 us -> none  [the longest x1 0.94 us: shards(): spread = picker.T * inverse_volume[:, None]]
    reshape x0 -> x1, local copies, waits for them, and re-layouts: none -> 0.89 us  [shards(): volume = nodal_volume.reshape(node_count, 1)]
    convert_element_type x0 -> x1, other arithmetic: none -> 0.85 us  [shards(): spread = (node_range[:, None] == interface[0][None, :]).astype(jnp.float32)]
    unnamed x24 -> x26, local copies, waits for them, and re-layouts: 2.9 us -> 2.9 us
where the time goes in v8:
time: 43 us; the launch traced here: 42.6 us
  Pallas kernels  27.6 us (64%)
  local copies, waits for them, and re-layouts  7.66 us (18%)
  matrix products  5.23 us (12%)
  other arithmetic  1.29 us (3%)
  between operations  0.87 us (2%)
    pallas_call x1, Pallas kernels, exchange_faces(): pl.pallas_call(functools.partial(face_kernel, n_sub, n_grp), out_shape=ja...  16.1 us
    pallas_call x1, Pallas kernels, fetch_corners(): pl.pallas_call(functools.partial(coarse_kernel, n_sub, n_grp), out_shape=...  11.5 us
    unnamed x26, local copies, waits for them, and re-layouts  2.9 us
    convert_element_type x3, local copies, waits for them, and re-layouts, shards(): force.reshape(3 * node_count, load_cases).astype(jnp.float32) - correction  2.05 us
    dot_general x1, matrix products, shards(): jnp.einsum('re,cel->crl', jnp.dot(picker, incidence), stress, precision=l...  1.57 us
    dot_general x1, matrix products, shards(): jnp.dot(coupling.astype(jnp.float32), corner_vals, precision=lax.Precisio...  1.23 us
    reshape x1, local copies, waits for them, and re-layouts, shards(): volume = nodal_volume.reshape(node_count, 1)  0.89 us

profile of v8, /device:TPU:121, one launch (start us, length us, event | category | flops | bytes accessed | tf_op | source)
XLA Modules:
  0.0 42.6 jit_solution(16715975124630223959)
XLA Ops:
  0.6 0.0 copy-start
  0.6 1.4 %copy.36 = f32[512,3,128]{2,1,0:T(4,128)S(1)} copy(bf16[512,3,128]{2,0,1:T(8,128)(2,1)} %param.15) | data formatting | bytes 1179648 | tf_op jit(solution)/shard_map/convert_element_type | solution.py:283
  2.1 0.4 reshape.60
  2.4 0.0 copy-start.4
  2.5 0.3 copy.37
  2.7 11.5 %shard_map.131 = f32[24,128]{1,0:T(8,128)} custom-call(f32[24,128]{1,0:T(8,128)} %block_ref.1, s32[1,24]{1,0:T(1,128)} %idx_ref.1), custom_call_target="tpu_custom_call" | custom-call | tf_op jit(solution)/shard_map/pallas_call | solution.py:226
  14.2 1.2 %fusion = bf16[1536,128]{0,1:T(8,128)(2,1)S(1)} fusion(f32[1536,128]{0,1:T(8,128)S(1)} %copy.37, f32[24,128]{1,0:T(8,128)} %shard_map.131, bf16[1536,24]{0,1:T(8,128)(2,1)S(1)} %copy-done.4), kind=kOutput, calls=%fused_computation.1 | convolution fusion | flops 57016320 | bytes 1265664 | tf_op jit(solution)/shard_map/dot_general | solution.py:281
  15.5 0.1 iota_compare_fusion.5
  15.6 0.5 %fusion.8 = bf16[4,384,128]{1,2,0:T(8,128)(2,1)S(1)} fusion(bf16[4,384,384]{2,1,0:T(8,128)(2,1)S(1)} %copy-done, bf16[16,4,8,384]{3,2,1,0:T(8,128)(2,1)S(1)} %bitcast.51, pred[4,384]{1,0:T(4,128)(4,1)S(1)} %iota_compare_fusion.5), kind=kOutput, calls=%fused_computation.12 | convolution fusion | flops 151584768 | bytes 1967616 | tf_op jit(solution)/shard_map/prc,pcl->prl/dot_general | solution.py:287
  16.1 0.0 copy-start.6
  16.1 0.2 copy.39
  16.3 0.1 copy.40
  16.4 0.0 copy-start.3
  16.4 0.3 copy-done.6
  16.8 0.1 copy.41
  16.9 0.1 eq.56
  17.0 0.8 %fusion.4 = bf16[1024,3,128]{2,0,1:T(8,128)(2,1)S(1)} fusion(bf16[3,512,128]{2,1,0:T(8,128)(2,1)S(1)} %bitcast.52, s32[1024]{0:T(1024)S(1)} %eq.56), kind=kOutput, calls=%fused_computation.7 | convolution fusion | flops 403570688 | bytes 1183744 | tf_op jit(solution)/shard_map/xn,cnl->xcl/dot_general | solution.py:297
  17.7 0.7 %copy.42 = bf16[1024,3,128]{2,1,0:T(4,128)(2,1)S(1)} copy(bf16[1024,3,128]{2,0,1:T(8,128)(2,1)S(1)} %fusion.4) | data formatting | bytes 1572864 | tf_op jit(solution)/shard_map/convert_element_type | solution.py:298
  18.4 0.6 %reshape.58 = bf16[128,24,128]{2,1,0:T(8,128)(2,1)S(1)} reshape(bf16[1024,3,128]{2,1,0:T(4,128)(2,1)S(1)} %copy.42) | data formatting | bytes 1572864 | tf_op jit(solution)/shard_map/reshape | solution.py:298
  19.1 0.1 copy-done.5
  19.2 0.2 copy.43
  19.4 0.4 convolution_bitcast_fusion.2
  19.8 0.1 copy-done.7
  19.9 0.6 %fusion.18 = f32[128,128,6]{1,2,0:T(8,128)S(1)} fusion(f32[128,6,128]{2,1,0:T(8,128)S(1)} %convolution_bitcast_fusion.2, f32[6,6,1]{1,0,2:T(8,128)S(1)} %copy-done.7), kind=kOutput, calls=%fused_computation.28 | convolution fusion | flops 7077888 | bytes 786576 | tf_op jit(solution)/shard_map/ik,ekl->iel/dot_general | solution.py:301
  20.5 0.1 fusion.13.stress_ref
  20.6 0.2 convert_reduce_fusion.own_ref
  20.9 0.3 convolution_bitcast_fusion.3
  21.1 1.6 %convolution_bitcast_fusion.1.send_ref = f32[6,224,128]{2,1,0:T(8,128)} fusion(f32[6,128,128]{2,1,0:T(8,128)S(1)} %fusion.13.stress_ref, f32[224,128,1]{1,0,2:T(8,128)S(1)} %convolution_bitcast_fusion.3), kind=kOutput, calls=%fused_computation.9 | convolution fusion | flops 264241152 | bytes 1196032 | tf_op jit(solution)/shard_map/re,cel->crl/dot_general | solution.py:308
  22.7 0.8 %fusion.11.spread_ref = f32[512,224]{1,0:T(8,128)} fusion(s32[224]{0:T(256)S(1)} %bitcast.56), kind=kLoop, calls=%fused_computation.18 | loop fusion | flops 229376 | bytes 459648 | tf_op jit(solution)/shard_map/convert_element_type | solution.py:311
  23.6 0.9 %copy.45.vol_ref = f32[512,1]{1,0:T(8,128)} copy(f32[512,1]{0,1:T(1,128)S(1)} %bitcast.57) | data formatting | bytes 4096 | tf_op jit(solution)/shard_map/reshape | solution.py:312
  24.5 16.1 %shard_map.132 = bf16[6,512,128]{2,1,0:T(8,128)(2,1)} custom-call(f32[6,224,128]{2,1,0:T(8,128)} %convolution_bitcast_fusion.1.send_ref, f32[6,128,128]{2,1,0:T(8,128)} %copy-done.1, f32[512,128]{1,0:T(8,128)} %copy-done.2, f32[512,224]{1,0:T(8,128)} %fusion.11.spread_ref, f32[512,1]{1,0:T(8,128)} %copy.45.vol_ref), custom_call_target="tpu_custom_call" | custom-call | tf_op jit(solution)/shard_map/pallas_call | solution.py:245
  40.6 2.1 %copy.53 = bf16[512,6,128]{2,0,1:T(8,128)(2,1)} copy(bf16[512,6,128]{2,0,1:T(8,128)(2,1)} %bitcast.49) | data formatting | bytes 1572864
  (18 shorter events, 0.0 us)
Async XLA Ops:
  0.6 14.9 %copy-start = (bf16[4,384,384]{2,1,0:T(8,128)(2,1)S(1)}, bf16[4,384,384]{2,1,0:T(8,128)(2,1)}, u32[]{:S(2)}) copy-start(bf16[4,384,384]{2,1,0:T(8,128)(2,1)} %param.16) | copy-start | bytes 3538948
  2.4 11.8 %copy-start.4 = (bf16[1536,24]{0,1:T(8,128)(2,1)S(1)}, bf16[1536,24]{0,1:T(8,128)(2,1)}, u32[]{:S(2)}) copy-start(bf16[1536,24]{0,1:T(8,128)(2,1)} %param.14) | copy-start | bytes 221188
  2.5 13.0 %copy-start.11 = (s32[1,4]{1,0:T(1,128)S(1)}, s32[1,4]{1,0:T(1,128)}, u32[]{:S(2)}) copy-start(s32[1,4]{1,0:T(1,128)} %param.17) | copy-start | bytes 52
  16.1 0.7 %copy-start.6 = (s32[8,128]{1,0:T(8,128)S(1)}, s32[8,128]{1,0:T(8,128)}, u32[]{:S(2)}) copy-start(s32[8,128]{1,0:T(8,128)} %param.20) | copy-start | bytes 12292
  16.4 1.3 %copy-start.3 = (bf16[3,4,128,128]{3,2,1,0:T(8,128)(2,1)}, bf16[3,4,128,128]{3,2,1,0:T(8,128)(2,1)S(1)}, u32[]{:S(2)}) copy-start(bf16[3,4,128,128]{3,2,1,0:T(8,128)(2,1)S(1)} %copy.40) | copy-start | bytes 1179652
  18.4 0.8 %copy-start.5 = (bf16[6,24,128]{2,1,0:T(8,128)(2,1)S(1)}, bf16[6,24,128]{2,1,0:T(8,128)(2,1)}, u32[]{:S(2)}) copy-start(bf16[6,24,128]{2,1,0:T(8,128)(2,1)} %param.18) | copy-start | bytes 110596
  19.2 0.7 %copy-start.7 = (f32[6,6,1]{1,0,2:T(8,128)S(1)}, f32[6,6,1]{1,0,2:T(8,128)}, u32[]{:S(2)}) copy-start(f32[6,6,1]{1,0,2:T(8,128)} %constant.15) | copy-start | bytes 436
  19.4 1.1 %copy-start.10 = (f32[128]{0:T(128)S(1)}, f32[128]{0:T(128)}, u32[]{:S(2)}) copy-start(f32[128]{0:T(128)} %param.19) | copy-start | bytes 1540
  19.9 1.0 %copy-start.8 = (s32[1,224]{1,0:T(1,128)S(1)}, s32[1,224]{1,0:T(1,128)}, u32[]{:S(2)}) copy-start(s32[1,224]{1,0:T(1,128)} %param.21) | copy-start | bytes 2692
  20.6 3.0 %copy-start.1 = (f32[6,128,128]{2,1,0:T(8,128)}, f32[6,128,128]{2,1,0:T(8,128)S(1)}, u32[]{:S(2)}) copy-start(f32[6,128,128]{2,1,0:T(8,128)S(1)} %fusion.13.stress_ref) | copy-start | bytes 1179652
  20.6 3.0 %copy-start.9 = (f32[512]{0:T(512)S(1)}, f32[512]{0:T(512)}, u32[]{:S(2)}) copy-start(f32[512]{0:T(512)} %param.22) | copy-start | bytes 6148
  20.9 3.6 %copy-start.2 = (f32[512,128]{1,0:T(8,128)}, f32[512,128]{1,0:T(8,128)S(1)}, u32[]{:S(2)}) copy-start(f32[512,128]{1,0:T(8,128)S(1)} %convert_reduce_fusion.own_ref) | copy-start | bytes 786436

commit v9 on v8

--- a/solution.py
+++ b/solution.py
@@ -244,7 +244,7 @@
     parts, nodes = stress.shape[0], own.shape[0]
     return pl.pallas_call(
         functools.partial(face_kernel, n_sub, n_grp),
-        out_shape=jax.ShapeDtypeStruct((parts, nodes, send.shape[2]), jnp.bfloat16),
+        out_shape=jax.ShapeDtypeStruct((parts, nodes, send.shape[2]), jnp.float32),
         in_specs=[pl.BlockSpec(memory_space=pltpu.VMEM)] * 5,
         out_specs=pl.BlockSpec(memory_space=pltpu.VMEM),
         scratch_shapes=[
@@ -256,6 +256,19 @@
         ],
         compiler_params=pltpu.CompilerParams(collective_id=1, has_side_effects=True),
     )(send, stress, own, spread, volume)
+
+
+def cast_kernel(in_ref, out_ref):
+    out_ref[...] = in_ref[...].astype(out_ref.dtype)
+
+
+def to_bf16(values):
+    return pl.pallas_call(
+        cast_kernel,
+        out_shape=jax.ShapeDtypeStruct(values.shape, jnp.bfloat16),
+        in_specs=[pl.BlockSpec(memory_space=pltpu.VMEM)],
+        out_specs=pl.BlockSpec(memory_space=pltpu.VMEM),
+    )(values)
 
 
 def shards(
@@ -310,7 +323,7 @@
     )
     spread = (node_range[:, None] == interface[0][None, :]).astype(jnp.float32)
     volume = nodal_volume.reshape(node_count, 1)
-    stress_out = exchange_faces(send, stress, incidence, spread, volume, n_sub, n_grp).transpose(1, 0, 2)
+    stress_out = to_bf16(exchange_faces(send, stress, incidence, spread, volume, n_sub, n_grp)).transpose(1, 0, 2)
     return (by_component.transpose(1, 0, 2), stress_out)
 
 

time: 43 us -> 49.7 us (1.16)
  other arithmetic: 1.29 us -> 4 us
  Pallas kernels: 27.6 us -> 30.1 us
  matrix products: 5.23 us -> 7.52 us
  local copies, waits for them, and re-layouts: 7.66 us -> 6.78 us
    pallas_call x0 -> x1, Pallas kernels: none -> 2.36 us  [to_bf16(): pl.pallas_call(cast_kernel, out_shape=jax.ShapeDtypeStruct(values.shape,...]
    dot_general x1, matrix products: 0.26 us -> 1.62 us  [shards(): jnp.dot(picker, incidence)]
    unnamed x26 -> x19, local copies, waits for them, and re-layouts: 2.9 us -> 1.78 us
    convert_element_type x3, local copies, waits for them, and re-layouts: 2.05 us -> 0.96 us  [shards(): force.reshape(3 * node_count, load_cases).astype(jnp.float32) - correction]
    mul x1, other arithmetic: 0.01 us -> 0.77 us  [shards(): live_mask = jnp.arange(panel_rows)[None, :] < 3 * panel_nodes[0][:, None]]
    dot_general x1, matrix products: 0.5 us -> 1.25 us  [shards(): jnp.einsum('prc,pcl->prl', panel_inv, reduced, preferred_element_type=jnp...]
    reduce_sum x1, other arithmetic: 0.24 us -> 0.94 us  [shards(): jnp.sum((connect[:, None, :] == node_range[None, :, None]).astype(jnp.flo...]
    transpose x1, local copies, waits for them, and re-layouts: 0.1 us -> 0.79 us  [shards(): connect.T.reshape(-1)[:, None] == node_range[None, :]]
where the time goes in v9:
time: 49.7 us; the launch traced here: 49.2 us
  Pallas kernels  30.1 us (61%)
  matrix products  7.52 us (15%)
  local copies, waits for them, and re-layouts  6.78 us (14%)
  other arithmetic  4 us (8%)
  between operations  0.85 us (2%)
    pallas_call x1, Pallas kernels, exchange_faces(): pl.pallas_call(functools.partial(face_kernel, n_sub, n_grp), out_shape=ja...  16.3 us
    pallas_call x1, Pallas kernels, fetch_corners(): pl.pallas_call(functools.partial(coarse_kernel, n_sub, n_grp), out_shape=...  11.3 us
    pallas_call x1, Pallas kernels, to_bf16(): pl.pallas_call(cast_kernel, out_shape=jax.ShapeDtypeStruct(values.shape,...  2.36 us
    unnamed x19, local copies, waits for them, and re-layouts  1.78 us
    dot_general x1, matrix products, shards(): jnp.dot(picker, incidence)  1.62 us
    dot_general x1, matrix products, shards(): jnp.einsum('re,cel->crl', jnp.dot(picker, incidence), stress, precision=l...  1.57 us
    reshape x1, local copies, waits for them, and re-layouts, shards(): volume = nodal_volume.reshape(node_count, 1)  1.54 us
    convert_element_type x1, other arithmetic, shards(): spread = (node_range[:, None] == interface[0][None, :]).astype(jnp.float32)  1.53 us

profile of v9, /device:TPU:121, one launch (start us, length us, event | category | flops | bytes accessed | tf_op | source)
XLA Modules:
  0.0 49.2 jit_solution(11622596580681502432)
XLA Ops:
  0.6 0.0 copy-start
  0.7 0.8 %multiply_bitcast_fusion = s32[4]{0:T(128)S(1)} fusion(s32[1,4]{1,0:T(1,128)} %param.17), kind=kLoop, calls=%fused_computation.26 | loop fusion | flops 4 | bytes 32 | tf_op jit(solution)/shard_map/mul | solution.py:295
  1.4 0.6 %iota_compare_fusion.5 = pred[4,384]{1,0:T(4,128)(4,1)} fusion(s32[4]{0:T(128)S(1)} %multiply_bitcast_fusion), kind=kLoop, calls=%fused_computation.25 | loop fusion | flops 1536 | bytes 1552 | tf_op jit(solution)/shard_map/lt | solution.py:295
  2.1 11.3 %shard_map.131 = f32[24,128]{1,0:T(8,128)} custom-call(f32[24,128]{1,0:T(8,128)} %block_ref.1, s32[1,24]{1,0:T(1,128)} %idx_ref.1), custom_call_target="tpu_custom_call" | custom-call | tf_op jit(solution)/shard_map/pallas_call | solution.py:226
  13.4 0.8 %copy.41 = s32[128,8]{1,0:T(8,128)S(1)} copy(s32[128,8]{0,1:T(8,128)} %bitcast.54) | data formatting | bytes 8192 | tf_op jit(solution)/shard_map/transpose | solution.py:309
  14.2 0.1 eq.56
  14.3 0.9 %convert_reduce_fusion.own_ref = f32[512,128]{1,0:T(8,128)S(1)} fusion(s32[8,128]{1,0:T(8,128)} %param.20), kind=kLoop, calls=%fused_computation.2 | loop fusion | flops 1507328 | bytes 266240 | tf_op jit(solution)/shard_map/reduce_sum | solution.py:317
  15.3 1.6 %convolution_bitcast_fusion.3 = f32[224,128,1]{1,0,2:T(8,128)} fusion(f32[512,128]{1,0:T(8,128)S(1)} %convert_reduce_fusion.own_ref, s32[224]{0:T(256)} %bitcast.55), kind=kOutput, calls=%fused_computation.13 | convolution fusion | flops 29474816 | bytes 377728 | tf_op jit(solution)/shard_map/dot_general | solution.py:322
  16.9 0.9 %copy.43 = bf16[6,24,128]{1,0,2:T(8,128)(2,1)S(1)} copy(bf16[6,24,128]{2,1,0:T(8,128)(2,1)} %param.18) | data formatting | bytes 73728 | tf_op args[6]
  17.8 1.5 %copy.45.vol_ref = f32[512,1]{1,0:T(8,128)} copy(f32[512,1]{0,1:T(1,128)} %bitcast.57) | data formatting | bytes 4096 | tf_op jit(solution)/shard_map/reshape | solution.py:325
  19.4 1.5 %fusion.11.spread_ref = f32[512,224]{1,0:T(8,128)} fusion(s32[224]{0:T(256)} %bitcast.56), kind=kLoop, calls=%fused_computation.18 | loop fusion | flops 229376 | bytes 459648 | tf_op jit(solution)/shard_map/convert_element_type | solution.py:324
  20.9 0.3 copy.36
  21.2 0.4 reshape.60
  21.6 0.3 copy.37
  21.9 0.0 copy-done.6
  21.9 1.4 %fusion = bf16[1536,128]{0,1:T(8,128)(2,1)S(1)} fusion(f32[1536,128]{0,1:T(8,128)S(1)} %copy.37, f32[24,128]{1,0:T(8,128)S(1)} %copy-done.6, bf16[1536,24]{0,1:T(8,128)(2,1)} %param.14), kind=kOutput, calls=%fused_computation.1 | convolution fusion | flops 57016320 | bytes 1265664 | tf_op jit(solution)/shard_map/dot_general | solution.py:294
  23.4 1.3 %fusion.8 = bf16[4,384,128]{1,2,0:T(8,128)(2,1)S(1)} fusion(bf16[4,384,384]{2,1,0:T(8,128)(2,1)S(1)} %copy-done, bf16[16,4,8,384]{3,2,1,0:T(8,128)(2,1)S(1)} %bitcast.51, pred[4,384]{1,0:T(4,128)(4,1)} %iota_compare_fusion.5), kind=kOutput, calls=%fused_computation.12 | convolution fusion | flops 151584768 | bytes 1967616 | tf_op jit(solution)/shard_map/prc,pcl->prl/dot_general | solution.py:300
  24.6 0.2 copy.39
  24.9 0.1 copy.40
  24.9 0.0 copy-start.4
  25.0 0.7 %copy-done.4 = bf16[3,4,128,128]{3,2,1,0:T(8,128)(2,1)} copy-done((bf16[3,4,128,128]{3,2,1,0:T(8,128)(2,1)}, bf16[3,4,128,128]{3,2,1,0:T(8,128)(2,1)S(1)}, u32[]{:S(2)}) %copy-start.4) | copy-done | bytes 393240
  25.7 0.8 %fusion.4 = bf16[1024,3,128]{2,0,1:T(8,128)(2,1)S(1)} fusion(bf16[3,512,128]{2,1,0:T(8,128)(2,1)S(1)} %bitcast.52, s32[1024]{0:T(1024)S(1)} %eq.56), kind=kOutput, calls=%fused_computation.7 | convolution fusion | flops 403570688 | bytes 1183744 | tf_op jit(solution)/shard_map/xn,cnl->xcl/dot_general | solution.py:310
  26.5 0.7 %copy.42 = bf16[1024,3,128]{2,1,0:T(4,128)(2,1)S(1)} copy(bf16[1024,3,128]{2,0,1:T(8,128)(2,1)S(1)} %fusion.4) | data formatting | bytes 1572864 | tf_op jit(solution)/shard_map/convert_element_type | solution.py:311
  27.1 0.0 copy-start.7
  27.2 0.6 %reshape.58 = bf16[128,24,128]{2,1,0:T(8,128)(2,1)S(1)} reshape(bf16[1024,3,128]{2,1,0:T(4,128)(2,1)S(1)} %copy.42) | data formatting | bytes 1572864 | tf_op jit(solution)/shard_map/reshape | solution.py:311
  27.8 0.0 copy-start.8
  27.8 0.4 convolution_bitcast_fusion.2
  28.2 0.6 %fusion.18 = f32[128,128,6]{1,2,0:T(8,128)S(1)} fusion(f32[128,6,128]{2,1,0:T(8,128)S(1)} %convolution_bitcast_fusion.2, f32[6,6,1]{1,0,2:T(8,128)S(1)} %copy-done.7), kind=kOutput, calls=%fused_computation.28 | convolution fusion | flops 7077888 | bytes 786576 | tf_op jit(solution)/shard_map/ik,ekl->iel/dot_general | solution.py:314
  28.8 0.1 fusion.13.stress_ref
  28.9 1.6 %convolution_bitcast_fusion.1.send_ref = f32[6,224,128]{2,1,0:T(8,128)} fusion(f32[6,128,128]{2,1,0:T(8,128)S(1)} %fusion.13.stress_ref, f32[224,128,1]{1,0,2:T(8,128)S(1)} %copy-done.3), kind=kOutput, calls=%fused_computation.9 | convolution fusion | flops 264241152 | bytes 1196032 | tf_op jit(solution)/shard_map/re,cel->crl/dot_general | solution.py:321
  30.5 16.3 %shard_map.132.in_ref = f32[6,512,128]{2,1,0:T(8,128)} custom-call(f32[6,224,128]{2,1,0:T(8,128)} %convolution_bitcast_fusion.1.send_ref, f32[6,128,128]{2,1,0:T(8,128)} %copy-done.1, f32[512,128]{1,0:T(8,128)} %copy-done.2, f32[512,224]{1,0:T(8,128)} %fusion.11.spread_ref, f32[512,1]{1,0:T(8,128)} %copy.45.vol_ref), custom_call_target="tpu_custom_call" | custom-call | tf_op jit(solution)/shard_map/pallas_call | solution.py:245
  46.8 2.4 %shard_map.133 = bf16[6,512,128]{2,1,0:T(8,128)(2,1)} custom-call(f32[6,512,128]{2,1,0:T(8,128)} %shard_map.132.in_ref), custom_call_target="tpu_custom_call" | custom-call | tf_op jit(solution)/shard_map/pallas_call | solution.py:266
  (12 shorter events, 0.0 us)
Async XLA Ops:
  0.6 22.7 %copy-start = (bf16[4,384,384]{2,1,0:T(8,128)(2,1)S(1)}, bf16[4,384,384]{2,1,0:T(8,128)(2,1)}, u32[]{:S(2)}) copy-start(bf16[4,384,384]{2,1,0:T(8,128)(2,1)} %param.16) | copy-start | bytes 3538948
  0.6 20.2 %copy-start.5 = (bf16[512,3,128]{2,0,1:T(8,128)(2,1)S(1)}, bf16[512,3,128]{2,0,1:T(8,128)(2,1)}, u32[]{:S(2)}) copy-start(bf16[512,3,128]{2,0,1:T(8,128)(2,1)} %param.15) | copy-start | bytes 1179652
  15.2 6.4 %copy-start.2 = (f32[512,128]{1,0:T(8,128)}, f32[512,128]{1,0:T(8,128)S(1)}, u32[]{:S(2)}) copy-start(f32[512,128]{1,0:T(8,128)S(1)} %convert_reduce_fusion.own_ref) | copy-start | bytes 786436
  21.2 0.7 %copy-start.6 = (f32[24,128]{1,0:T(8,128)S(1)}, f32[24,128]{1,0:T(8,128)}, u32[]{:S(2)}) copy-start(f32[24,128]{1,0:T(8,128)} %shard_map.131) | copy-start | bytes 36868
  24.9 0.7 %copy-start.4 = (bf16[3,4,128,128]{3,2,1,0:T(8,128)(2,1)}, bf16[3,4,128,128]{3,2,1,0:T(8,128)(2,1)S(1)}, u32[]{:S(2)}) copy-start(bf16[3,4,128,128]{3,2,1,0:T(8,128)(2,1)S(1)} %copy.40) | copy-start | bytes 1179652
  27.1 1.0 %copy-start.7 = (f32[6,6,1]{1,0,2:T(8,128)S(1)}, f32[6,6,1]{1,0,2:T(8,128)}, u32[]{:S(2)}) copy-start(f32[6,6,1]{1,0,2:T(8,128)} %constant.15) | copy-start | bytes 436
  27.8 1.0 %copy-start.8 = (f32[128]{0:T(128)S(1)}, f32[128]{0:T(128)}, u32[]{:S(2)}) copy-start(f32[128]{0:T(128)} %param.19) | copy-start | bytes 1540
  27.8 1.1 %copy-start.3 = (f32[224,128,1]{1,0,2:T(8,128)S(1)}, f32[224,128,1]{1,0,2:T(8,128)}, u32[]{:S(2)}) copy-start(f32[224,128,1]{1,0,2:T(8,128)} %convolution_bitcast_fusion.3) | copy-start | bytes 344068
  28.9 1.6 %copy-start.1 = (f32[6,128,128]{2,1,0:T(8,128)}, f32[6,128,128]{2,1,0:T(8,128)S(1)}, u32[]{:S(2)}) copy-start(f32[6,128,128]{2,1,0:T(8,128)S(1)} %fusion.13.stress_ref) | copy-start | bytes 1179652

commit v10 on v6

--- a/solution.py
+++ b/solution.py
@@ -277,7 +277,7 @@
     load_cases = force.shape[2]
     panels = panel_inv.shape[0]
     panel_rows = panel_inv.shape[1]
-    correction = jnp.dot(coupling.astype(jnp.float32), corner_vals, precision=lax.Precision.HIGHEST)
+    correction = jnp.dot(coupling.astype(jnp.float32), corner_vals, precision=lax.Precision.HIGH)
     live_mask = jnp.arange(panel_rows)[None, :] < 3 * panel_nodes[0][:, None]
     reduced = (force.reshape(3 * node_count, load_cases).astype(jnp.float32) - correction).reshape(
         panels, panel_rows, load_cases
@@ -305,7 +305,7 @@
     )
     picker = (interface[0][:, None] == node_range[None, :]).astype(jnp.float32)
     send = jnp.einsum(
-        "re,cel->crl", jnp.dot(picker, incidence), stress, precision=lax.Precision.HIGHEST
+        "re,cel->crl", jnp.dot(picker, incidence), stress, precision=lax.Precision.HIGH
     )
     inverse_volume = 1.0 / nodal_volume
     own = incidence * inverse_volume[:, None]

time: 43 us -> 42.6 us (level)
  no operation moved by 1% of the time
where the time goes in v10:
time: 42.6 us; the launch traced here: 42.2 us
  Pallas kernels  27.5 us (65%)
  local copies, waits for them, and re-layouts  6.76 us (16%)
  matrix products  4.82 us (11%)
  other arithmetic  2.24 us (5%)
  between operations  0.86 us (2%)
    pallas_call x1, Pallas kernels, exchange_faces(): pl.pallas_call(functools.partial(face_kernel, n_sub, n_grp), out_shape=ja...  16 us
    pallas_call x1, Pallas kernels, fetch_corners(): pl.pallas_call(functools.partial(coarse_kernel, n_sub, n_grp), out_shape=...  11.5 us
    unnamed x24, local copies, waits for them, and re-layouts  2.9 us
    convert_element_type x3, local copies, waits for them, and re-layouts, shards(): force.reshape(3 * node_count, load_cases).astype(jnp.float32) - correction  2.05 us
    dot_general x1, matrix products, shards(): jnp.einsum('re,cel->crl', jnp.dot(picker, incidence), stress, precision=l...  1.27 us
    dot_general x1, matrix products, shards(): jnp.dot(coupling.astype(jnp.float32), corner_vals, precision=lax.Precisio...  1.12 us
    mul x1, other arithmetic, shards(): spread = picker.T * inverse_volume[:, None]  0.94 us

profile of v10, /device:TPU:121, one launch (start us, length us, event | category | flops | bytes accessed | tf_op | source)
XLA Modules:
  0.0 42.2 jit_solution(6268732571980732306)
XLA Ops:
  0.6 0.0 copy-start
  0.6 1.4 %copy.34 = f32[512,3,128]{2,1,0:T(4,128)S(1)} copy(bf16[512,3,128]{2,0,1:T(8,128)(2,1)} %param.15) | data formatting | bytes 1179648 | tf_op jit(solution)/shard_map/convert_element_type | solution.py:282
  2.1 0.4 reshape.57
  2.4 0.0 copy-start.3
  2.5 0.3 copy.35
  2.7 11.5 %shard_map.131 = f32[24,128]{1,0:T(8,128)} custom-call(f32[24,128]{1,0:T(8,128)} %block_ref.1, s32[1,24]{1,0:T(1,128)} %idx_ref.1), custom_call_target="tpu_custom_call" | custom-call | tf_op jit(solution)/shard_map/pallas_call | solution.py:225
  14.2 1.1 %fusion = bf16[1536,128]{0,1:T(8,128)(2,1)S(1)} fusion(f32[1536,128]{0,1:T(8,128)S(1)} %copy.35, f32[24,128]{1,0:T(8,128)} %shard_map.131, bf16[1536,24]{0,1:T(8,128)(2,1)S(1)} %copy-done.3), kind=kOutput, calls=%fused_computation.1 | convolution fusion | flops 28704768 | bytes 1265664 | tf_op jit(solution)/shard_map/dot_general | solution.py:280
  15.4 0.1 iota_compare_fusion.5
  15.5 0.5 %fusion.8 = bf16[4,384,128]{1,2,0:T(8,128)(2,1)S(1)} fusion(bf16[4,384,384]{2,1,0:T(8,128)(2,1)S(1)} %copy-done, bf16[16,4,8,384]{3,2,1,0:T(8,128)(2,1)S(1)} %bitcast.50, pred[4,384]{1,0:T(4,128)(4,1)S(1)} %iota_compare_fusion.5), kind=kOutput, calls=%fused_computation.12 | convolution fusion | flops 151584768 | bytes 1967616 | tf_op jit(solution)/shard_map/prc,pcl->prl/dot_general | solution.py:286
  16.0 0.2 copy.37
  16.2 0.1 copy.38
  16.3 0.0 copy-start.2
  16.3 0.3 copy-done.5
  16.7 0.1 copy.39
  16.8 0.1 eq.50
  16.9 0.8 %fusion.4 = bf16[1024,3,128]{2,0,1:T(8,128)(2,1)S(1)} fusion(bf16[3,512,128]{2,1,0:T(8,128)(2,1)S(1)} %bitcast.51, s32[1024]{0:T(1024)S(1)} %eq.50), kind=kOutput, calls=%fused_computation.7 | convolution fusion | flops 403570688 | bytes 1183744 | tf_op jit(solution)/shard_map/xn,cnl->xcl/dot_general | solution.py:296
  17.6 0.7 %copy.40 = bf16[1024,3,128]{2,1,0:T(4,128)(2,1)S(1)} copy(bf16[1024,3,128]{2,0,1:T(8,128)(2,1)S(1)} %fusion.4) | data formatting | bytes 1572864 | tf_op jit(solution)/shard_map/convert_element_type | solution.py:297
  18.3 0.6 %reshape.56 = bf16[128,24,128]{2,1,0:T(8,128)(2,1)S(1)} reshape(bf16[1024,3,128]{2,1,0:T(4,128)(2,1)S(1)} %copy.40) | data formatting | bytes 1572864 | tf_op jit(solution)/shard_map/reshape | solution.py:297
  19.0 0.1 copy-done.4
  19.1 0.2 copy.41
  19.3 0.0 copy-start.9
  19.3 0.4 convolution_bitcast_fusion.2
  19.6 0.1 copy-done.6
  19.8 0.6 %fusion.18 = f32[128,128,6]{1,2,0:T(8,128)S(1)} fusion(f32[128,6,128]{2,1,0:T(8,128)S(1)} %convolution_bitcast_fusion.2, f32[6,6,1]{1,0,2:T(8,128)S(1)} %copy-done.6), kind=kOutput, calls=%fused_computation.30 | convolution fusion | flops 7077888 | bytes 786576 | tf_op jit(solution)/shard_map/ik,ekl->iel/dot_general | solution.py:300
  20.4 0.1 fusion.13.stress_ref
  20.5 0.2 convert_reduce_fusion
  20.8 0.3 convolution_bitcast_fusion.3
  21.0 1.3 %convolution_bitcast_fusion.1.send_ref = f32[6,224,128]{2,1,0:T(8,128)} fusion(f32[6,128,128]{2,1,0:T(8,128)S(1)} %fusion.13.stress_ref, f32[224,128,1]{1,0,2:T(8,128)S(1)} %convolution_bitcast_fusion.3), kind=kOutput, calls=%fused_computation.9 | convolution fusion | flops 132120576 | bytes 1196032 | tf_op jit(solution)/shard_map/re,cel->crl/dot_general | solution.py:307
  22.3 0.8 %broadcast_multiply_fusion.own_ref = f32[512,128]{1,0:T(8,128)} fusion(f32[512,128]{1,0:T(8,128)S(1)} %convert_reduce_fusion, f32[512]{0:T(512)S(1)} %broadcast_divide_fusion), kind=kLoop, calls=%fused_computation.25 | loop fusion | flops 65536 | bytes 526336 | tf_op jit(solution)/shard_map/mul | solution.py:311
  23.2 0.9 %fusion.11.spread_ref = f32[512,224]{1,0:T(8,128)} fusion(f32[512]{0:T(512)S(1)} %broadcast_divide_fusion, s32[224]{0:T(256)S(1)} %bitcast.55), kind=kLoop, calls=%fused_computation.18 | loop fusion | flops 229376 | bytes 461696 | tf_op jit(solution)/shard_map/mul | solution.py:312
  24.1 16.0 %shard_map.132 = bf16[6,512,128]{2,1,0:T(8,128)(2,1)} custom-call(f32[6,224,128]{2,1,0:T(8,128)} %convolution_bitcast_fusion.1.send_ref, f32[6,128,128]{2,1,0:T(8,128)} %copy-done.1, f32[512,128]{1,0:T(8,128)} %broadcast_multiply_fusion.own_ref, f32[512,224]{1,0:T(8,128)} %fusion.11.spread_ref), custom_call_target="tpu_custom_call" | custom-call | tf_op jit(solution)/shard_map/pallas_call | solution.py:244
  40.1 2.1 %copy.50 = bf16[512,6,128]{2,0,1:T(8,128)(2,1)} copy(bf16[512,6,128]{2,0,1:T(8,128)(2,1)} %bitcast.48) | data formatting | bytes 1572864
  (17 shorter events, 0.0 us)
Async XLA Ops:
  0.6 14.8 %copy-start = (bf16[4,384,384]{2,1,0:T(8,128)(2,1)S(1)}, bf16[4,384,384]{2,1,0:T(8,128)(2,1)}, u32[]{:S(2)}) copy-start(bf16[4,384,384]{2,1,0:T(8,128)(2,1)} %param.16) | copy-start | bytes 3538948
  2.4 11.8 %copy-start.3 = (bf16[1536,24]{0,1:T(8,128)(2,1)S(1)}, bf16[1536,24]{0,1:T(8,128)(2,1)}, u32[]{:S(2)}) copy-start(bf16[1536,24]{0,1:T(8,128)(2,1)} %param.14) | copy-start | bytes 221188
  2.5 12.9 %copy-start.10 = (s32[1,4]{1,0:T(1,128)S(1)}, s32[1,4]{1,0:T(1,128)}, u32[]{:S(2)}) copy-start(s32[1,4]{1,0:T(1,128)} %param.17) | copy-start | bytes 52
  16.0 0.7 %copy-start.5 = (s32[8,128]{1,0:T(8,128)S(1)}, s32[8,128]{1,0:T(8,128)}, u32[]{:S(2)}) copy-start(s32[8,128]{1,0:T(8,128)} %param.20) | copy-start | bytes 12292
  16.3 1.3 %copy-start.2 = (bf16[3,4,128,128]{3,2,1,0:T(8,128)(2,1)}, bf16[3,4,128,128]{3,2,1,0:T(8,128)(2,1)S(1)}, u32[]{:S(2)}) copy-start(bf16[3,4,128,128]{3,2,1,0:T(8,128)(2,1)S(1)} %copy.38) | copy-start | bytes 1179652
  18.3 0.8 %copy-start.4 = (bf16[6,24,128]{2,1,0:T(8,128)(2,1)S(1)}, bf16[6,24,128]{2,1,0:T(8,128)(2,1)}, u32[]{:S(2)}) copy-start(bf16[6,24,128]{2,1,0:T(8,128)(2,1)} %param.18) | copy-start | bytes 110596
  19.1 0.7 %copy-start.6 = (f32[6,6,1]{1,0,2:T(8,128)S(1)}, f32[6,6,1]{1,0,2:T(8,128)}, u32[]{:S(2)}) copy-start(f32[6,6,1]{1,0,2:T(8,128)} %constant.18) | copy-start | bytes 436
  19.3 1.1 %copy-start.9 = (f32[128]{0:T(128)S(1)}, f32[128]{0:T(128)}, u32[]{:S(2)}) copy-start(f32[128]{0:T(128)} %param.19) | copy-start | bytes 1540
  19.8 1.0 %copy-start.7 = (s32[1,224]{1,0:T(1,128)S(1)}, s32[1,224]{1,0:T(1,128)}, u32[]{:S(2)}) copy-start(s32[1,224]{1,0:T(1,128)} %param.21) | copy-start | bytes 2692
  20.4 1.9 %copy-start.8 = (f32[512]{0:T(512)S(1)}, f32[512]{0:T(512)}, u32[]{:S(2)}) copy-start(f32[512]{0:T(512)} %param.22) | copy-start | bytes 6148
  20.5 2.7 %copy-start.1 = (f32[6,128,128]{2,1,0:T(8,128)}, f32[6,128,128]{2,1,0:T(8,128)S(1)}, u32[]{:S(2)}) copy-start(f32[6,128,128]{2,1,0:T(8,128)S(1)} %fusion.13.stress_ref) | copy-start | bytes 1179652

commit v11 on v10

--- a/solution.py
+++ b/solution.py
@@ -195,7 +195,7 @@
     added[...] = jnp.zeros(added.shape, added.dtype)
     for c in range(acc.shape[0]):
         acc[c] = jnp.dot(
-            own_ref[...], stress_ref[c], precision=lax.Precision.HIGHEST,
+            own_ref[...], stress_ref[c], precision=lax.Precision.HIGH,
             preferred_element_type=jnp.float32,
         )
     for j, (k, lo, hi, row) in enumerate(SEND_PIECES):
@@ -213,7 +213,7 @@
         pl.when(exists(-ds, -dg))(take)
     for c in range(acc.shape[0]):
         total = acc[c] + jnp.dot(
-            spread_ref[...], added[c], precision=lax.Precision.HIGHEST,
+            spread_ref[...], added[c], precision=lax.Precision.HIGH,
             preferred_element_type=jnp.float32,
         )
         out_ref[c] = total.astype(out_ref.dtype)

time: 42.6 us -> 41.3 us (0.969)
  Pallas kernels: 27.5 us -> 26.3 us
    pallas_call x1, Pallas kernels: 16 us -> 14.8 us  [exchange_faces(): pl.pallas_call(functools.partial(face_kernel, n_sub, n_grp), out_shape=ja...]
where the time goes in v11:
time: 41.3 us; the launch traced here: 41 us
  Pallas kernels  26.3 us (64%)
  local copies, waits for them, and re-layouts  6.76 us (16%)
  matrix products  4.82 us (12%)
  other arithmetic  2.24 us (5%)
  between operations  0.86 us (2%)
    pallas_call x1, Pallas kernels, exchange_faces(): pl.pallas_call(functools.partial(face_kernel, n_sub, n_grp), out_shape=ja...  14.8 us
    pallas_call x1, Pallas kernels, fetch_corners(): pl.pallas_call(functools.partial(coarse_kernel, n_sub, n_grp), out_shape=...  11.5 us
    unnamed x24, local copies, waits for them, and re-layouts  2.9 us
    convert_element_type x3, local copies, waits for them, and re-layouts, shards(): force.reshape(3 * node_count, load_cases).astype(jnp.float32) - correction  2.05 us
    dot_general x1, matrix products, shards(): jnp.einsum('re,cel->crl', jnp.dot(picker, incidence), stress, precision=l...  1.27 us
    dot_general x1, matrix products, shards(): jnp.dot(coupling.astype(jnp.float32), corner_vals, precision=lax.Precisio...  1.12 us
    mul x1, other arithmetic, shards(): spread = picker.T * inverse_volume[:, None]  0.94 us
    mul x1, other arithmetic, shards(): own = incidence * inverse_volume[:, None]  0.85 us

profile of v11, /device:TPU:121, one launch (start us, length us, event | category | flops | bytes accessed | tf_op | source)
XLA Modules:
  0.0 41.0 jit_solution(5052810261493825704)
XLA Ops:
  0.6 0.0 copy-start
  0.6 1.4 %copy.34 = f32[512,3,128]{2,1,0:T(4,128)S(1)} copy(bf16[512,3,128]{2,0,1:T(8,128)(2,1)} %param.15) | data formatting | bytes 1179648 | tf_op jit(solution)/shard_map/convert_element_type | solution.py:282
  2.1 0.4 reshape.57
  2.4 0.0 copy-start.3
  2.5 0.3 copy.35
  2.7 11.5 %shard_map.131 = f32[24,128]{1,0:T(8,128)} custom-call(f32[24,128]{1,0:T(8,128)} %block_ref.1, s32[1,24]{1,0:T(1,128)} %idx_ref.1), custom_call_target="tpu_custom_call" | custom-call | tf_op jit(solution)/shard_map/pallas_call | solution.py:225
  14.2 1.1 %fusion = bf16[1536,128]{0,1:T(8,128)(2,1)S(1)} fusion(f32[1536,128]{0,1:T(8,128)S(1)} %copy.35, f32[24,128]{1,0:T(8,128)} %shard_map.131, bf16[1536,24]{0,1:T(8,128)(2,1)S(1)} %copy-done.3), kind=kOutput, calls=%fused_computation.1 | convolution fusion | flops 28704768 | bytes 1265664 | tf_op jit(solution)/shard_map/dot_general | solution.py:280
  15.4 0.1 iota_compare_fusion.5
  15.5 0.5 %fusion.8 = bf16[4,384,128]{1,2,0:T(8,128)(2,1)S(1)} fusion(bf16[4,384,384]{2,1,0:T(8,128)(2,1)S(1)} %copy-done, bf16[16,4,8,384]{3,2,1,0:T(8,128)(2,1)S(1)} %bitcast.50, pred[4,384]{1,0:T(4,128)(4,1)S(1)} %iota_compare_fusion.5), kind=kOutput, calls=%fused_computation.12 | convolution fusion | flops 151584768 | bytes 1967616 | tf_op jit(solution)/shard_map/prc,pcl->prl/dot_general | solution.py:286
  16.0 0.2 copy.37
  16.2 0.1 copy.38
  16.3 0.0 copy-start.2
  16.3 0.3 copy-done.5
  16.7 0.1 copy.39
  16.8 0.1 eq.50
  16.9 0.8 %fusion.4 = bf16[1024,3,128]{2,0,1:T(8,128)(2,1)S(1)} fusion(bf16[3,512,128]{2,1,0:T(8,128)(2,1)S(1)} %bitcast.51, s32[1024]{0:T(1024)S(1)} %eq.50), kind=kOutput, calls=%fused_computation.7 | convolution fusion | flops 403570688 | bytes 1183744 | tf_op jit(solution)/shard_map/xn,cnl->xcl/dot_general | solution.py:296
  17.6 0.7 %copy.40 = bf16[1024,3,128]{2,1,0:T(4,128)(2,1)S(1)} copy(bf16[1024,3,128]{2,0,1:T(8,128)(2,1)S(1)} %fusion.4) | data formatting | bytes 1572864 | tf_op jit(solution)/shard_map/convert_element_type | solution.py:297
  18.3 0.6 %reshape.56 = bf16[128,24,128]{2,1,0:T(8,128)(2,1)S(1)} reshape(bf16[1024,3,128]{2,1,0:T(4,128)(2,1)S(1)} %copy.40) | data formatting | bytes 1572864 | tf_op jit(solution)/shard_map/reshape | solution.py:297
  19.0 0.1 copy-done.4
  19.1 0.2 copy.41
  19.3 0.0 copy-start.9
  19.3 0.4 convolution_bitcast_fusion.2
  19.6 0.1 copy-done.6
  19.8 0.6 %fusion.18 = f32[128,128,6]{1,2,0:T(8,128)S(1)} fusion(f32[128,6,128]{2,1,0:T(8,128)S(1)} %convolution_bitcast_fusion.2, f32[6,6,1]{1,0,2:T(8,128)S(1)} %copy-done.6), kind=kOutput, calls=%fused_computation.30 | convolution fusion | flops 7077888 | bytes 786576 | tf_op jit(solution)/shard_map/ik,ekl->iel/dot_general | solution.py:300
  20.4 0.1 fusion.13.stress_ref
  20.5 0.2 convert_reduce_fusion
  20.8 0.3 convolution_bitcast_fusion.3
  21.0 1.3 %convolution_bitcast_fusion.1.send_ref = f32[6,224,128]{2,1,0:T(8,128)} fusion(f32[6,128,128]{2,1,0:T(8,128)S(1)} %fusion.13.stress_ref, f32[224,128,1]{1,0,2:T(8,128)S(1)} %convolution_bitcast_fusion.3), kind=kOutput, calls=%fused_computation.9 | convolution fusion | flops 132120576 | bytes 1196032 | tf_op jit(solution)/shard_map/re,cel->crl/dot_general | solution.py:307
  22.3 0.8 %broadcast_multiply_fusion.own_ref = f32[512,128]{1,0:T(8,128)} fusion(f32[512,128]{1,0:T(8,128)S(1)} %convert_reduce_fusion, f32[512]{0:T(512)S(1)} %broadcast_divide_fusion), kind=kLoop, calls=%fused_computation.25 | loop fusion | flops 65536 | bytes 526336 | tf_op jit(solution)/shard_map/mul | solution.py:311
  23.2 0.9 %fusion.11.spread_ref = f32[512,224]{1,0:T(8,128)} fusion(f32[512]{0:T(512)S(1)} %broadcast_divide_fusion, s32[224]{0:T(256)S(1)} %bitcast.55), kind=kLoop, calls=%fused_computation.18 | loop fusion | flops 229376 | bytes 461696 | tf_op jit(solution)/shard_map/mul | solution.py:312
  24.1 14.8 %shard_map.132 = bf16[6,512,128]{2,1,0:T(8,128)(2,1)} custom-call(f32[6,224,128]{2,1,0:T(8,128)} %convolution_bitcast_fusion.1.send_ref, f32[6,128,128]{2,1,0:T(8,128)} %copy-done.1, f32[512,128]{1,0:T(8,128)} %broadcast_multiply_fusion.own_ref, f32[512,224]{1,0:T(8,128)} %fusion.11.spread_ref), custom_call_target="tpu_custom_call" | custom-call | tf_op jit(solution)/shard_map/pallas_call | solution.py:244
  38.9 2.1 %copy.50 = bf16[512,6,128]{2,0,1:T(8,128)(2,1)} copy(bf16[512,6,128]{2,0,1:T(8,128)(2,1)} %bitcast.48) | data formatting | bytes 1572864
  (17 shorter events, 0.0 us)
Async XLA Ops:
  0.6 14.8 %copy-start = (bf16[4,384,384]{2,1,0:T(8,128)(2,1)S(1)}, bf16[4,384,384]{2,1,0:T(8,128)(2,1)}, u32[]{:S(2)}) copy-start(bf16[4,384,384]{2,1,0:T(8,128)(2,1)} %param.16) | copy-start | bytes 3538948
  2.4 11.8 %copy-start.3 = (bf16[1536,24]{0,1:T(8,128)(2,1)S(1)}, bf16[1536,24]{0,1:T(8,128)(2,1)}, u32[]{:S(2)}) copy-start(bf16[1536,24]{0,1:T(8,128)(2,1)} %param.14) | copy-start | bytes 221188
  2.5 12.9 %copy-start.10 = (s32[1,4]{1,0:T(1,128)S(1)}, s32[1,4]{1,0:T(1,128)}, u32[]{:S(2)}) copy-start(s32[1,4]{1,0:T(1,128)} %param.17) | copy-start | bytes 52
  16.0 0.7 %copy-start.5 = (s32[8,128]{1,0:T(8,128)S(1)}, s32[8,128]{1,0:T(8,128)}, u32[]{:S(2)}) copy-start(s32[8,128]{1,0:T(8,128)} %param.20) | copy-start | bytes 12292
  16.3 1.3 %copy-start.2 = (bf16[3,4,128,128]{3,2,1,0:T(8,128)(2,1)}, bf16[3,4,128,128]{3,2,1,0:T(8,128)(2,1)S(1)}, u32[]{:S(2)}) copy-start(bf16[3,4,128,128]{3,2,1,0:T(8,128)(2,1)S(1)} %copy.38) | copy-start | bytes 1179652
  18.3 0.8 %copy-start.4 = (bf16[6,24,128]{2,1,0:T(8,128)(2,1)S(1)}, bf16[6,24,128]{2,1,0:T(8,128)(2,1)}, u32[]{:S(2)}) copy-start(bf16[6,24,128]{2,1,0:T(8,128)(2,1)} %param.18) | copy-start | bytes 110596
  19.1 0.7 %copy-start.6 = (f32[6,6,1]{1,0,2:T(8,128)S(1)}, f32[6,6,1]{1,0,2:T(8,128)}, u32[]{:S(2)}) copy-start(f32[6,6,1]{1,0,2:T(8,128)} %constant.18) | copy-start | bytes 436
  19.3 1.1 %copy-start.9 = (f32[128]{0:T(128)S(1)}, f32[128]{0:T(128)}, u32[]{:S(2)}) copy-start(f32[128]{0:T(128)} %param.19) | copy-start | bytes 1540
  19.8 1.0 %copy-start.7 = (s32[1,224]{1,0:T(1,128)S(1)}, s32[1,224]{1,0:T(1,128)}, u32[]{:S(2)}) copy-start(s32[1,224]{1,0:T(1,128)} %param.21) | copy-start | bytes 2692
  20.4 1.9 %copy-start.8 = (f32[512]{0:T(512)S(1)}, f32[512]{0:T(512)}, u32[]{:S(2)}) copy-start(f32[512]{0:T(512)} %param.22) | copy-start | bytes 6148
  20.5 2.7 %copy-start.1 = (f32[6,128,128]{2,1,0:T(8,128)}, f32[6,128,128]{2,1,0:T(8,128)S(1)}, u32[]{:S(2)}) copy-start(f32[6,128,128]{2,1,0:T(8,128)S(1)} %fusion.13.stress_ref) | copy-start | bytes 1179652

commit v12 on v11

--- a/solution.py
+++ b/solution.py
@@ -297,7 +297,7 @@
     element = element.astype(jnp.bfloat16).reshape(elem_count, 24, load_cases)
     strain = jnp.einsum("ije,ejl->eil", strain_disp, element, preferred_element_type=jnp.float32)
     stress = (
-        jnp.einsum("ik,ekl->iel", iso_matrix(), strain, precision=lax.Precision.HIGHEST)
+        jnp.einsum("ik,ekl->iel", iso_matrix(), strain, precision=lax.Precision.HIGH)
         * modulus[None, :, None]
     )
     incidence = jnp.sum(

time: 41.3 us -> 41.1 us (level)
  no operation moved by 1% of the time
where the time goes in v12:
time: 41.1 us; the launch traced here: 40.7 us
  Pallas kernels  26.3 us (64%)
  local copies, waits for them, and re-layouts  6.76 us (16%)
  matrix products  4.61 us (11%)
  other arithmetic  2.24 us (5%)
  between operations  0.86 us (2%)
    pallas_call x1, Pallas kernels, exchange_faces(): pl.pallas_call(functools.partial(face_kernel, n_sub, n_grp), out_shape=ja...  14.8 us
    pallas_call x1, Pallas kernels, fetch_corners(): pl.pallas_call(functools.partial(coarse_kernel, n_sub, n_grp), out_shape=...  11.5 us
    unnamed x24, local copies, waits for them, and re-layouts  2.9 us
    convert_element_type x3, local copies, waits for them, and re-layouts, shards(): force.reshape(3 * node_count, load_cases).astype(jnp.float32) - correction  2.05 us
    dot_general x1, matrix products, shards(): jnp.einsum('re,cel->crl', jnp.dot(picker, incidence), stress, precision=l...  1.27 us
    dot_general x1, matrix products, shards(): jnp.dot(coupling.astype(jnp.float32), corner_vals, precision=lax.Precisio...  1.12 us
    mul x1, other arithmetic, shards(): spread = picker.T * inverse_volume[:, None]  0.94 us
    mul x1, other arithmetic, shards(): own = incidence * inverse_volume[:, None]  0.85 us

profile of v12, /device:TPU:121, one launch (start us, length us, event | category | flops | bytes accessed | tf_op | source)
XLA Modules:
  0.0 40.7 jit_solution(14614097908972400707)
XLA Ops:
  0.6 0.0 copy-start
  0.6 1.4 %copy.34 = f32[512,3,128]{2,1,0:T(4,128)S(1)} copy(bf16[512,3,128]{2,0,1:T(8,128)(2,1)} %param.15) | data formatting | bytes 1179648 | tf_op jit(solution)/shard_map/convert_element_type | solution.py:282
  2.1 0.4 reshape.57
  2.4 0.0 copy-start.3
  2.5 0.3 copy.35
  2.7 11.5 %shard_map.131 = f32[24,128]{1,0:T(8,128)} custom-call(f32[24,128]{1,0:T(8,128)} %block_ref.1, s32[1,24]{1,0:T(1,128)} %idx_ref.1), custom_call_target="tpu_custom_call" | custom-call | tf_op jit(solution)/shard_map/pallas_call | solution.py:225
  14.2 1.1 %fusion = bf16[1536,128]{0,1:T(8,128)(2,1)S(1)} fusion(f32[1536,128]{0,1:T(8,128)S(1)} %copy.35, f32[24,128]{1,0:T(8,128)} %shard_map.131, bf16[1536,24]{0,1:T(8,128)(2,1)S(1)} %copy-done.3), kind=kOutput, calls=%fused_computation.1 | convolution fusion | flops 28704768 | bytes 1265664 | tf_op jit(solution)/shard_map/dot_general | solution.py:280
  15.4 0.1 iota_compare_fusion.5
  15.5 0.5 %fusion.8 = bf16[4,384,128]{1,2,0:T(8,128)(2,1)S(1)} fusion(bf16[4,384,384]{2,1,0:T(8,128)(2,1)S(1)} %copy-done, bf16[16,4,8,384]{3,2,1,0:T(8,128)(2,1)S(1)} %bitcast.50, pred[4,384]{1,0:T(4,128)(4,1)S(1)} %iota_compare_fusion.5), kind=kOutput, calls=%fused_computation.12 | convolution fusion | flops 151584768 | bytes 1967616 | tf_op jit(solution)/shard_map/prc,pcl->prl/dot_general | solution.py:286
  16.0 0.2 copy.37
  16.2 0.1 copy.38
  16.3 0.0 copy-start.2
  16.3 0.3 copy-done.5
  16.7 0.1 copy.39
  16.8 0.1 eq.50
  16.9 0.8 %fusion.4 = bf16[1024,3,128]{2,0,1:T(8,128)(2,1)S(1)} fusion(bf16[3,512,128]{2,1,0:T(8,128)(2,1)S(1)} %bitcast.51, s32[1024]{0:T(1024)S(1)} %eq.50), kind=kOutput, calls=%fused_computation.7 | convolution fusion | flops 403570688 | bytes 1183744 | tf_op jit(solution)/shard_map/xn,cnl->xcl/dot_general | solution.py:296
  17.6 0.7 %copy.40 = bf16[1024,3,128]{2,1,0:T(4,128)(2,1)S(1)} copy(bf16[1024,3,128]{2,0,1:T(8,128)(2,1)S(1)} %fusion.4) | data formatting | bytes 1572864 | tf_op jit(solution)/shard_map/convert_element_type | solution.py:297
  18.3 0.6 %reshape.56 = bf16[128,24,128]{2,1,0:T(8,128)(2,1)S(1)} reshape(bf16[1024,3,128]{2,1,0:T(4,128)(2,1)S(1)} %copy.40) | data formatting | bytes 1572864 | tf_op jit(solution)/shard_map/reshape | solution.py:297
  19.0 0.1 copy-done.4
  19.1 0.2 copy.41
  19.3 0.0 copy-start.9
  19.3 0.4 convolution_bitcast_fusion.2
  19.6 0.1 copy-done.6
  19.8 0.3 fusion.18
  20.2 0.1 fusion.13.stress_ref
  20.3 0.2 convert_reduce_fusion
  20.5 0.3 convolution_bitcast_fusion.3
  20.8 1.3 %convolution_bitcast_fusion.1.send_ref = f32[6,224,128]{2,1,0:T(8,128)} fusion(f32[6,128,128]{2,1,0:T(8,128)S(1)} %fusion.13.stress_ref, f32[224,128,1]{1,0,2:T(8,128)S(1)} %convolution_bitcast_fusion.3), kind=kOutput, calls=%fused_computation.9 | convolution fusion | flops 132120576 | bytes 1196032 | tf_op jit(solution)/shard_map/re,cel->crl/dot_general | solution.py:307
  22.1 0.8 %broadcast_multiply_fusion.own_ref = f32[512,128]{1,0:T(8,128)} fusion(f32[512,128]{1,0:T(8,128)S(1)} %convert_reduce_fusion, f32[512]{0:T(512)S(1)} %broadcast_divide_fusion), kind=kLoop, calls=%fused_computation.25 | loop fusion | flops 65536 | bytes 526336 | tf_op jit(solution)/shard_map/mul | solution.py:311
  22.9 0.9 %fusion.11.spread_ref = f32[512,224]{1,0:T(8,128)} fusion(f32[512]{0:T(512)S(1)} %broadcast_divide_fusion, s32[224]{0:T(256)S(1)} %bitcast.55), kind=kLoop, calls=%fused_computation.18 | loop fusion | flops 229376 | bytes 461696 | tf_op jit(solution)/shard_map/mul | solution.py:312
  23.9 14.8 %shard_map.132 = bf16[6,512,128]{2,1,0:T(8,128)(2,1)} custom-call(f32[6,224,128]{2,1,0:T(8,128)} %convolution_bitcast_fusion.1.send_ref, f32[6,128,128]{2,1,0:T(8,128)} %copy-done.1, f32[512,128]{1,0:T(8,128)} %broadcast_multiply_fusion.own_ref, f32[512,224]{1,0:T(8,128)} %fusion.11.spread_ref), custom_call_target="tpu_custom_call" | custom-call | tf_op jit(solution)/shard_map/pallas_call | solution.py:244
  38.7 2.1 %copy.50 = bf16[512,6,128]{2,0,1:T(8,128)(2,1)} copy(bf16[512,6,128]{2,0,1:T(8,128)(2,1)} %bitcast.48) | data formatting | bytes 1572864
  (17 shorter events, 0.0 us)
Async XLA Ops:
  0.6 14.8 %copy-start = (bf16[4,384,384]{2,1,0:T(8,128)(2,1)S(1)}, bf16[4,384,384]{2,1,0:T(8,128)(2,1)}, u32[]{:S(2)}) copy-start(bf16[4,384,384]{2,1,0:T(8,128)(2,1)} %param.16) | copy-start | bytes 3538948
  2.4 11.8 %copy-start.3 = (bf16[1536,24]{0,1:T(8,128)(2,1)S(1)}, bf16[1536,24]{0,1:T(8,128)(2,1)}, u32[]{:S(2)}) copy-start(bf16[1536,24]{0,1:T(8,128)(2,1)} %param.14) | copy-start | bytes 221188
  2.5 12.9 %copy-start.10 = (s32[1,4]{1,0:T(1,128)S(1)}, s32[1,4]{1,0:T(1,128)}, u32[]{:S(2)}) copy-start(s32[1,4]{1,0:T(1,128)} %param.17) | copy-start | bytes 52
  16.0 0.7 %copy-start.5 = (s32[8,128]{1,0:T(8,128)S(1)}, s32[8,128]{1,0:T(8,128)}, u32[]{:S(2)}) copy-start(s32[8,128]{1,0:T(8,128)} %param.20) | copy-start | bytes 12292
  16.3 1.3 %copy-start.2 = (bf16[3,4,128,128]{3,2,1,0:T(8,128)(2,1)}, bf16[3,4,128,128]{3,2,1,0:T(8,128)(2,1)S(1)}, u32[]{:S(2)}) copy-start(bf16[3,4,128,128]{3,2,1,0:T(8,128)(2,1)S(1)} %copy.38) | copy-start | bytes 1179652
  18.3 0.8 %copy-start.4 = (bf16[6,24,128]{2,1,0:T(8,128)(2,1)S(1)}, bf16[6,24,128]{2,1,0:T(8,128)(2,1)}, u32[]{:S(2)}) copy-start(bf16[6,24,128]{2,1,0:T(8,128)(2,1)} %param.18) | copy-start | bytes 110596
  19.1 0.7 %copy-start.6 = (f32[6,6,1]{1,0,2:T(8,128)S(1)}, f32[6,6,1]{1,0,2:T(8,128)}, u32[]{:S(2)}) copy-start(f32[6,6,1]{1,0,2:T(8,128)} %constant.18) | copy-start | bytes 436
  19.3 0.9 %copy-start.9 = (f32[128]{0:T(128)S(1)}, f32[128]{0:T(128)}, u32[]{:S(2)}) copy-start(f32[128]{0:T(128)} %param.19) | copy-start | bytes 1540
  19.8 0.8 %copy-start.7 = (s32[1,224]{1,0:T(1,128)S(1)}, s32[1,224]{1,0:T(1,128)}, u32[]{:S(2)}) copy-start(s32[1,224]{1,0:T(1,128)} %param.21) | copy-start | bytes 2692
  20.1 1.9 %copy-start.8 = (f32[512]{0:T(512)S(1)}, f32[512]{0:T(512)}, u32[]{:S(2)}) copy-start(f32[512]{0:T(512)} %param.22) | copy-start | bytes 6148
  20.3 2.7 %copy-start.1 = (f32[6,128,128]{2,1,0:T(8,128)}, f32[6,128,128]{2,1,0:T(8,128)S(1)}, u32[]{:S(2)}) copy-start(f32[6,128,128]{2,1,0:T(8,128)S(1)} %fusion.13.stress_ref) | copy-start | bytes 1179652

commit v13 on v12

--- a/solution.py
+++ b/solution.py
@@ -149,8 +149,9 @@
 
 
 def face_kernel(
-    n_sub, n_grp, send_ref, stress_ref, own_ref, spread_ref, out_ref, buf, added, acc, send_sem, recv_sem
+    n_sub, n_grp, send_ref, stress_ref, scaled_ref, out_ref, buf, added, acc, send_sem, recv_sem
 ):
+    width = stress_ref.shape[1]
     s = lax.axis_index("sub")
     g = lax.axis_index("grp")
     barrier = pltpu.get_barrier_semaphore()
@@ -195,7 +196,7 @@
     added[...] = jnp.zeros(added.shape, added.dtype)
     for c in range(acc.shape[0]):
         acc[c] = jnp.dot(
-            own_ref[...], stress_ref[c], precision=lax.Precision.HIGH,
+            scaled_ref[:, :width], stress_ref[c], precision=lax.Precision.HIGH,
             preferred_element_type=jnp.float32,
         )
     for j, (k, lo, hi, row) in enumerate(SEND_PIECES):
@@ -213,7 +214,7 @@
         pl.when(exists(-ds, -dg))(take)
     for c in range(acc.shape[0]):
         total = acc[c] + jnp.dot(
-            spread_ref[...], added[c], precision=lax.Precision.HIGH,
+            scaled_ref[:, width:], added[c], precision=lax.Precision.HIGH,
             preferred_element_type=jnp.float32,
         )
         out_ref[c] = total.astype(out_ref.dtype)
@@ -239,12 +240,12 @@
     )(block, corner_idx)
 
 
-def exchange_faces(send, stress, own, spread, n_sub, n_grp):
-    parts, nodes = stress.shape[0], own.shape[0]
+def exchange_faces(send, stress, scaled, n_sub, n_grp):
+    parts, nodes = stress.shape[0], scaled.shape[0]
     return pl.pallas_call(
         functools.partial(face_kernel, n_sub, n_grp),
         out_shape=jax.ShapeDtypeStruct((parts, nodes, send.shape[2]), jnp.bfloat16),
-        in_specs=[pl.BlockSpec(memory_space=pltpu.VMEM)] * 4,
+        in_specs=[pl.BlockSpec(memory_space=pltpu.VMEM)] * 3,
         out_specs=pl.BlockSpec(memory_space=pltpu.VMEM),
         scratch_shapes=[
             pltpu.VMEM((send.shape[0], int(SLOT_START[-1]), send.shape[2]), send.dtype),
@@ -254,7 +255,7 @@
             pltpu.SemaphoreType.DMA((len(SEND_PIECES),)),
         ],
         compiler_params=pltpu.CompilerParams(collective_id=1, has_side_effects=True),
-    )(send, stress, own, spread)
+    )(send, stress, scaled)
 
 
 def shards(
@@ -308,9 +309,8 @@
         "re,cel->crl", jnp.dot(picker, incidence), stress, precision=lax.Precision.HIGH
     )
     inverse_volume = 1.0 / nodal_volume
-    own = incidence * inverse_volume[:, None]
-    spread = picker.T * inverse_volume[:, None]
-    stress_out = exchange_faces(send, stress, own, spread, n_sub, n_grp).transpose(1, 0, 2)
+    scaled = jnp.concatenate([incidence, picker.T], axis=1) * inverse_volume[:, None]
+    stress_out = exchange_faces(send, stress, scaled, n_sub, n_grp).transpose(1, 0, 2)
     return (by_component.transpose(1, 0, 2), stress_out)
 
 

time: 41.1 us -> 40.5 us (0.985)
  other arithmetic: 2.24 us -> 1.51 us
    mul x2 -> x1, other arithmetic: 1.79 us -> 1.02 us  [shards(): jnp.concatenate([incidence, picker.T], axis=1) * inverse_volume[:, None]]
where the time goes in v13:
time: 40.5 us; the launch traced here: 40.1 us
  Pallas kernels  26.3 us (65%)
  local copies, waits for them, and re-layouts  6.76 us (17%)
  matrix products  4.63 us (11%)
  other arithmetic  1.51 us (4%)
  between operations  0.89 us (2%)
    pallas_call x1, Pallas kernels, exchange_faces(): pl.pallas_call(functools.partial(face_kernel, n_sub, n_grp), out_shape=ja...  14.8 us
    pallas_call x1, Pallas kernels, fetch_corners(): pl.pallas_call(functools.partial(coarse_kernel, n_sub, n_grp), out_shape=...  11.5 us
    unnamed x24, local copies, waits for them, and re-layouts  2.9 us
    convert_element_type x3, local copies, waits for them, and re-layouts, shards(): force.reshape(3 * node_count, load_cases).astype(jnp.float32) - correction  2.05 us
    dot_general x1, matrix products, shards(): jnp.einsum('re,cel->crl', jnp.dot(picker, incidence), stress, precision=l...  1.29 us
    dot_general x1, matrix products, shards(): jnp.dot(coupling.astype(jnp.float32), corner_vals, precision=lax.Precisio...  1.12 us
    mul x1, other arithmetic, shards(): jnp.concatenate([incidence, picker.T], axis=1) * inverse_volume[:, None]  1.02 us

profile of v13, /device:TPU:121, one launch (start us, length us, event | category | flops | bytes accessed | tf_op | source)
XLA Modules:
  0.0 40.1 jit_solution(5164858951145738334)
XLA Ops:
  0.6 0.0 copy-start
  0.6 1.4 %copy.34 = f32[512,3,128]{2,1,0:T(4,128)S(1)} copy(bf16[512,3,128]{2,0,1:T(8,128)(2,1)} %param.15) | data formatting | bytes 1179648 | tf_op jit(solution)/shard_map/convert_element_type | solution.py:283
  2.1 0.4 reshape.57
  2.4 0.0 copy-start.3
  2.5 0.0 copy-start.10
  2.5 0.3 copy.35
  2.7 11.5 %shard_map.131 = f32[24,128]{1,0:T(8,128)} custom-call(f32[24,128]{1,0:T(8,128)} %block_ref.1, s32[1,24]{1,0:T(1,128)} %idx_ref.1), custom_call_target="tpu_custom_call" | custom-call | tf_op jit(solution)/shard_map/pallas_call | solution.py:226
  14.2 1.1 %fusion = bf16[1536,128]{0,1:T(8,128)(2,1)S(1)} fusion(f32[1536,128]{0,1:T(8,128)S(1)} %copy.35, f32[24,128]{1,0:T(8,128)} %shard_map.131, bf16[1536,24]{0,1:T(8,128)(2,1)S(1)} %copy-done.3), kind=kOutput, calls=%fused_computation.1 | convolution fusion | flops 28704768 | bytes 1265664 | tf_op jit(solution)/shard_map/dot_general | solution.py:281
  15.4 0.1 iota_compare_fusion.5
  15.5 0.5 %fusion.8 = bf16[4,384,128]{1,2,0:T(8,128)(2,1)S(1)} fusion(bf16[4,384,384]{2,1,0:T(8,128)(2,1)S(1)} %copy-done, bf16[16,4,8,384]{3,2,1,0:T(8,128)(2,1)S(1)} %bitcast.50, pred[4,384]{1,0:T(4,128)(4,1)S(1)} %iota_compare_fusion.5), kind=kOutput, calls=%fused_computation.12 | convolution fusion | flops 151584768 | bytes 1967616 | tf_op jit(solution)/shard_map/prc,pcl->prl/dot_general | solution.py:287
  16.0 0.2 copy.37
  16.2 0.1 copy.38
  16.3 0.0 copy-start.2
  16.3 0.3 copy-done.5
  16.7 0.1 copy.39
  16.8 0.1 eq.50
  16.9 0.8 %fusion.4 = bf16[1024,3,128]{2,0,1:T(8,128)(2,1)S(1)} fusion(bf16[3,512,128]{2,1,0:T(8,128)(2,1)S(1)} %bitcast.51, s32[1024]{0:T(1024)S(1)} %eq.50), kind=kOutput, calls=%fused_computation.7 | convolution fusion | flops 403570688 | bytes 1183744 | tf_op jit(solution)/shard_map/xn,cnl->xcl/dot_general | solution.py:297
  17.6 0.7 %copy.40 = bf16[1024,3,128]{2,1,0:T(4,128)(2,1)S(1)} copy(bf16[1024,3,128]{2,0,1:T(8,128)(2,1)S(1)} %fusion.4) | data formatting | bytes 1572864 | tf_op jit(solution)/shard_map/convert_element_type | solution.py:298
  18.3 0.6 %reshape.56 = bf16[128,24,128]{2,1,0:T(8,128)(2,1)S(1)} reshape(bf16[1024,3,128]{2,1,0:T(4,128)(2,1)S(1)} %copy.40) | data formatting | bytes 1572864 | tf_op jit(solution)/shard_map/reshape | solution.py:298
  19.0 0.1 copy-done.4
  19.1 0.2 copy.41
  19.3 0.0 copy-start.9
  19.3 0.4 convolution_bitcast_fusion.2
  19.6 0.1 copy-done.6
  19.8 0.3 fusion.18
  20.1 0.1 fusion.13.stress_ref
  20.3 0.2 convert_reduce_fusion
  20.5 0.3 convolution_bitcast_fusion.3
  20.8 1.3 %convolution_bitcast_fusion.1.send_ref = f32[6,224,128]{2,1,0:T(8,128)} fusion(f32[6,128,128]{2,1,0:T(8,128)S(1)} %fusion.13.stress_ref, f32[224,128,1]{1,0,2:T(8,128)S(1)} %convolution_bitcast_fusion.3), kind=kOutput, calls=%fused_computation.9 | convolution fusion | flops 132120576 | bytes 1196032 | tf_op jit(solution)/shard_map/re,cel->crl/dot_general | solution.py:308
  22.2 1.0 %maximum_multiply_fusion.scaled_ref = f32[512,352]{1,0:T(8,128)} fusion(f32[512,224]{1,0:T(8,128)S(1)} %fusion.11, f32[512,128]{1,0:T(8,128)S(1)} %convert_reduce_fusion, f32[512]{0:T(512)S(1)} %broadcast_divide_fusion), kind=kLoop, calls=%fused_computation.17 | loop fusion | flops 360448 | bytes 1443840 | tf_op jit(solution)/shard_map/mul | solution.py:312
  23.2 14.8 %shard_map.132 = bf16[6,512,128]{2,1,0:T(8,128)(2,1)} custom-call(f32[6,224,128]{2,1,0:T(8,128)} %convolution_bitcast_fusion.1.send_ref, f32[6,128,128]{2,1,0:T(8,128)} %copy-done.1, f32[512,352]{1,0:T(8,128)} %maximum_multiply_fusion.scaled_ref), custom_call_target="tpu_custom_call" | custom-call | tf_op jit(solution)/shard_map/pallas_call | solution.py:245
  38.0 2.1 %copy.50 = bf16[512,6,128]{2,0,1:T(8,128)(2,1)} copy(bf16[512,6,128]{2,0,1:T(8,128)(2,1)} %bitcast.48) | data formatting | bytes 1572864
  (17 shorter events, 0.1 us)
Async XLA Ops:
  0.6 14.8 %copy-start = (bf16[4,384,384]{2,1,0:T(8,128)(2,1)S(1)}, bf16[4,384,384]{2,1,0:T(8,128)(2,1)}, u32[]{:S(2)}) copy-start(bf16[4,384,384]{2,1,0:T(8,128)(2,1)} %param.16) | copy-start | bytes 3538948
  2.4 11.8 %copy-start.3 = (bf16[1536,24]{0,1:T(8,128)(2,1)S(1)}, bf16[1536,24]{0,1:T(8,128)(2,1)}, u32[]{:S(2)}) copy-start(bf16[1536,24]{0,1:T(8,128)(2,1)} %param.14) | copy-start | bytes 221188
  2.5 12.9 %copy-start.10 = (s32[1,4]{1,0:T(1,128)S(1)}, s32[1,4]{1,0:T(1,128)}, u32[]{:S(2)}) copy-start(s32[1,4]{1,0:T(1,128)} %param.17) | copy-start | bytes 52
  16.0 0.7 %copy-start.5 = (s32[8,128]{1,0:T(8,128)S(1)}, s32[8,128]{1,0:T(8,128)}, u32[]{:S(2)}) copy-start(s32[8,128]{1,0:T(8,128)} %param.20) | copy-start | bytes 12292
  16.3 1.3 %copy-start.2 = (bf16[3,4,128,128]{3,2,1,0:T(8,128)(2,1)}, bf16[3,4,128,128]{3,2,1,0:T(8,128)(2,1)S(1)}, u32[]{:S(2)}) copy-start(bf16[3,4,128,128]{3,2,1,0:T(8,128)(2,1)S(1)} %copy.38) | copy-start | bytes 1179652
  18.3 0.8 %copy-start.4 = (bf16[6,24,128]{2,1,0:T(8,128)(2,1)S(1)}, bf16[6,24,128]{2,1,0:T(8,128)(2,1)}, u32[]{:S(2)}) copy-start(bf16[6,24,128]{2,1,0:T(8,128)(2,1)} %param.18) | copy-start | bytes 110596
  19.1 0.7 %copy-start.6 = (f32[6,6,1]{1,0,2:T(8,128)S(1)}, f32[6,6,1]{1,0,2:T(8,128)}, u32[]{:S(2)}) copy-start(f32[6,6,1]{1,0,2:T(8,128)} %constant.17) | copy-start | bytes 436
  19.3 0.9 %copy-start.9 = (f32[128]{0:T(128)S(1)}, f32[128]{0:T(128)}, u32[]{:S(2)}) copy-start(f32[128]{0:T(128)} %param.19) | copy-start | bytes 1540
  19.8 0.8 %copy-start.7 = (s32[1,224]{1,0:T(1,128)S(1)}, s32[1,224]{1,0:T(1,128)}, u32[]{:S(2)}) copy-start(s32[1,224]{1,0:T(1,128)} %param.21) | copy-start | bytes 2692
  20.3 1.9 %copy-start.1 = (f32[6,128,128]{2,1,0:T(8,128)}, f32[6,128,128]{2,1,0:T(8,128)S(1)}, u32[]{:S(2)}) copy-start(f32[6,128,128]{2,1,0:T(8,128)S(1)} %fusion.13.stress_ref) | copy-start | bytes 1179652
  20.3 1.9 %copy-start.8 = (f32[512]{0:T(512)S(1)}, f32[512]{0:T(512)}, u32[]{:S(2)}) copy-start(f32[512]{0:T(512)} %param.22) | copy-start | bytes 6148
